TPU v7x, 256 devices: a whole 4x4x8 slice. The times are simulated.
256 devices in a mesh: head: 4 (over x), tok: 64 (over z, y, core).
Axes of the slice: x: 4, y: 4, z: 8, core: 2. Of those that a mesh axis runs over, the one named last changes fastest.
Arguments:
- queries: bfloat16 [2, 16384, 5120], P(None, 'tok', 'head'), may hold values from -6 to 6
- key_rows: bfloat16 [16384, 5120], P('tok', 'head'), may hold values from -6 to 6
- value_rows: bfloat16 [16384, 5120], P('tok', 'head'), may hold values from -6 to 6
- step_rates: float32 [20, 16384], P('head', 'tok'), may hold values from 0.05 to 1
- gate_fast: float32 [20, 256, 256], P('head'), may hold values from -0.375 to 0.375
- up_fast: float32 [20, 256, 256], P('head'), may hold values from -0.375 to 0.375
- down_fast: float32 [20, 256, 256], P('head'), may hold values from -0.375 to 0.375
Outputs:
- out_rows: bfloat16 [2, 16384, 5120], P(None, ('tok', 'head'))
All inputs are finite; a program needn't handle non-finite values.
Results may differ from a plain program's by a relative error of at most 0.011.
Values may be sent and summed in bfloat16 or wider, within the bound.
No kernel may reach another device: no remote copies, remote signals or barrier semaphores. Data moves between devices by JAX's collectives and lax.ppermute only.
A program may use at most 64 MiB of HBM per device.

v0:
```python
import jax
import jax.numpy as jnp
from jax import lax
from jax.sharding import PartitionSpec as P

NS_STEPS = 3


coef_first = 3.4445
coef_second = -4.775
coef_third = 2.0315


def fast_apply(inputs, gate_mat, up_mat, down_mat):
    gate_pre = jnp.einsum("thd,hdf->thf", inputs, gate_mat, preferred_element_type=jnp.float32)
    up_pre = jnp.einsum("thd,hdf->thf", inputs, up_mat, preferred_element_type=jnp.float32)
    hidden = (jax.nn.silu(gate_pre) * up_pre).astype(jnp.bfloat16)
    result = jnp.einsum("thf,hfd->thd", hidden, down_mat, preferred_element_type=jnp.float32)
    return result.astype(jnp.bfloat16).reshape(inputs.shape[0], -1)


def orthogonal(gradient):
    scale = jnp.sqrt(jnp.sum(gradient * gradient, axis=(1, 2), keepdims=True)) + 1e-07
    iterate = gradient / scale
    for sweep in range(NS_STEPS):
        gram = jnp.einsum("hdf,hdg->hfg", iterate, iterate, precision=lax.Precision.HIGHEST)
        square = jnp.einsum("hfg,hgk->hfk", gram, gram, precision=lax.Precision.HIGHEST)
        poly = coef_second * gram + coef_third * square
        iterate = coef_first * iterate + jnp.einsum(
            "hdf,hfg->hdg", iterate, poly, precision=lax.Precision.HIGHEST
        )
    return iterate


def local(queries, key_rows, value_rows, step_rates, gate_fast, up_fast, down_fast):
    heads_here = gate_fast.shape[0]
    head_size = gate_fast.shape[1]
    local_rows = key_rows.shape[0]
    gate_half = gate_fast.astype(jnp.bfloat16)
    up_half = up_fast.astype(jnp.bfloat16)
    down_half = down_fast.astype(jnp.bfloat16)
    query_heads = queries.reshape(2, local_rows, heads_here, head_size)
    first_out = fast_apply(query_heads[0], gate_half, up_half, down_half)
    key_heads = key_rows.reshape(local_rows, heads_here, head_size)
    value_heads = value_rows.reshape(local_rows, heads_here, head_size)
    gate_pre = jnp.einsum("thd,hdf->thf", key_heads, gate_half, preferred_element_type=jnp.float32)
    up_pre = jnp.einsum("thd,hdf->thf", key_heads, up_half, preferred_element_type=jnp.float32)
    sigmoid_gate = jax.nn.sigmoid(gate_pre)
    silu_gate = jax.nn.silu(gate_pre)
    hidden = (silu_gate * up_pre).astype(jnp.bfloat16)
    rates = jnp.transpose(step_rates)[:, :, None]
    down_in = (-(rates * value_heads.astype(jnp.float32))).astype(jnp.bfloat16)
    down_grad = jnp.einsum("thf,thd->hfd", hidden, down_in, preferred_element_type=jnp.float32)
    hidden_grad = jnp.einsum("thd,hfd->thf", down_in, down_half, preferred_element_type=jnp.float32)
    up_in = (hidden_grad * silu_gate).astype(jnp.bfloat16)
    gate_in = (
        hidden_grad * up_pre * sigmoid_gate * (1.0 + gate_pre * (1.0 - sigmoid_gate))
    ).astype(jnp.bfloat16)
    gate_grad = jnp.einsum("thd,thf->hdf", key_heads, gate_in, preferred_element_type=jnp.float32)
    up_grad = jnp.einsum("thd,thf->hdf", key_heads, up_in, preferred_element_type=jnp.float32)
    gate_sum, up_sum, down_sum = lax.psum((gate_grad, up_grad, down_grad), "tok")
    gate_next = (gate_fast - orthogonal(gate_sum)).astype(jnp.bfloat16)
    up_next = (up_fast - orthogonal(up_sum)).astype(jnp.bfloat16)
    down_next = (down_fast - orthogonal(down_sum)).astype(jnp.bfloat16)
    second_out = fast_apply(query_heads[1], gate_next, up_next, down_next)
    return lax.all_to_all(
        jnp.stack((first_out, second_out), 0), "head", split_axis=1, concat_axis=2, tiled=True
    )


def solution(mesh):
    placed = (
        P(None, "tok", "head"),
        P("tok", "head"),
        P("tok", "head"),
        P("head", "tok"),
        P("head", None, None),
        P("head", None, None),
        P("head", None, None),
    )
    return jax.shard_map(
        local, mesh=mesh, in_specs=placed, out_specs=P(None, ("tok", "head"), None), check_vma=False
    )
```

profile of v0, /device:TPU:33, one launch (start us, length us, event | category | flops | bytes accessed | tf_op | source)
XLA Modules:
  0.0 306.0 jit_solution(3345028966825901015)
XLA Ops:
  12.3 1.6 fusion.22
  13.9 1.8 convolution_bitcast_fusion.4
  15.7 1.6 convolution_bitcast_fusion.2
  17.4 2.2 fusion.44
  22.1 2.5 convolution_bitcast_fusion.8
  24.6 3.6 %convolution_convert_fusion.1 = bf16[5,256,256]{1,2,0:T(8,128)(2,1)} fusion(bf16[256,5,256]{0,2,1:T(8,128)(2,1)} %bitcast.111, f32[256,5,256]{0,2,1:T(8,128)} %convolution_bitcast_fusion.8, f32[5,256,256]{2,1,0:T(8,128)} %param.13, f32[5,256,256]{2,1,0:T(8,128)S(1)} %copy-done.1), kind=kOutput, calls=%fused_computation.47 | convolution fusion | flops 338493440 | bytes 5242880 | tf_op jit(solution)/shard_map/thf,hfd->thd/dot_general | solution.py:18
  28.2 4.3 %copy.143 = bf16[1,256,1280]{2,0,1:T(2,128)(2,1)} copy(bf16[1,256,1280]{1,2,0:T(8,128)(2,1)} %bitcast.115) | data formatting | bytes 1310720 | tf_op jit(solution)/shard_map/stack;reshape | solution.py:67
  32.4 181.2 %all-reduce.3.cloned.1.call-done = (f32[5,256,256]{2,1,0:T(8,128)}, f32[5,256,256]{2,1,0:T(8,128)}, f32[5,256,256]{2,1,0:T(8,128)}) async-done(((f32[5,256,256]{2,1,0:T(8,128)}, f32[5,256,256]{2,1,0:T(8,128)}, f32[5,256,256]{2,1,0:T(8,128)}), (f32[5,256,256]{2,1,0:T(8,128)}, f32[5,256,256]{2,1,0:T(8,128)}, f32[5,256,256]{2,1,0:T(8,128)})) %all-reduce.3.cloned.1.call-update) | async-done | bytes 3932176 | tf_op jit(solution)/shard_map/psum | solution.py:61
  213.7 1.6 multiply_reduce_fusion.2
  215.4 1.8 multiply_reduce_fusion
  217.2 2.4 fusion.37
  221.1 1.5 convolution_add_fusion.5
  222.6 2.3 fusion.47
  224.9 1.5 fusion.6
  227.9 2.5 fusion.48
  230.4 1.5 fusion.5
  233.4 2.4 fusion.38
  237.3 1.5 convolution_add_fusion.2
  238.8 2.3 fusion.49
  241.1 1.7 fusion.2
  244.2 2.2 fusion.50
  248.0 2.3 fusion.18
  250.3 2.4 fusion.36
  252.7 1.5 fusion.11
  254.2 1.9 convolution_add_fusion.8
  256.1 2.3 fusion.45
  261.5 2.3 fusion.46
  265.3 1.5 fusion.16
  267.9 1.8 convolution_convert_fusion
  269.7 2.7 copy.144
  272.5 3.0 pad_maximum_fusion
  275.4 22.2 %all_to_all.18 = bf16[2,256,1280]{2,0,1:T(2,128)(2,1)S(1)} all-to-all(bf16[2,256,1280]{2,0,1:T(2,128)(2,1)S(1)} %pad_maximum_fusion), channel_id=1, replica_groups=mesh['head'=4,'tok'=64] {'head'}, dimensions={1} | all-to-all | bytes 2621440 | tf_op jit(solution)/shard_map/all_to_all | solution.py:66
  (48 shorter events, 24.0 us)
Async XLA Ops:
  6.5 1.5 copy-start.10
  6.5 2.6 copy-start
  6.5 207.1 %all-reduce.3.cloned.1.call-start = ((), (), s32[]{:S(2)}) async-start(), calls=%async_computation.1 | async-start | bytes 7864320 | tf_op jit(solution)/shard_map/psum | solution.py:61
  9.1 1.3 copy-start.1
  10.4 1.3 copy-start.2
  10.4 1.5 copy-start.5
  10.4 1.5 copy-start.11
  213.7 1.7 copy-start.7
  215.4 1.8 copy-start.8
  248.0 2.3 copy-start.6
  263.8 1.5 copy-start.3
  266.8 1.1 copy-start.9
  269.7 2.7 copy-start.4
Sparse Core Ops, SparseCore 0:
  17.5 196.0 all-reduce.2
where the time goes:
time: 311 us; the launch traced here: 306 us
  waiting for transfers between devices  181 us (58%)
  matrix products  63.9 us (21%)
  blocking collectives  22.2 us (7%)
  local copies, waits for them, and re-layouts  18.3 us (6%)
  between operations  13.9 us (4%)
  other arithmetic  6.38 us (2%)
    psum x1, waiting for transfers between devices, local(): lax.psum((gate_grad, up_grad, down_grad), 'tok')  181 us
    all_to_all x1, blocking collectives, local(): lax.all_to_all(jnp.stack((first_out, second_out), 0), 'head', split_axis=...  22.2 us
    dot_general x9, matrix products, orthogonal(): jnp.einsum('hdf,hdg->hfg', iterate, iterate, precision=lax.Precision.HIGH...  21.2 us
    dot_general x9, matrix products, orthogonal(): jnp.einsum('hdf,hfg->hdg', iterate, poly, precision=lax.Precision.HIGHEST)  14.6 us
    dot_general x9, matrix products, orthogonal(): jnp.einsum('hfg,hgk->hfk', gram, gram, precision=lax.Precision.HIGHEST)  13.6 us
    unnamed x28, local copies, waits for them, and re-layouts  7.83 us
    another operation x2, local copies, waits for them, and re-layouts, local(): jnp.stack((first_out, second_out), 0)  6.97 us
  transfers between devices with their start and end apart: 1, of which 1 were waited for; matrix products, arithmetic and copies ran while one was open for 5% of the time, Pallas kernels for 0%

commit v1 on v0

v1 whole, which is shorter than its diff:
```python
import jax
import jax.numpy as jnp
from jax import lax
from jax.experimental import pallas as pl
from jax.experimental.pallas import tpu as pltpu
from jax.sharding import Mesh, PartitionSpec as P

NS_STEPS = 3
coef_first = 3.4445
coef_second = -4.775
coef_third = 2.0315
F32 = jnp.float32
BF16 = jnp.bfloat16
HD = 256
HALF = 128
HEADS_HERE = 5
MATS = 3 * HEADS_HERE
GROUP = 8
PIECES = 32
VMEM_LIMIT = 48 * 1024 * 1024


def dot_f32(a, b):
    return lax.dot_general(a, b, (((1,), (0,)), ((), ())), preferred_element_type=F32)


def dot_nt(a, b):
    return lax.dot_general(a, b, (((1,), (1,)), ((), ())), preferred_element_type=F32)


def dot_tn(a, b):
    return lax.dot_general(a, b, (((0,), (0,)), ((), ())), preferred_element_type=F32)


def sigmoid(x):
    return 1.0 / (1.0 + jnp.exp(-x))


def apply_fast(rows, gate, up, down):
    zg = dot_f32(rows, gate)
    zu = dot_f32(rows, up)
    hidden = (zg * sigmoid(zg) * zu).astype(BF16)
    return dot_f32(hidden, down).astype(BF16)


def store_rows(out_ref, rows):
    for r in range(out_ref.shape[0]):
        out_ref[r, 0] = rows[r * 64 : (r + 1) * 64, :]


def first_kernel(core_ref, q_ref, k_ref, v_ref, rate_ref, g_ref, u_ref, d_ref, out_ref, keep_ref, send_ref, grad_ref):
    head = pl.program_id(0)
    core = core_ref[0]
    gate = g_ref[0].astype(BF16)
    up = u_ref[0].astype(BF16)
    down = d_ref[0].astype(BF16)
    store_rows(out_ref, apply_fast(q_ref[0], gate, up, down))
    keys = k_ref[...]
    zg = dot_f32(keys, gate)
    zu = dot_f32(keys, up)
    sig = sigmoid(zg)
    silu = zg * sig
    hidden = (silu * zu).astype(BF16)
    rate = rate_ref[pl.ds(head, 1), :]
    rate = jnp.transpose(jnp.broadcast_to(rate, (HALF, rate.shape[1])))
    rate = jnp.concatenate([rate, rate], axis=1)
    dout = (-(rate * v_ref[...].astype(F32))).astype(BF16)
    dh = dot_nt(dout, down)
    dzu = (dh * silu).astype(BF16)
    dzg = (dh * zu * sig * (1.0 + zg * (1.0 - sig))).astype(BF16)
    grad_ref[0] = dot_tn(keys, dzg)
    grad_ref[1] = dot_tn(keys, dzu)
    grad_ref[2] = dot_tn(hidden, dout)
    mine = pl.multiple_of(core * HALF, HALF)
    other = pl.multiple_of((1 - core) * HALF, HALF)
    for mat in range(3):
        for side in range(2):
            cols = slice(side * HALF, (side + 1) * HALF)
            at = slice(side * 16, (side + 1) * 16)
            keep_ref[at, mat] = grad_ref[mat, pl.ds(mine, HALF), cols].reshape(16, 8, HALF)
            send_ref[at, mat] = grad_ref[mat, pl.ds(other, HALF), cols].reshape(16, 8, HALF).astype(BF16)


def split(x):
    high = x.astype(BF16)
    return high, (x - high.astype(F32)).astype(BF16)


def half_matrix(piece):
    piece = piece.astype(F32)
    left = piece[:16].reshape(HALF, HALF)
    right = piece[16:].reshape(HALF, HALF)
    return jnp.concatenate([left, right], axis=1)


def orth_kernel(core_ref, *refs):
    count = (len(refs) - 1) // 2
    out_ref = refs[-1]
    low_core = core_ref[0] == 0
    xs = []
    for i in range(count):
        mine = half_matrix(refs[2 * i][:, 0])
        other = half_matrix(refs[2 * i + 1][:, 0])
        top = jnp.where(low_core, mine, other)
        bottom = jnp.where(low_core, other, mine)
        m = jnp.concatenate([top, bottom], axis=0)
        norm = jnp.sqrt(jnp.sum(m * m, keepdims=True)) + 1e-07
        xs.append(m / norm)
    for sweep in range(NS_STEPS):
        if sweep < NS_STEPS - 1:
            lows = [x.astype(BF16) for x in xs]
            grams = [dot_nt(x, x) for x in lows]
            halves = [a.astype(BF16) for a in grams]
            squares = [dot_f32(a, a) for a in halves]
            polys = [(coef_second * a + coef_third * s).astype(BF16) for a, s in zip(grams, squares)]
            xs = [coef_first * x + dot_f32(p, l) for x, p, l in zip(xs, polys, lows)]
        else:
            parts = [split(x) for x in xs]
            grams = [dot_nt(h, h) + (dot_nt(h, l) + dot_nt(l, h)) for h, l in parts]
            gparts = [split(a) for a in grams]
            squares = [dot_f32(h, h) + (dot_f32(h, l) + dot_f32(l, h)) for h, l in gparts]
            polys = [split(coef_second * a + coef_third * s) for a, s in zip(grams, squares)]
            xs = [
                coef_first * x + (dot_f32(ph, h) + (dot_f32(ph, l) + dot_f32(pw, h)))
                for x, (ph, pw), (h, l) in zip(xs, polys, parts)
            ]
    for i in range(count):
        out_ref[i] = xs[i].astype(BF16)


def second_kernel(core_ref, buf_ref, q_ref, g_ref, u_ref, d_ref, mine_ref, other_ref, out_ref):
    head = pl.program_id(0)
    low_core = core_ref[0] == 0
    nexts = []
    for mat, ref in enumerate((g_ref, u_ref, d_ref)):
        at = head * 3 + mat
        in_low = at < GROUP
        index = jnp.where(in_low, at, at - (GROUP - 1))
        orth = jnp.where(in_low == low_core, mine_ref[index], other_ref[index])
        nexts.append((ref[0] - orth.astype(F32)).astype(BF16))
    store_rows(out_ref, apply_fast(q_ref[0], *nexts))


def local(queries, key_rows, value_rows, step_rates, gate_fast, up_fast, down_fast):
    rows = key_rows.shape[0]
    width = key_rows.shape[1]
    core = lax.axis_index("core").astype(jnp.int32).reshape(1)
    n_head = lax.axis_size("head")
    params = pltpu.CompilerParams(dimension_semantics=("arbitrary",), vmem_limit_bytes=VMEM_LIMIT)
    weight_spec = pl.BlockSpec((1, HD, HD), lambda h, c: (h, 0, 0))
    buf_shape = jax.ShapeDtypeStruct((n_head, 2, rows // n_head, width), BF16)

    def out_spec(block):
        return pl.BlockSpec((n_head, 1, rows // n_head, HD), lambda h, c: (0, block, 0, h))

    piece_spec = pl.BlockSpec((PIECES, 3, 8, HALF), lambda h, c: (0, h, 0, 0))
    buf, keep, send = pl.pallas_call(
        first_kernel,
        grid_spec=pltpu.PrefetchScalarGridSpec(
            num_scalar_prefetch=1,
            grid=(HEADS_HERE,),
            in_specs=[
                pl.BlockSpec((1, rows, HD), lambda h, c: (0, 0, h)),
                pl.BlockSpec((rows, HD), lambda h, c: (0, h)),
                pl.BlockSpec((rows, HD), lambda h, c: (0, h)),
                pl.BlockSpec((HEADS_HERE, rows), lambda h, c: (0, 0)),
                weight_spec,
                weight_spec,
                weight_spec,
            ],
            out_specs=[out_spec(0), piece_spec, piece_spec],
            scratch_shapes=[pltpu.VMEM((3, HD, HD), F32)],
        ),
        out_shape=[
            buf_shape,
            jax.ShapeDtypeStruct((PIECES, MATS, 8, HALF), F32),
            jax.ShapeDtypeStruct((PIECES, MATS, 8, HALF), BF16),
        ],
        compiler_params=params,
        name="first_and_grads",
    )(core, queries, key_rows, value_rows, step_rates, gate_fast, up_fast, down_fast)

    swap = [(0, 1), (1, 0)]
    received = lax.ppermute(send, "core", swap)
    chip_sum = (keep + received.astype(F32)).astype(BF16)
    scattered = lax.all_to_all(chip_sum, ("z", "y"), split_axis=0, concat_axis=0, tiled=True)
    piece = jnp.sum(scattered.astype(F32), axis=0).astype(BF16)
    spread = jnp.broadcast_to(piece[None], (PIECES,) + piece.shape)
    mine = lax.all_to_all(spread, ("z", "y"), split_axis=0, concat_axis=0, tiled=True)
    other = lax.ppermute(mine, "core", swap)

    per_step = 2
    mat_specs = []
    for i in range(per_step):
        spec = pl.BlockSpec((PIECES, 1, 8, HALF), lambda s, c, i=i: (0, c[0] * (GROUP - 1) + s * per_step + i, 0, 0))
        mat_specs += [spec, spec]
    orth_mine = pl.pallas_call(
        orth_kernel,
        grid_spec=pltpu.PrefetchScalarGridSpec(
            num_scalar_prefetch=1,
            grid=(GROUP // per_step,),
            in_specs=mat_specs,
            out_specs=pl.BlockSpec((per_step, HD, HD), lambda s, c: (s, 0, 0)),
        ),
        out_shape=jax.ShapeDtypeStruct((GROUP, HD, HD), BF16),
        compiler_params=params,
        name="orthogonalize",
    )(core, *([mine, other] * per_step))
    orth_other = lax.ppermute(orth_mine, "core", swap)

    group_spec = pl.BlockSpec((GROUP, HD, HD), lambda h, c: (0, 0, 0))
    buf = pl.pallas_call(
        second_kernel,
        grid_spec=pltpu.PrefetchScalarGridSpec(
            num_scalar_prefetch=1,
            grid=(HEADS_HERE,),
            in_specs=[
                pl.BlockSpec(memory_space=pl.ANY),
                pl.BlockSpec((1, rows, HD), lambda h, c: (1, 0, h)),
                weight_spec,
                weight_spec,
                weight_spec,
                group_spec,
                group_spec,
            ],
            out_specs=out_spec(1),
        ),
        out_shape=buf_shape,
        input_output_aliases={1: 0},
        compiler_params=params,
        name="second",
    )(core, buf, queries, gate_fast, up_fast, down_fast, orth_mine, orth_other)

    swapped = lax.all_to_all(buf, "head", split_axis=0, concat_axis=0, tiled=True)
    return swapped.transpose(1, 2, 0, 3).reshape(2, rows // n_head, n_head * width)


def solution(mesh):
    heads = mesh.shape["head"]
    fine = Mesh(mesh.devices.reshape(heads, 8, 4, 2), ("head", "z", "y", "core"))
    tok = ("z", "y", "core")
    placed = (
        P(None, tok, "head"),
        P(tok, "head"),
        P(tok, "head"),
        P("head", tok),
        P("head", None, None),
        P("head", None, None),
        P("head", None, None),
    )
    return jax.shard_map(
        local, mesh=fine, in_specs=placed, out_specs=P(None, tok + ("head",), None), check_vma=False
    )
```

time: 311 us -> 129 us (0.41)
  the two profiles are of different devices: /device:TPU:33 before, /device:TPU:1 now
where the time goes in v1:
time: 129 us; the launch traced here: 128 us
  blocking collectives  85.9 us (67%)
  Pallas kernels  20.8 us (16%)
  starting transfers between devices  6.91 us (5%)
  waiting for transfers between devices  6.67 us (5%)
  local copies, waits for them, and re-layouts  5.51 us (4%)
  other arithmetic  1.91 us (1%)
    all_to_all x1, blocking collectives, local(): lax.all_to_all(chip_sum, ('z', 'y'), split_axis=0, concat_axis=0, tiled=T...  34.3 us
    all_to_all x1, blocking collectives, local(): lax.all_to_all(spread, ('z', 'y'), split_axis=0, concat_axis=0, tiled=True)  30.7 us
    all_to_all x1, blocking collectives, local(): lax.all_to_all(buf, 'head', split_axis=0, concat_axis=0, tiled=True)  20.9 us
    pallas_call x1, Pallas kernels, local(): pl.pallas_call(orth_kernel, grid_spec=pltpu.PrefetchScalarGridSpec(num_sc...  9.57 us
    pallas_call x1, Pallas kernels, local(): pl.pallas_call(first_kernel, grid_spec=pltpu.PrefetchScalarGridSpec(num_s...  6.82 us
    pallas_call x1, Pallas kernels, local(): pl.pallas_call(second_kernel, grid_spec=pltpu.PrefetchScalarGridSpec(num_...  4.45 us
    unnamed x12, local copies, waits for them, and re-layouts  4.19 us
    ppermute x1, starting transfers between devices, local(): received = lax.ppermute(send, 'core', swap)  3.24 us
  transfers between devices with their start and end apart: 3, of which 3 were waited for; matrix products, arithmetic and copies ran while one was open for 0% of the time, Pallas kernels for 0%

profile of v1, /device:TPU:1, one launch (start us, length us, event | category | flops | bytes accessed | tf_op | source)
XLA Modules:
  0.0 127.8 jit_solution(4179674458920261518)
XLA Ops:
  0.0 0.0 copy-start
  0.0 1.3 %copy-done = bf16[2,256,1280]{2,1,0:T(8,128)(2,1)S(1)} copy-done((bf16[2,256,1280]{2,1,0:T(8,128)(2,1)S(1)}, bf16[2,256,1280]{2,1,0:T(8,128)(2,1)}, u32[]{:S(2)}) %copy-start) | copy-done | bytes 1310744
  1.3 0.0 copy-start.3
  1.3 1.1 copy-done.3
  2.4 0.0 copy-start.4
  2.4 1.1 copy-done.4
  3.5 0.0 copy-start.5
  3.5 0.7 copy-done.5
  4.2 6.8 %first_and_grads.1 = (bf16[4,2,64,1280]{3,2,1,0:T(8,128)(2,1)S(1)}, f32[32,15,8,128]{3,2,1,0:T(8,128)}, bf16[32,15,8,128]{3,2,1,0:T(8,128)(2,1)S(1)}) custom-call(s32[1]{0:T(128)} %bitcast.core_ref, bf16[2,256,1280]{2,1,0:T(8,128)(2,1)S(1)} %copy-done, bf16[256,1280]{1,0:T(8,128)(2,1)S(1)} %copy-done.3, bf16[256,1280]{1,0:T(8,128)(2,1)S(1)} %copy-done.4, ...), custom_call_target="tpu_custom_call" | custom-call | tf_op jit(solution)/shard_map/first_and_grads/pallas_call | solution.py:157
  11.0 3.2 %collective-permute-start = (bf16[32,15,8,128]{3,2,1,0:T(8,128)(2,1)S(1)}, bf16[32,15,8,128]{3,2,1,0:T(8,128)(2,1)S(1)}, u32[]{:S(2)}, u32[]{:S(2)}) collective-permute-start(bf16[32,15,8,128]{3,2,1,0:T(8,128)(2,1)S(1)} %get-tuple-element.10), channel_id=1, source_target_pairs={{0,1},{1,0},{2,3},{3,2},{4,5},{5,4},{6,7},{7,6},{8,9},{9,8},{10,11... | collective-permute-start | bytes 2949128 | tf_op jit(solution)/shard_map/ppermute | solution.py:184
  14.2 2.2 %collective-permute-done = bf16[32,15,8,128]{3,2,1,0:T(8,128)(2,1)S(1)} collective-permute-done((bf16[32,15,8,128]{3,2,1,0:T(8,128)(2,1)S(1)}, bf16[32,15,8,128]{3,2,1,0:T(8,128)(2,1)S(1)}, u32[]{:S(2)}, u32[]{:S(2)}) %collective-permute-start) | collective-permute-done | bytes 983072 | tf_op jit(solution)/shard_map/ppermute | solution.py:184
  16.4 1.8 %add_convert_fusion = bf16[32,15,8,128]{3,2,1,0:T(8,128)(2,1)S(1)} fusion(f32[32,15,8,128]{3,2,1,0:T(8,128)} %get-tuple-element.9, bf16[32,15,8,128]{3,2,1,0:T(8,128)(2,1)S(1)} %collective-permute-done), kind=kLoop, calls=%fused_computation | loop fusion | flops 1474560 | bytes 3932160 | tf_op jit(solution)/shard_map/convert_element_type | solution.py:185
  18.2 34.3 %all_to_all.15 = bf16[32,15,8,128]{3,2,1,0:T(8,128)(2,1)S(1)} all-to-all(bf16[32,15,8,128]{3,2,1,0:T(8,128)(2,1)S(1)} %add_convert_fusion), channel_id=1, replica_groups=mesh['head'=4,'z'=8,'y'=4,'core'=2] {'z','y'}, dimensions={0} | all-to-all | bytes 1966080 | tf_op jit(solution)/shard_map/all_to_all | solution.py:186
  52.5 0.1 reduce_sum.12
  52.7 0.1 broadcast_in_dim.2
  52.8 30.7 %all_to_all.16.refs_0_.refs_2_ = bf16[32,15,8,128]{3,2,1,0:T(8,128)(2,1)S(1)} all-to-all(bf16[32,15,8,128]{3,2,1,0:T(8,128)(2,1)S(1)} %broadcast_in_dim.2), channel_id=1, replica_groups=mesh['head'=4,'z'=8,'y'=4,'core'=2] {'z','y'}, dimensions={0} | all-to-all | bytes 1966080 | tf_op jit(solution)/shard_map/all_to_all | solution.py:189
  83.5 0.0 copy-start.1
  83.5 0.0 copy-start.2
  83.5 3.2 %collective-permute-start.1 = (bf16[32,15,8,128]{3,2,1,0:T(8,128)(2,1)S(1)}, bf16[32,15,8,128]{3,2,1,0:T(8,128)(2,1)S(1)}, u32[]{:S(2)}, u32[]{:S(2)}) collective-permute-start(bf16[32,15,8,128]{3,2,1,0:T(8,128)(2,1)S(1)} %all_to_all.16.refs_0_.refs_2_), channel_id=1, source_target_pairs={{0,1},{1,0},{2,3},{3,2},{4,5},{5,4},{6,7},{7,6},{8,9},{9,8},{10,11... | collective-permute-start | bytes 2949128 | tf_op jit(solution)/shard_map/ppermute | solution.py:190
  86.7 2.2 %collective-permute-done.1.refs_1_.refs_3_ = bf16[32,15,8,128]{3,2,1,0:T(8,128)(2,1)S(1)} collective-permute-done((bf16[32,15,8,128]{3,2,1,0:T(8,128)(2,1)S(1)}, bf16[32,15,8,128]{3,2,1,0:T(8,128)(2,1)S(1)}, u32[]{:S(2)}, u32[]{:S(2)}) %collective-permute-start.1) | collective-permute-done | bytes 983072 | tf_op jit(solution)/shard_map/ppermute | solution.py:190
  88.9 9.6 %orthogonalize.1.mine_ref = bf16[8,256,256]{2,1,0:T(8,128)(2,1)S(1)} custom-call(s32[1]{0:T(128)} %bitcast.core_ref, bf16[32,15,8,128]{3,2,1,0:T(8,128)(2,1)S(1)} %all_to_all.16.refs_0_.refs_2_, bf16[32,15,8,128]{3,2,1,0:T(8,128)(2,1)S(1)} %collective-permute-done.1.refs_1_.refs_3_, bf16[32,15,8,128]{3,2,1,0:T(8,128)(2,1)S(1)} %all_to_all.16.refs_0_.refs_2_, ...), custom_call_target="tpu_custom_call" | custom-call | tf_op jit(solution)/shard_map/orthogonalize/pallas_call | solution.py:197
  98.5 0.5 collective-permute-start.2
  98.9 2.3 %collective-permute-done.2.other_ref = bf16[8,256,256]{2,1,0:T(8,128)(2,1)S(1)} collective-permute-done((bf16[8,256,256]{2,1,0:T(8,128)(2,1)S(1)}, bf16[8,256,256]{2,1,0:T(8,128)(2,1)S(1)}, u32[]{:S(2)}, u32[]{:S(2)}) %collective-permute-start.2) | collective-permute-done | bytes 1048608 | tf_op jit(solution)/shard_map/ppermute | solution.py:209
  101.2 0.0 copy-done.1
  101.2 0.0 copy-done.2
  101.2 4.5 %second.1 = bf16[4,2,64,1280]{3,2,1,0:T(8,128)(2,1)S(1)} custom-call(s32[1]{0:T(128)} %bitcast.core_ref, bf16[4,2,64,1280]{3,2,1,0:T(8,128)(2,1)S(1)} %get-tuple-element.8.buf_ref, bf16[2,256,1280]{2,1,0:T(8,128)(2,1)S(1)} %copy-done.1, f32[5,256,256]{2,1,0:T(8,128)S(1)} %copy-done.2, f32[5,256,256]{2,1,0:T(8,128)} %u_ref.3, ...), custom_call_target="tpu_custom_call", output_to_operand_aliasing={{}: (1, {})} | custom-call | tf_op jit(solution)/shard_map/second/pallas_call | solution.py:212
  105.7 20.9 %all_to_all.17 = bf16[4,2,64,1280]{3,2,1,0:T(8,128)(2,1)S(1)} all-to-all(bf16[4,2,64,1280]{3,2,1,0:T(8,128)(2,1)S(1)} %second.1), channel_id=1, replica_groups=mesh['head'=4,'z'=8,'y'=4,'core'=2] {'head'}, dimensions={0} | all-to-all | bytes 2621440 | tf_op jit(solution)/shard_map/all_to_all | solution.py:234
  126.6 1.2 copy.10
Async XLA Ops:
  0.0 1.3 %copy-start = (bf16[2,256,1280]{2,1,0:T(8,128)(2,1)S(1)}, bf16[2,256,1280]{2,1,0:T(8,128)(2,1)}, u32[]{:S(2)}) copy-start(bf16[2,256,1280]{2,1,0:T(8,128)(2,1)} %q_ref.3) | copy-start | bytes 3932164
  1.3 1.1 copy-start.3
  2.4 1.1 copy-start.4
  3.5 0.7 copy-start.5
  11.0 5.4 %collective-permute-start = (bf16[32,15,8,128]{3,2,1,0:T(8,128)(2,1)S(1)}, bf16[32,15,8,128]{3,2,1,0:T(8,128)(2,1)S(1)}, u32[]{:S(2)}, u32[]{:S(2)}) collective-permute-start(bf16[32,15,8,128]{3,2,1,0:T(8,128)(2,1)S(1)} %get-tuple-element.10), channel_id=1, source_target_pairs={{0,1},{1,0},{2,3},{3,2},{4,5},{5,4},{6,7},{7,6},{8,9},{9,8},{10,11... | collective-permute-start | bytes 2949128 | tf_op jit(solution)/shard_map/ppermute | solution.py:184
  83.5 17.7 %copy-start.1 = (bf16[2,256,1280]{2,1,0:T(8,128)(2,1)S(1)}, bf16[2,256,1280]{2,1,0:T(8,128)(2,1)}, u32[]{:S(2)}) copy-start(bf16[2,256,1280]{2,1,0:T(8,128)(2,1)} %q_ref.3) | copy-start | bytes 3932164
  83.5 17.7 %copy-start.2 = (f32[5,256,256]{2,1,0:T(8,128)S(1)}, f32[5,256,256]{2,1,0:T(8,128)}, u32[]{:S(2)}) copy-start(f32[5,256,256]{2,1,0:T(8,128)} %g_ref.3) | copy-start | bytes 3932164
  83.5 5.4 %collective-permute-start.1 = (bf16[32,15,8,128]{3,2,1,0:T(8,128)(2,1)S(1)}, bf16[32,15,8,128]{3,2,1,0:T(8,128)(2,1)S(1)}, u32[]{:S(2)}, u32[]{:S(2)}) collective-permute-start(bf16[32,15,8,128]{3,2,1,0:T(8,128)(2,1)S(1)} %all_to_all.16.refs_0_.refs_2_), channel_id=1, source_target_pairs={{0,1},{1,0},{2,3},{3,2},{4,5},{5,4},{6,7},{7,6},{8,9},{9,8},{10,11... | collective-permute-start | bytes 2949128 | tf_op jit(solution)/shard_map/ppermute | solution.py:190
  98.5 2.8 %collective-permute-start.2 = (bf16[8,256,256]{2,1,0:T(8,128)(2,1)S(1)}, bf16[8,256,256]{2,1,0:T(8,128)(2,1)S(1)}, u32[]{:S(2)}, u32[]{:S(2)}) collective-permute-start(bf16[8,256,256]{2,1,0:T(8,128)(2,1)S(1)} %orthogonalize.1.mine_ref), channel_id=1, source_target_pairs={{0,1},{1,0},{2,3},{3,2},{4,5},{5,4},{6,7},{7,6},{8,9},{9,8},{10,11... | collective-permute-start | bytes 3145736 | tf_op jit(solution)/shard_map/ppermute | solution.py:209

commit v2 on v1

--- a/solution.py
+++ b/solution.py
@@ -16,7 +16,10 @@
 HEADS_HERE = 5
 MATS = 3 * HEADS_HERE
 GROUP = 8
-PIECES = 32
+Y = 4
+Z = 8
+PER_Y = GROUP // Y
+ROWS = 64
 VMEM_LIMIT = 48 * 1024 * 1024
 
 
@@ -33,7 +36,7 @@
 
 
 def sigmoid(x):
-    return 1.0 / (1.0 + jnp.exp(-x))
+    return 0.5 * jnp.tanh(0.5 * x) + 0.5
 
 
 def apply_fast(rows, gate, up, down):
@@ -48,7 +51,7 @@
         out_ref[r, 0] = rows[r * 64 : (r + 1) * 64, :]
 
 
-def first_kernel(core_ref, q_ref, k_ref, v_ref, rate_ref, g_ref, u_ref, d_ref, out_ref, keep_ref, send_ref, grad_ref):
+def first_kernel(core_ref, q_ref, k_ref, v_ref, rate_ref, g_ref, u_ref, d_ref, out_ref, keep_ref, send_ref):
     head = pl.program_id(0)
     core = core_ref[0]
     gate = g_ref[0].astype(BF16)
@@ -68,17 +71,22 @@
     dh = dot_nt(dout, down)
     dzu = (dh * silu).astype(BF16)
     dzg = (dh * zu * sig * (1.0 + zg * (1.0 - sig))).astype(BF16)
-    grad_ref[0] = dot_tn(keys, dzg)
-    grad_ref[1] = dot_tn(keys, dzu)
-    grad_ref[2] = dot_tn(hidden, dout)
-    mine = pl.multiple_of(core * HALF, HALF)
-    other = pl.multiple_of((1 - core) * HALF, HALF)
+    grads = (dot_tn(keys, dzg), dot_tn(keys, dzu), dot_tn(hidden, dout))
     for mat in range(3):
-        for side in range(2):
-            cols = slice(side * HALF, (side + 1) * HALF)
-            at = slice(side * 16, (side + 1) * 16)
-            keep_ref[at, mat] = grad_ref[mat, pl.ds(mine, HALF), cols].reshape(16, 8, HALF)
-            send_ref[at, mat] = grad_ref[mat, pl.ds(other, HALF), cols].reshape(16, 8, HALF).astype(BF16)
+        grad = grads[mat].astype(BF16)
+        at = head * 3 + mat
+        for group in range(2):
+            slot = at - group * (GROUP - 1)
+            inside = (slot >= 0) & (slot < GROUP)
+            for ref, wanted in ((keep_ref, core == group), (send_ref, core != group)):
+
+                @pl.when(inside & wanted)
+                def _(ref=ref, slot=slot, grad=grad):
+                    for z in range(Z):
+                        side, block = z // 4, z % 4
+                        ref[slot // 2, z, slot % 2] = grad[
+                            block * ROWS : (block + 1) * ROWS, side * HALF : (side + 1) * HALF
+                        ]
 
 
 def split(x):
@@ -86,24 +94,14 @@
     return high, (x - high.astype(F32)).astype(BF16)
 
 
-def half_matrix(piece):
-    piece = piece.astype(F32)
-    left = piece[:16].reshape(HALF, HALF)
-    right = piece[16:].reshape(HALF, HALF)
-    return jnp.concatenate([left, right], axis=1)
-
-
-def orth_kernel(core_ref, *refs):
-    count = (len(refs) - 1) // 2
-    out_ref = refs[-1]
-    low_core = core_ref[0] == 0
+def orth_kernel(rows_ref, out_ref):
     xs = []
-    for i in range(count):
-        mine = half_matrix(refs[2 * i][:, 0])
-        other = half_matrix(refs[2 * i + 1][:, 0])
-        top = jnp.where(low_core, mine, other)
-        bottom = jnp.where(low_core, other, mine)
-        m = jnp.concatenate([top, bottom], axis=0)
+    for i in range(PER_Y):
+        sides = [
+            jnp.concatenate([rows_ref[side * 4 + block, i].astype(F32) for block in range(4)], axis=0)
+            for side in range(2)
+        ]
+        m = jnp.concatenate(sides, axis=1)
         norm = jnp.sqrt(jnp.sum(m * m, keepdims=True)) + 1e-07
         xs.append(m / norm)
     for sweep in range(NS_STEPS):
@@ -124,8 +122,9 @@
                 coef_first * x + (dot_f32(ph, h) + (dot_f32(ph, l) + dot_f32(pw, h)))
                 for x, (ph, pw), (h, l) in zip(xs, polys, parts)
             ]
-    for i in range(count):
-        out_ref[i] = xs[i].astype(BF16)
+    for i in range(PER_Y):
+        for y in range(Y):
+            out_ref[y, i] = xs[i].astype(BF16)
 
 
 def second_kernel(core_ref, buf_ref, q_ref, g_ref, u_ref, d_ref, mine_ref, other_ref, out_ref):
@@ -153,7 +152,10 @@
     def out_spec(block):
         return pl.BlockSpec((n_head, 1, rows // n_head, HD), lambda h, c: (0, block, 0, h))
 
-    piece_spec = pl.BlockSpec((PIECES, 3, 8, HALF), lambda h, c: (0, h, 0, 0))
+    piece_shape = (Y, Z, PER_Y, ROWS, HALF)
+    piece_spec = pl.BlockSpec(piece_shape, lambda h, c: (0, 0, 0, 0, 0))
+    args = (queries, key_rows, value_rows, step_rates, gate_fast, up_fast, down_fast)
+    in_hbm = [pltpu.with_memory_space_constraint(x, pltpu.HBM) for x in args]
     buf, keep, send = pl.pallas_call(
         first_kernel,
         grid_spec=pltpu.PrefetchScalarGridSpec(
@@ -169,43 +171,33 @@
                 weight_spec,
             ],
             out_specs=[out_spec(0), piece_spec, piece_spec],
-            scratch_shapes=[pltpu.VMEM((3, HD, HD), F32)],
         ),
         out_shape=[
             buf_shape,
-            jax.ShapeDtypeStruct((PIECES, MATS, 8, HALF), F32),
-            jax.ShapeDtypeStruct((PIECES, MATS, 8, HALF), BF16),
+            jax.ShapeDtypeStruct(piece_shape, BF16),
+            jax.ShapeDtypeStruct(piece_shape, BF16),
         ],
         compiler_params=params,
         name="first_and_grads",
-    )(core, queries, key_rows, value_rows, step_rates, gate_fast, up_fast, down_fast)
+    )(core, *in_hbm)
 
     swap = [(0, 1), (1, 0)]
     received = lax.ppermute(send, "core", swap)
-    chip_sum = (keep + received.astype(F32)).astype(BF16)
-    scattered = lax.all_to_all(chip_sum, ("z", "y"), split_axis=0, concat_axis=0, tiled=True)
-    piece = jnp.sum(scattered.astype(F32), axis=0).astype(BF16)
-    spread = jnp.broadcast_to(piece[None], (PIECES,) + piece.shape)
-    mine = lax.all_to_all(spread, ("z", "y"), split_axis=0, concat_axis=0, tiled=True)
-    other = lax.ppermute(mine, "core", swap)
-
-    per_step = 2
-    mat_specs = []
-    for i in range(per_step):
-        spec = pl.BlockSpec((PIECES, 1, 8, HALF), lambda s, c, i=i: (0, c[0] * (GROUP - 1) + s * per_step + i, 0, 0))
-        mat_specs += [spec, spec]
-    orth_mine = pl.pallas_call(
+    chip_sum = (keep.astype(F32) + received.astype(F32)).astype(BF16)
+    by_y = lax.all_to_all(chip_sum, "y", split_axis=0, concat_axis=0, tiled=True)
+    y_sum = jnp.sum(by_y.astype(F32), axis=0).astype(BF16)
+    by_z = lax.all_to_all(y_sum, "z", split_axis=0, concat_axis=0, tiled=True)
+    piece = jnp.sum(by_z.astype(F32), axis=0).astype(BF16)
+    spread = jnp.broadcast_to(piece[None], (Z,) + piece.shape)
+    whole = lax.all_to_all(spread, "z", split_axis=0, concat_axis=0, tiled=True)
+
+    orth = pl.pallas_call(
         orth_kernel,
-        grid_spec=pltpu.PrefetchScalarGridSpec(
-            num_scalar_prefetch=1,
-            grid=(GROUP // per_step,),
-            in_specs=mat_specs,
-            out_specs=pl.BlockSpec((per_step, HD, HD), lambda s, c: (s, 0, 0)),
-        ),
-        out_shape=jax.ShapeDtypeStruct((GROUP, HD, HD), BF16),
-        compiler_params=params,
+        out_shape=jax.ShapeDtypeStruct((Y, PER_Y, HD, HD), BF16),
+        compiler_params=pltpu.CompilerParams(vmem_limit_bytes=VMEM_LIMIT),
         name="orthogonalize",
-    )(core, *([mine, other] * per_step))
+    )(whole)
+    orth_mine = lax.all_to_all(orth, "y", split_axis=0, concat_axis=0, tiled=True).reshape(GROUP, HD, HD)
     orth_other = lax.ppermute(orth_mine, "core", swap)
 
     group_spec = pl.BlockSpec((GROUP, HD, HD), lambda h, c: (0, 0, 0))

time: 129 us -> 109 us (0.84)
  Pallas kernels: 20.8 us -> 13.1 us
  blocking collectives: 85.9 us -> 79.6 us
  local copies, waits for them, and re-layouts: 5.51 us -> 1.24 us
  waiting for transfers between devices: 6.67 us -> 4.57 us
  starting transfers between devices: 6.91 us -> 8.83 us
    pallas_call x1, Pallas kernels: 9.57 us -> 2.25 us  [local(): pl.pallas_call(orth_kernel, out_shape=jax.ShapeDtypeStruct((Y, PER_Y, HD,...]
    all_to_all x2 -> x4, blocking collectives: 65 us -> 58.7 us  [the longest x1 17.1 us: local(): lax.all_to_all(chip_sum, 'y', split_axis=0, concat_axis=0, tiled=True)]
    ppermute x1, starting transfers between devices: 0.46 us -> 5.51 us  [local(): orth_other = lax.ppermute(orth_mine, 'core', swap)]
    unnamed x12 -> x4, local copies, waits for them, and re-layouts: 4.19 us -> 0.01 us
    ppermute x1 -> x0, starting transfers between devices: 3.2 us -> none  [local(): other = lax.ppermute(mine, 'core', swap)]
    ppermute x1 -> x0, waiting for transfers between devices: 2.19 us -> none  [local(): other = lax.ppermute(mine, 'core', swap)]
  transfers between devices with their start and end apart: 3 -> 2, of which waited for: 3 -> 2; matrix products, arithmetic and copies ran while one was open for 0% -> 0% of each run, Pallas kernels for 0% -> 0%
where the time goes in v2:
time: 109 us; the launch traced here: 108 us
  blocking collectives  79.6 us (73%)
  Pallas kernels  13.1 us (12%)
  starting transfers between devices  8.83 us (8%)
  waiting for transfers between devices  4.57 us (4%)
  local copies, waits for them, and re-layouts  1.24 us (1%)
    all_to_all x1, blocking collectives, local(): lax.all_to_all(buf, 'head', split_axis=0, concat_axis=0, tiled=True)  20.9 us
    all_to_all x1, blocking collectives, local(): lax.all_to_all(chip_sum, 'y', split_axis=0, concat_axis=0, tiled=True)  17.1 us
    all_to_all x1, blocking collectives, local(): by_z = lax.all_to_all(y_sum, 'z', split_axis=0, concat_axis=0, tiled=True)  16.6 us
    all_to_all x1, blocking collectives, local(): lax.all_to_all(orth, 'y', split_axis=0, concat_axis=0, tiled=True)  13.1 us
    all_to_all x1, blocking collectives, local(): whole = lax.all_to_all(spread, 'z', split_axis=0, concat_axis=0, tiled=True)  11.9 us
    pallas_call x1, Pallas kernels, local(): pl.pallas_call(first_kernel, grid_spec=pltpu.PrefetchScalarGridSpec(num_s...  6.44 us
    ppermute x1, starting transfers between devices, local(): orth_other = lax.ppermute(orth_mine, 'core', swap)  5.51 us
    pallas_call x1, Pallas kernels, local(): pl.pallas_call(second_kernel, grid_spec=pltpu.PrefetchScalarGridSpec(num_...  4.43 us
  transfers between devices with their start and end apart: 2, of which 2 were waited for; matrix products, arithmetic and copies ran while one was open for 0% of the time, Pallas kernels for 0%

profile of v2, /device:TPU:1, one launch (start us, length us, event | category | flops | bytes accessed | tf_op | source)
XLA Modules:
  0.0 108.1 jit_solution(12012851830841139893)
XLA Ops:
  0.0 6.4 %first_and_grads.1 = (bf16[4,2,64,1280]{3,2,1,0:T(8,128)(2,1)S(1)}, bf16[4,8,2,64,128]{4,3,2,1,0:T(8,128)(2,1)S(1)}, bf16[4,8,2,64,128]{4,3,2,1,0:T(8,128)(2,1)S(1)}) custom-call(s32[1]{0:T(128)} %bitcast.core_ref, bf16[2,256,1280]{2,1,0:T(8,128)(2,1)} %q_ref.3, bf16[256,1280]{1,0:T(8,128)(2,1)} %k_ref.1, bf16[256,1280]{1,0:T(8,128)(2,1)} %v_ref.1, ...), custom_call_target="tpu_custom_call" | custom-call | tf_op jit(solution)/shard_map/first_and_grads/pallas_call | solution.py:159
  6.4 3.3 %collective-permute-start = (bf16[4,8,2,64,128]{4,3,2,1,0:T(8,128)(2,1)S(1)}, bf16[4,8,2,64,128]{4,3,2,1,0:T(8,128)(2,1)S(1)}, u32[]{:S(2)}, u32[]{:S(2)}) collective-permute-start(bf16[4,8,2,64,128]{4,3,2,1,0:T(8,128)(2,1)S(1)} %get-tuple-element.10), channel_id=1, source_target_pairs={{0,1},{1,0},{2,3},{3,2},{4,5},{5,4},{6,7},{7,6},{8,9},{9,8},{10,11... | collective-permute-start | bytes 3145736 | tf_op jit(solution)/shard_map/ppermute | solution.py:185
  9.8 2.3 %collective-permute-done = bf16[4,8,2,64,128]{4,3,2,1,0:T(8,128)(2,1)S(1)} collective-permute-done((bf16[4,8,2,64,128]{4,3,2,1,0:T(8,128)(2,1)S(1)}, bf16[4,8,2,64,128]{4,3,2,1,0:T(8,128)(2,1)S(1)}, u32[]{:S(2)}, u32[]{:S(2)}) %collective-permute-start) | collective-permute-done | bytes 1048608 | tf_op jit(solution)/shard_map/ppermute | solution.py:185
  12.1 0.5 add_convert_fusion
  12.6 17.1 %all_to_all.25 = bf16[4,8,2,64,128]{4,3,2,1,0:T(8,128)(2,1)S(1)} all-to-all(bf16[4,8,2,64,128]{4,3,2,1,0:T(8,128)(2,1)S(1)} %add_convert_fusion), channel_id=1, replica_groups=mesh['head'=4,'z'=8,'y'=4,'core'=2] {'y'}, dimensions={0} | all-to-all | bytes 2097152 | tf_op jit(solution)/shard_map/all_to_all | solution.py:187
  29.7 0.2 reduce_sum.24
  29.9 16.6 %all_to_all.26 = bf16[8,2,64,128]{3,2,1,0:T(8,128)(2,1)S(1)} all-to-all(bf16[8,2,64,128]{3,2,1,0:T(8,128)(2,1)S(1)} %reduce_sum.24), channel_id=1, replica_groups=mesh['head'=4,'z'=8,'y'=4,'core'=2] {'z'}, dimensions={0} | all-to-all | bytes 524288 | tf_op jit(solution)/shard_map/all_to_all | solution.py:189
  46.5 11.9 %all_to_all.27.rows_ref = bf16[8,2,64,128]{3,2,1,0:T(8,128)(2,1)S(1)} all-to-all(bf16[8,2,64,128]{3,2,1,0:T(8,128)(2,1)S(1)} %broadcast_in_dim.2), channel_id=1, replica_groups=mesh['head'=4,'z'=8,'y'=4,'core'=2] {'z'}, dimensions={0} | all-to-all | bytes 524288 | tf_op jit(solution)/shard_map/all_to_all | solution.py:192
  58.5 0.0 copy-start.1
  58.5 2.2 %orthogonalize.1 = bf16[4,2,256,256]{3,2,1,0:T(8,128)(2,1)S(1)} custom-call(bf16[8,2,64,128]{3,2,1,0:T(8,128)(2,1)S(1)} %all_to_all.27.rows_ref), custom_call_target="tpu_custom_call" | custom-call | tf_op jit(solution)/shard_map/orthogonalize/pallas_call | solution.py:194
  60.7 0.0 copy-start
  60.7 13.1 %all_to_all.28 = bf16[4,2,256,256]{3,2,1,0:T(8,128)(2,1)S(1)} all-to-all(bf16[4,2,256,256]{3,2,1,0:T(8,128)(2,1)S(1)} %orthogonalize.1), channel_id=1, replica_groups=mesh['head'=4,'z'=8,'y'=4,'core'=2] {'y'}, dimensions={0} | all-to-all | bytes 2097152 | tf_op jit(solution)/shard_map/all_to_all | solution.py:200
  73.8 5.5 %collective-permute-start.1 = (bf16[8,256,256]{2,1,0:T(8,128)(2,1)S(1)}, bf16[8,256,256]{2,1,0:T(8,128)(2,1)S(1)}, u32[]{:S(2)}, u32[]{:S(2)}) collective-permute-start(bf16[8,256,256]{2,1,0:T(8,128)(2,1)S(1)} %bitcast.5), channel_id=1, source_target_pairs={{0,1},{1,0},{2,3},{3,2},{4,5},{5,4},{6,7},{7,6},{8,9},{9,8},{10,11... | collective-permute-start | bytes 3145736 | tf_op jit(solution)/shard_map/ppermute | solution.py:201
  79.3 2.3 %collective-permute-done.1.other_ref = bf16[8,256,256]{2,1,0:T(8,128)(2,1)S(1)} collective-permute-done((bf16[8,256,256]{2,1,0:T(8,128)(2,1)S(1)}, bf16[8,256,256]{2,1,0:T(8,128)(2,1)S(1)}, u32[]{:S(2)}, u32[]{:S(2)}) %collective-permute-start.1) | collective-permute-done | bytes 1048608 | tf_op jit(solution)/shard_map/ppermute | solution.py:201
  81.6 0.0 copy-done.1
  81.6 0.0 copy-done
  81.6 4.4 %second.1 = bf16[4,2,64,1280]{3,2,1,0:T(8,128)(2,1)S(1)} custom-call(s32[1]{0:T(128)} %bitcast.core_ref, bf16[4,2,64,1280]{3,2,1,0:T(8,128)(2,1)S(1)} %get-tuple-element.8.buf_ref, bf16[2,256,1280]{2,1,0:T(8,128)(2,1)S(1)} %copy-done, f32[5,256,256]{2,1,0:T(8,128)S(1)} %copy-done.1, f32[5,256,256]{2,1,0:T(8,128)} %u_ref.3, ...), custom_call_target="tpu_custom_call", output_to_operand_aliasing={{}: (1, {})} | custom-call | tf_op jit(solution)/shard_map/second/pallas_call | solution.py:204
  86.1 20.9 %all_to_all.29 = bf16[4,2,64,1280]{3,2,1,0:T(8,128)(2,1)S(1)} all-to-all(bf16[4,2,64,1280]{3,2,1,0:T(8,128)(2,1)S(1)} %second.1), channel_id=1, replica_groups=mesh['head'=4,'z'=8,'y'=4,'core'=2] {'head'}, dimensions={0} | all-to-all | bytes 2621440 | tf_op jit(solution)/shard_map/all_to_all | solution.py:226
  106.9 1.2 %copy.11 = bf16[4,2,8,8,1280]{4,3,0,2,1:T(8,128)(2,1)} copy(bf16[4,2,8,8,1280]{4,3,2,1,0:T(8,128)(2,1)S(1)} %bitcast.7) | data formatting | bytes 2621440 | tf_op jit(solution)/shard_map/reshape | solution.py:227
  (2 shorter events, 0.1 us)
Async XLA Ops:
  6.4 5.6 %collective-permute-start = (bf16[4,8,2,64,128]{4,3,2,1,0:T(8,128)(2,1)S(1)}, bf16[4,8,2,64,128]{4,3,2,1,0:T(8,128)(2,1)S(1)}, u32[]{:S(2)}, u32[]{:S(2)}) collective-permute-start(bf16[4,8,2,64,128]{4,3,2,1,0:T(8,128)(2,1)S(1)} %get-tuple-element.10), channel_id=1, source_target_pairs={{0,1},{1,0},{2,3},{3,2},{4,5},{5,4},{6,7},{7,6},{8,9},{9,8},{10,11... | collective-permute-start | bytes 3145736 | tf_op jit(solution)/shard_map/ppermute | solution.py:185
  58.5 23.2 %copy-start.1 = (f32[5,256,256]{2,1,0:T(8,128)S(1)}, f32[5,256,256]{2,1,0:T(8,128)}, u32[]{:S(2)}) copy-start(f32[5,256,256]{2,1,0:T(8,128)} %g_ref.3) | copy-start | bytes 3932164
  60.7 20.9 %copy-start = (bf16[2,256,1280]{2,1,0:T(8,128)(2,1)S(1)}, bf16[2,256,1280]{2,1,0:T(8,128)(2,1)}, u32[]{:S(2)}) copy-start(bf16[2,256,1280]{2,1,0:T(8,128)(2,1)} %q_ref.3) | copy-start | bytes 3932164
  73.8 7.8 %collective-permute-start.1 = (bf16[8,256,256]{2,1,0:T(8,128)(2,1)S(1)}, bf16[8,256,256]{2,1,0:T(8,128)(2,1)S(1)}, u32[]{:S(2)}, u32[]{:S(2)}) collective-permute-start(bf16[8,256,256]{2,1,0:T(8,128)(2,1)S(1)} %bitcast.5), channel_id=1, source_target_pairs={{0,1},{1,0},{2,3},{3,2},{4,5},{5,4},{6,7},{7,6},{8,9},{9,8},{10,11... | collective-permute-start | bytes 3145736 | tf_op jit(solution)/shard_map/ppermute | solution.py:201

commit v3 on v2

--- a/solution.py
+++ b/solution.py
@@ -19,6 +19,7 @@
 Y = 4
 Z = 8
 PER_Y = GROUP // Y
+OWN_HEADS = 2
 ROWS = 64
 VMEM_LIMIT = 48 * 1024 * 1024
 
@@ -46,18 +47,17 @@
     return dot_f32(hidden, down).astype(BF16)
 
 
-def store_rows(out_ref, rows):
-    for r in range(out_ref.shape[0]):
-        out_ref[r, 0] = rows[r * 64 : (r + 1) * 64, :]
-
-
-def first_kernel(core_ref, q_ref, k_ref, v_ref, rate_ref, g_ref, u_ref, d_ref, out_ref, keep_ref, send_ref):
+def first_kernel(q_ref, g_ref, u_ref, d_ref, out_ref):
+    weights = [ref[0].astype(BF16) for ref in (g_ref, u_ref, d_ref)]
+    out_ref[...] = apply_fast(q_ref[0], *weights)
+
+
+def grad_kernel(core_ref, k_ref, v_ref, rate_ref, g_ref, u_ref, d_ref, keep_ref, send_ref):
     head = pl.program_id(0)
     core = core_ref[0]
     gate = g_ref[0].astype(BF16)
     up = u_ref[0].astype(BF16)
     down = d_ref[0].astype(BF16)
-    store_rows(out_ref, apply_fast(q_ref[0], gate, up, down))
     keys = k_ref[...]
     zg = dot_f32(keys, gate)
     zu = dot_f32(keys, up)
@@ -71,9 +71,10 @@
     dh = dot_nt(dout, down)
     dzu = (dh * silu).astype(BF16)
     dzg = (dh * zu * sig * (1.0 + zg * (1.0 - sig))).astype(BF16)
-    grads = (dot_tn(keys, dzg), dot_tn(keys, dzu), dot_tn(hidden, dout))
+    pair = dot_tn(keys, jnp.concatenate([dzg, dzu], axis=1)).astype(BF16)
+    grads = (pair[:, :HD], pair[:, HD:], dot_tn(hidden, dout).astype(BF16))
     for mat in range(3):
-        grad = grads[mat].astype(BF16)
+        grad = grads[mat]
         at = head * 3 + mat
         for group in range(2):
             slot = at - group * (GROUP - 1)
@@ -127,8 +128,19 @@
             out_ref[y, i] = xs[i].astype(BF16)
 
 
-def second_kernel(core_ref, buf_ref, q_ref, g_ref, u_ref, d_ref, mine_ref, other_ref, out_ref):
-    head = pl.program_id(0)
+def next_weight(fast, orth):
+    return (fast - orth.astype(F32)).astype(BF16)
+
+
+def own_second_kernel(core_ref, heads_ref, q_ref, g_ref, u_ref, d_ref, mine_ref, out_ref):
+    head = heads_ref[pl.program_id(0)]
+    base = head * 3 - core_ref[0] * (GROUP - 1)
+    nexts = [next_weight(ref[0], mine_ref[base + mat]) for mat, ref in enumerate((g_ref, u_ref, d_ref))]
+    out_ref[...] = apply_fast(q_ref[0], *nexts)
+
+
+def rest_second_kernel(core_ref, heads_ref, buf_ref, q_ref, g_ref, u_ref, d_ref, mine_ref, other_ref, out_ref):
+    head = heads_ref[OWN_HEADS + pl.program_id(0)]
     low_core = core_ref[0] == 0
     nexts = []
     for mat, ref in enumerate((g_ref, u_ref, d_ref)):
@@ -136,8 +148,13 @@
         in_low = at < GROUP
         index = jnp.where(in_low, at, at - (GROUP - 1))
         orth = jnp.where(in_low == low_core, mine_ref[index], other_ref[index])
-        nexts.append((ref[0] - orth.astype(F32)).astype(BF16))
-    store_rows(out_ref, apply_fast(q_ref[0], *nexts))
+        nexts.append(next_weight(ref[0], orth))
+    out_ref[...] = apply_fast(q_ref[0], *nexts)
+
+
+def join_kernel(place_ref, first_ref, second_ref, out_ref):
+    out_ref[0] = first_ref[0]
+    out_ref[1] = second_ref[0]
 
 
 def local(queries, key_rows, value_rows, step_rates, gate_fast, up_fast, down_fast):
@@ -145,44 +162,51 @@
     width = key_rows.shape[1]
     core = lax.axis_index("core").astype(jnp.int32).reshape(1)
     n_head = lax.axis_size("head")
+    part = rows // n_head
     params = pltpu.CompilerParams(dimension_semantics=("arbitrary",), vmem_limit_bytes=VMEM_LIMIT)
-    weight_spec = pl.BlockSpec((1, HD, HD), lambda h, c: (h, 0, 0))
-    buf_shape = jax.ShapeDtypeStruct((n_head, 2, rows // n_head, width), BF16)
-
-    def out_spec(block):
-        return pl.BlockSpec((n_head, 1, rows // n_head, HD), lambda h, c: (0, block, 0, h))
+    weight_spec = pl.BlockSpec((1, HD, HD), lambda h, *_: (h, 0, 0))
+    rows_spec = pl.BlockSpec((rows, HD), lambda h, *_: (0, h))
+    rows_shape = jax.ShapeDtypeStruct((rows, width), BF16)
 
     piece_shape = (Y, Z, PER_Y, ROWS, HALF)
     piece_spec = pl.BlockSpec(piece_shape, lambda h, c: (0, 0, 0, 0, 0))
     args = (queries, key_rows, value_rows, step_rates, gate_fast, up_fast, down_fast)
-    in_hbm = [pltpu.with_memory_space_constraint(x, pltpu.HBM) for x in args]
-    buf, keep, send = pl.pallas_call(
-        first_kernel,
+    q_hbm, k_hbm, v_hbm, rate_hbm, g_hbm, u_hbm, d_hbm = [
+        pltpu.with_memory_space_constraint(x, pltpu.HBM) for x in args
+    ]
+    keep, send = pl.pallas_call(
+        grad_kernel,
         grid_spec=pltpu.PrefetchScalarGridSpec(
             num_scalar_prefetch=1,
             grid=(HEADS_HERE,),
             in_specs=[
-                pl.BlockSpec((1, rows, HD), lambda h, c: (0, 0, h)),
-                pl.BlockSpec((rows, HD), lambda h, c: (0, h)),
-                pl.BlockSpec((rows, HD), lambda h, c: (0, h)),
+                rows_spec,
+                rows_spec,
                 pl.BlockSpec((HEADS_HERE, rows), lambda h, c: (0, 0)),
                 weight_spec,
                 weight_spec,
                 weight_spec,
             ],
-            out_specs=[out_spec(0), piece_spec, piece_spec],
-        ),
-        out_shape=[
-            buf_shape,
-            jax.ShapeDtypeStruct(piece_shape, BF16),
-            jax.ShapeDtypeStruct(piece_shape, BF16),
-        ],
-        compiler_params=params,
-        name="first_and_grads",
-    )(core, *in_hbm)
+            out_specs=[piece_spec, piece_spec],
+        ),
+        out_shape=[jax.ShapeDtypeStruct(piece_shape, BF16), jax.ShapeDtypeStruct(piece_shape, BF16)],
+        compiler_params=params,
+        name="grads",
+    )(core, k_hbm, v_hbm, rate_hbm, g_hbm, u_hbm, d_hbm)
 
     swap = [(0, 1), (1, 0)]
     received = lax.ppermute(send, "core", swap)
+    first = pl.pallas_call(
+        first_kernel,
+        grid=(HEADS_HERE,),
+        in_specs=[pl.BlockSpec((1, rows, HD), lambda h: (0, 0, h)), weight_spec, weight_spec, weight_spec],
+        out_specs=rows_spec,
+        out_shape=rows_shape,
+        compiler_params=params,
+        name="first",
+    )(q_hbm, g_hbm, u_hbm, d_hbm)
+    first_all = lax.all_gather(first, "head", axis=0)
+
     chip_sum = (keep.astype(F32) + received.astype(F32)).astype(BF16)
     by_y = lax.all_to_all(chip_sum, "y", split_axis=0, concat_axis=0, tiled=True)
     y_sum = jnp.sum(by_y.astype(F32), axis=0).astype(BF16)
@@ -200,31 +224,59 @@
     orth_mine = lax.all_to_all(orth, "y", split_axis=0, concat_axis=0, tiled=True).reshape(GROUP, HD, HD)
     orth_other = lax.ppermute(orth_mine, "core", swap)
 
-    group_spec = pl.BlockSpec((GROUP, HD, HD), lambda h, c: (0, 0, 0))
-    buf = pl.pallas_call(
-        second_kernel,
+    def second_specs(start):
+        def at(s, heads):
+            return heads[start + s]
+
+        query = pl.BlockSpec((1, rows, HD), lambda s, c, heads: (1, 0, at(s, heads)))
+        weight = pl.BlockSpec((1, HD, HD), lambda s, c, heads: (at(s, heads), 0, 0))
+        out = pl.BlockSpec((rows, HD), lambda s, c, heads: (0, at(s, heads)))
+        return [query, weight, weight, weight], out
+
+    heads = (jnp.arange(HEADS_HERE, dtype=jnp.int32) + core * (HEADS_HERE - OWN_HEADS)) % HEADS_HERE
+    group_spec = pl.BlockSpec((GROUP, HD, HD), lambda s, c, heads: (0, 0, 0))
+    specs, out_spec = second_specs(0)
+    second = pl.pallas_call(
+        own_second_kernel,
+        grid_spec=pltpu.PrefetchScalarGridSpec(
+            num_scalar_prefetch=2, grid=(OWN_HEADS,), in_specs=specs + [group_spec], out_specs=out_spec
+        ),
+        out_shape=rows_shape,
+        compiler_params=params,
+        name="second_own",
+    )(core, heads, queries, gate_fast, up_fast, down_fast, orth_mine)
+    specs, out_spec = second_specs(OWN_HEADS)
+    second = pl.pallas_call(
+        rest_second_kernel,
+        grid_spec=pltpu.PrefetchScalarGridSpec(
+            num_scalar_prefetch=2,
+            grid=(HEADS_HERE - OWN_HEADS,),
+            in_specs=[pl.BlockSpec(memory_space=pl.ANY)] + specs + [group_spec, group_spec],
+            out_specs=out_spec,
+        ),
+        out_shape=rows_shape,
+        input_output_aliases={2: 0},
+        compiler_params=params,
+        name="second_rest",
+    )(core, heads, second, queries, gate_fast, up_fast, down_fast, orth_mine, orth_other)
+
+    swapped = lax.all_to_all(second.reshape(n_head, part, width), "head", split_axis=0, concat_axis=0, tiled=True)
+    place = lax.axis_index("head").astype(jnp.int32).reshape(1)
+    return pl.pallas_call(
+        join_kernel,
         grid_spec=pltpu.PrefetchScalarGridSpec(
             num_scalar_prefetch=1,
-            grid=(HEADS_HERE,),
+            grid=(n_head,),
             in_specs=[
-                pl.BlockSpec(memory_space=pl.ANY),
-                pl.BlockSpec((1, rows, HD), lambda h, c: (1, 0, h)),
-                weight_spec,
-                weight_spec,
-                weight_spec,
-                group_spec,
-                group_spec,
+                pl.BlockSpec((1, part, width), lambda s, p: (s, p[0], 0)),
+                pl.BlockSpec((1, part, width), lambda s, p: (s, 0, 0)),
             ],
-            out_specs=out_spec(1),
-        ),
-        out_shape=buf_shape,
-        input_output_aliases={1: 0},
-        compiler_params=params,
-        name="second",
-    )(core, buf, queries, gate_fast, up_fast, down_fast, orth_mine, orth_other)
-
-    swapped = lax.all_to_all(buf, "head", split_axis=0, concat_axis=0, tiled=True)
-    return swapped.transpose(1, 2, 0, 3).reshape(2, rows // n_head, n_head * width)
+            out_specs=pl.BlockSpec((2, part, width), lambda s, p: (0, 0, s)),
+        ),
+        out_shape=jax.ShapeDtypeStruct((2, part, n_head * width), BF16),
+        compiler_params=params,
+        name="join",
+    )(place, pltpu.with_memory_space_constraint(first_all, pltpu.HBM), swapped)
 
 
 def solution(mesh):

time: 109 us -> 120 us (1.10)
  blocking collectives: 79.6 us -> 42.4 us
  waiting for transfers between devices: 4.57 us -> 22.2 us
  between operations: 0.06 us -> 13.5 us
  Pallas kernels: 13.1 us -> 24.2 us
  starting transfers between devices: 8.83 us -> 15.7 us
    all_to_all x2 -> x0, blocking collectives: 38 us -> none  [the longest x1 20.9 us: local(): lax.all_to_all(buf, 'head', split_axis=0, concat_axis=0, tiled=True)]
    all_to_all x0 -> x2, waiting for transfers between devices: none -> 19.9 us  [the longest x1 10.7 us: local(): lax.all_to_all(second.reshape(n_head, part, width), 'head', split_axis=0,...]
    pallas_call x2 -> x5, Pallas kernels: 10.9 us -> 22 us  [the longest x1 5.88 us: local(): pl.pallas_call(grad_kernel, grid_spec=pltpu.PrefetchScalarGridSpec(num_sc...]
    all_to_all x0 -> x2, starting transfers between devices: none -> 7.53 us  [the longest x1 4.01 us: local(): lax.all_to_all(second.reshape(n_head, part, width), 'head', split_axis=0,...]
    ppermute x1, waiting for transfers between devices: 2.29 us -> 0.01 us  [local(): orth_other = lax.ppermute(orth_mine, 'core', swap)]
  transfers between devices with their start and end apart: 2 -> 5, of which waited for: 2 -> 3; matrix products, arithmetic and copies ran while one was open for 0% -> 0% of each run, Pallas kernels for 0% -> 13%
where the time goes in v3:
time: 120 us
  blocking collectives  42.4 us (35%)
  Pallas kernels  24.2 us (20%)
  waiting for transfers between devices  22.2 us (18%)
  starting transfers between devices  15.7 us (13%)
  between operations  13.5 us (11%)
  other arithmetic  1.62 us (1%)
    all_to_all x1, blocking collectives, local(): by_z = lax.all_to_all(y_sum, 'z', split_axis=0, concat_axis=0, tiled=True)  16.1 us
    all_to_all x1, blocking collectives, local(): lax.all_to_all(orth, 'y', split_axis=0, concat_axis=0, tiled=True)  13.8 us
    all_to_all x1, blocking collectives, local(): whole = lax.all_to_all(spread, 'z', split_axis=0, concat_axis=0, tiled=True)  12.5 us
    all_to_all x1, waiting for transfers between devices, local(): lax.all_to_all(second.reshape(n_head, part, width), 'head', split_axis=0,...  10.7 us
    all_to_all x1, waiting for transfers between devices, local(): lax.all_to_all(chip_sum, 'y', split_axis=0, concat_axis=0, tiled=True)  9.17 us
    pallas_call x1, Pallas kernels, local(): pl.pallas_call(grad_kernel, grid_spec=pltpu.PrefetchScalarGridSpec(num_sc...  5.88 us
    pallas_call x1, Pallas kernels, local(): pl.pallas_call(first_kernel, grid=(HEADS_HERE,), in_specs=[pl.BlockSpec((...  5.57 us
    ppermute x1, starting transfers between devices, local(): orth_other = lax.ppermute(orth_mine, 'core', swap)  4.82 us
  transfers between devices with their start and end apart: 5, of which 3 were waited for; matrix products, arithmetic and copies ran while one was open for 0% of the time, Pallas kernels for 13%

profile of v3, /device:TPU:1, one launch (start us, length us, event | category | flops | bytes accessed | tf_op | source)
XLA Modules:
  0.0 119.7 jit_solution(495920649675958668)
XLA Ops:
  6.5 5.9 %grads.1 = (bf16[4,8,2,64,128]{4,3,2,1,0:T(8,128)(2,1)S(1)}, bf16[4,8,2,64,128]{4,3,2,1,0:T(8,128)(2,1)S(1)}) custom-call(s32[1]{0:T(128)} %bitcast.2.core_ref, bf16[256,1280]{1,0:T(8,128)(2,1)} %k_ref.1, bf16[256,1280]{1,0:T(8,128)(2,1)} %v_ref.1, f32[5,256]{1,0:T(8,128)} %rate_ref.1, f32[5,256,256]{2,1,0:T(8,128)} %g_ref.7, f32[5,256,256]{2,1,0:T(8,128)} %u_ref.7, ...), custom_call_target="tpu_custom_call" | custom-call | tf_op jit(solution)/shard_map/grads/pallas_call | solution.py:177
  12.4 3.3 %collective-permute-start = (bf16[4,8,2,64,128]{4,3,2,1,0:T(8,128)(2,1)S(1)}, bf16[4,8,2,64,128]{4,3,2,1,0:T(8,128)(2,1)S(1)}, u32[]{:S(2)}, u32[]{:S(2)}) collective-permute-start(bf16[4,8,2,64,128]{4,3,2,1,0:T(8,128)(2,1)S(1)} %get-tuple-element.8), channel_id=1, source_target_pairs={{0,1},{1,0},{2,3},{3,2},{4,5},{5,4},{6,7},{7,6},{8,9},{9,8},{10,11... | collective-permute-start | bytes 3145736 | tf_op jit(solution)/shard_map/ppermute | solution.py:198
  15.7 2.3 %collective-permute-done = bf16[4,8,2,64,128]{4,3,2,1,0:T(8,128)(2,1)S(1)} collective-permute-done((bf16[4,8,2,64,128]{4,3,2,1,0:T(8,128)(2,1)S(1)}, bf16[4,8,2,64,128]{4,3,2,1,0:T(8,128)(2,1)S(1)}, u32[]{:S(2)}, u32[]{:S(2)}) %collective-permute-start) | collective-permute-done | bytes 1048608 | tf_op jit(solution)/shard_map/ppermute | solution.py:198
  18.0 1.4 %add_convert_fusion = bf16[4,8,2,64,128]{4,3,2,1,0:T(8,128)(2,1)} fusion(bf16[4,8,2,64,128]{4,3,2,1,0:T(8,128)(2,1)S(1)} %collective-permute-done, bf16[4,8,2,64,128]{4,3,2,1,0:T(8,128)(2,1)S(1)} %get-tuple-element.7), kind=kLoop, calls=%fused_computation | loop fusion | flops 2097152 | bytes 3145728 | tf_op jit(solution)/shard_map/convert_element_type | solution.py:210
  19.4 3.5 %all-to-all-start = ((bf16[4,8,2,64,128]{4,3,2,1,0:T(8,128)(2,1)}), bf16[4,8,2,64,128]{4,3,2,1,0:T(8,128)(2,1)S(1)}, u32[]{:S(2)}, u32[]{:S(2)}) async-start(bf16[4,8,2,64,128]{4,3,2,1,0:T(8,128)(2,1)} %add_convert_fusion), calls=%async_computation | async-start | bytes 2097152 | tf_op jit(solution)/shard_map/all_to_all | solution.py:211
  22.9 0.0 all-gather.3.cloned.1.call-start
  23.0 5.6 %first.1 = bf16[256,1280]{1,0:T(8,128)(2,1)} custom-call(bf16[2,256,1280]{2,1,0:T(8,128)(2,1)} %q_ref.5, f32[5,256,256]{2,1,0:T(8,128)} %g_ref.7, f32[5,256,256]{2,1,0:T(8,128)} %u_ref.7, f32[5,256,256]{2,1,0:T(8,128)} %d_ref.7), custom_call_target="tpu_custom_call" | custom-call | tf_op jit(solution)/shard_map/first/pallas_call | solution.py:199
  28.5 0.0 all-gather.3.cloned.1.call-update
  28.6 9.2 %all-to-all-done = bf16[4,8,2,64,128]{4,3,2,1,0:T(8,128)(2,1)S(1)} async-done(((bf16[4,8,2,64,128]{4,3,2,1,0:T(8,128)(2,1)}), bf16[4,8,2,64,128]{4,3,2,1,0:T(8,128)(2,1)S(1)}, u32[]{:S(2)}, u32[]{:S(2)}) %all-to-all-start) | async-done | bytes 1048608 | tf_op jit(solution)/shard_map/all_to_all | solution.py:211
  37.7 0.2 reduce_sum.24
  37.9 16.1 %all_to_all.25 = bf16[8,2,64,128]{3,2,1,0:T(8,128)(2,1)S(1)} all-to-all(bf16[8,2,64,128]{3,2,1,0:T(8,128)(2,1)S(1)} %reduce_sum.24), channel_id=1, replica_groups=mesh['head'=4,'z'=8,'y'=4,'core'=2] {'z'}, dimensions={0} | all-to-all | bytes 524288 | tf_op jit(solution)/shard_map/all_to_all | solution.py:213
  54.1 0.0 copy-start.2
  54.1 12.5 %all_to_all.26.rows_ref = bf16[8,2,64,128]{3,2,1,0:T(8,128)(2,1)S(1)} all-to-all(bf16[8,2,64,128]{3,2,1,0:T(8,128)(2,1)S(1)} %broadcast_in_dim.2), channel_id=1, replica_groups=mesh['head'=4,'z'=8,'y'=4,'core'=2] {'z'}, dimensions={0} | all-to-all | bytes 524288 | tf_op jit(solution)/shard_map/all_to_all | solution.py:216
  66.6 0.0 copy-start.1
  66.6 2.3 %orthogonalize.1 = bf16[4,2,256,256]{3,2,1,0:T(8,128)(2,1)S(1)} custom-call(bf16[8,2,64,128]{3,2,1,0:T(8,128)(2,1)S(1)} %all_to_all.26.rows_ref), custom_call_target="tpu_custom_call" | custom-call | tf_op jit(solution)/shard_map/orthogonalize/pallas_call | solution.py:218
  68.9 0.0 copy-start
  68.9 13.8 %all_to_all.27 = bf16[4,2,256,256]{3,2,1,0:T(8,128)(2,1)S(1)} all-to-all(bf16[4,2,256,256]{3,2,1,0:T(8,128)(2,1)S(1)} %orthogonalize.1), channel_id=1, replica_groups=mesh['head'=4,'z'=8,'y'=4,'core'=2] {'y'}, dimensions={0} | all-to-all | bytes 2097152 | tf_op jit(solution)/shard_map/all_to_all | solution.py:224
  82.7 4.8 %collective-permute-start.1 = (bf16[8,256,256]{2,1,0:T(8,128)(2,1)S(1)}, bf16[8,256,256]{2,1,0:T(8,128)(2,1)S(1)}, u32[]{:S(2)}, u32[]{:S(2)}) collective-permute-start(bf16[8,256,256]{2,1,0:T(8,128)(2,1)S(1)} %bitcast.6), channel_id=1, source_target_pairs={{0,1},{1,0},{2,3},{3,2},{4,5},{5,4},{6,7},{7,6},{8,9},{9,8},{10,11... | collective-permute-start | bytes 3145736 | tf_op jit(solution)/shard_map/ppermute | solution.py:225
  87.5 0.0 copy-done.2
  87.5 0.0 copy-done.1
  87.5 0.0 copy-done
  87.6 3.0 %second_own.1.buf_ref = bf16[256,1280]{1,0:T(8,128)(2,1)} custom-call(s32[1]{0:T(128)} %bitcast.2.core_ref, s32[5]{0:T(128)S(1)} %and_select_fusion.heads_ref, bf16[2,256,1280]{2,1,0:T(8,128)(2,1)S(1)} %copy-done.2, f32[5,256,256]{2,1,0:T(8,128)S(1)} %copy-done, f32[5,256,256]{2,1,0:T(8,128)S(1)} %copy-done.1, f32[5,256,256]{2,1,0:T(8,128)} %d_ref.7, ...), custom_call_target="tpu_custom_call" | custom-call | tf_op jit(solution)/shard_map/second_own/pallas_call | solution.py:239
  90.6 0.0 collective-permute-done.1.other_ref
  90.6 4.2 %second_rest.1 = bf16[256,1280]{1,0:T(8,128)(2,1)} custom-call(s32[1]{0:T(128)} %bitcast.2.core_ref, s32[5]{0:T(128)S(1)} %and_select_fusion.heads_ref, bf16[256,1280]{1,0:T(8,128)(2,1)} %second_own.1.buf_ref, bf16[2,256,1280]{2,1,0:T(8,128)(2,1)S(1)} %copy-done.2, f32[5,256,256]{2,1,0:T(8,128)S(1)} %copy-done, ...), custom_call_target="tpu_custom_call", output_to_operand_aliasing={{}: (2, {})} | custom-call | tf_op jit(solution)/shard_map/second_rest/pallas_call | solution.py:249
  94.8 4.0 %all-to-all-start.4 = ((bf16[4,64,1280]{2,1,0:T(8,128)(2,1)}), bf16[4,64,1280]{2,1,0:T(8,128)(2,1)S(1)}, u32[]{:S(2)}, u32[]{:S(2)}) async-start(bf16[4,64,1280]{2,1,0:T(8,128)(2,1)} %bitcast.5), calls=%async_computation.4 | async-start | bytes 1310720 | tf_op jit(solution)/shard_map/all_to_all | solution.py:263
  98.8 0.0 all-gather.3.cloned.1.call-done
  98.8 10.7 %all-to-all-done.4.second_ref = bf16[4,64,1280]{2,1,0:T(8,128)(2,1)S(1)} async-done(((bf16[4,64,1280]{2,1,0:T(8,128)(2,1)}), bf16[4,64,1280]{2,1,0:T(8,128)(2,1)S(1)}, u32[]{:S(2)}, u32[]{:S(2)}) %all-to-all-start.4) | async-done | bytes 655392 | tf_op jit(solution)/shard_map/all_to_all | solution.py:263
  109.5 3.3 %join.1 = bf16[2,64,5120]{2,1,0:T(8,128)(2,1)} custom-call(s32[1]{0:T(128)} %bitcast.place_ref, bf16[4,256,1280]{2,1,0:T(8,128)(2,1)} %bitcast.9, bf16[4,64,1280]{2,1,0:T(8,128)(2,1)S(1)} %all-to-all-done.4.second_ref), custom_call_target="tpu_custom_call" | custom-call | tf_op jit(solution)/shard_map/join/pallas_call | solution.py:265
  (3 shorter events, 0.1 us)
Async XLA Ops:
  12.4 5.6 %collective-permute-start = (bf16[4,8,2,64,128]{4,3,2,1,0:T(8,128)(2,1)S(1)}, bf16[4,8,2,64,128]{4,3,2,1,0:T(8,128)(2,1)S(1)}, u32[]{:S(2)}, u32[]{:S(2)}) collective-permute-start(bf16[4,8,2,64,128]{4,3,2,1,0:T(8,128)(2,1)S(1)} %get-tuple-element.8), channel_id=1, source_target_pairs={{0,1},{1,0},{2,3},{3,2},{4,5},{5,4},{6,7},{7,6},{8,9},{9,8},{10,11... | collective-permute-start | bytes 3145736 | tf_op jit(solution)/shard_map/ppermute | solution.py:198
  19.4 18.3 %all-to-all-start = ((bf16[4,8,2,64,128]{4,3,2,1,0:T(8,128)(2,1)}), bf16[4,8,2,64,128]{4,3,2,1,0:T(8,128)(2,1)S(1)}, u32[]{:S(2)}, u32[]{:S(2)}) async-start(bf16[4,8,2,64,128]{4,3,2,1,0:T(8,128)(2,1)} %add_convert_fusion), calls=%async_computation | async-start | bytes 2097152 | tf_op jit(solution)/shard_map/all_to_all | solution.py:211
  22.9 75.8 %all-gather.3.cloned.1.call-start = ((), (), s32[]{:S(2)}) async-start(), calls=%async_computation.5 | async-start | bytes 3276800 | tf_op jit(solution)/shard_map/all_gather | solution.py:208
  54.1 33.4 %copy-start.2 = (bf16[2,256,1280]{2,1,0:T(8,128)(2,1)S(1)}, bf16[2,256,1280]{2,1,0:T(8,128)(2,1)}, u32[]{:S(2)}) copy-start(bf16[2,256,1280]{2,1,0:T(8,128)(2,1)} %q_ref.5) | copy-start | bytes 3932164
  66.6 20.9 %copy-start.1 = (f32[5,256,256]{2,1,0:T(8,128)S(1)}, f32[5,256,256]{2,1,0:T(8,128)}, u32[]{:S(2)}) copy-start(f32[5,256,256]{2,1,0:T(8,128)} %u_ref.7) | copy-start | bytes 3932164
  68.9 18.6 %copy-start = (f32[5,256,256]{2,1,0:T(8,128)S(1)}, f32[5,256,256]{2,1,0:T(8,128)}, u32[]{:S(2)}) copy-start(f32[5,256,256]{2,1,0:T(8,128)} %g_ref.7) | copy-start | bytes 3932164
  82.7 7.9 %collective-permute-start.1 = (bf16[8,256,256]{2,1,0:T(8,128)(2,1)S(1)}, bf16[8,256,256]{2,1,0:T(8,128)(2,1)S(1)}, u32[]{:S(2)}, u32[]{:S(2)}) collective-permute-start(bf16[8,256,256]{2,1,0:T(8,128)(2,1)S(1)} %bitcast.6), channel_id=1, source_target_pairs={{0,1},{1,0},{2,3},{3,2},{4,5},{5,4},{6,7},{7,6},{8,9},{9,8},{10,11... | collective-permute-start | bytes 3145736 | tf_op jit(solution)/shard_map/ppermute | solution.py:225
  94.8 14.7 %all-to-all-start.4 = ((bf16[4,64,1280]{2,1,0:T(8,128)(2,1)}), bf16[4,64,1280]{2,1,0:T(8,128)(2,1)S(1)}, u32[]{:S(2)}, u32[]{:S(2)}) async-start(bf16[4,64,1280]{2,1,0:T(8,128)(2,1)} %bitcast.5), calls=%async_computation.4 | async-start | bytes 1310720 | tf_op jit(solution)/shard_map/all_to_all | solution.py:263
Sparse Core Ops, SparseCore 0:
  28.7 39.8 all-gather.2

commit v4 on v3

--- a/solution.py
+++ b/solution.py
@@ -19,7 +19,6 @@
 Y = 4
 Z = 8
 PER_Y = GROUP // Y
-OWN_HEADS = 2
 ROWS = 64
 VMEM_LIMIT = 48 * 1024 * 1024
 
@@ -47,9 +46,15 @@
     return dot_f32(hidden, down).astype(BF16)
 
 
-def first_kernel(q_ref, g_ref, u_ref, d_ref, out_ref):
+def first_kernel(place_ref, q_ref, g_ref, u_ref, d_ref, *refs):
+    out_refs, rows_ref = refs[:-1], refs[-1]
     weights = [ref[0].astype(BF16) for ref in (g_ref, u_ref, d_ref)]
-    out_ref[...] = apply_fast(q_ref[0], *weights)
+    rows_ref[...] = apply_fast(q_ref[0], *weights)
+    count = len(out_refs)
+    part = rows_ref.shape[0] // count
+    for hop, out_ref in enumerate(out_refs):
+        to = lax.rem(place_ref[0] + hop, count)
+        out_ref[...] = rows_ref[pl.ds(pl.multiple_of(to * part, part), part), :]
 
 
 def grad_kernel(core_ref, k_ref, v_ref, rate_ref, g_ref, u_ref, d_ref, keep_ref, send_ref):
@@ -132,15 +137,8 @@
     return (fast - orth.astype(F32)).astype(BF16)
 
 
-def own_second_kernel(core_ref, heads_ref, q_ref, g_ref, u_ref, d_ref, mine_ref, out_ref):
-    head = heads_ref[pl.program_id(0)]
-    base = head * 3 - core_ref[0] * (GROUP - 1)
-    nexts = [next_weight(ref[0], mine_ref[base + mat]) for mat, ref in enumerate((g_ref, u_ref, d_ref))]
-    out_ref[...] = apply_fast(q_ref[0], *nexts)
-
-
-def rest_second_kernel(core_ref, heads_ref, buf_ref, q_ref, g_ref, u_ref, d_ref, mine_ref, other_ref, out_ref):
-    head = heads_ref[OWN_HEADS + pl.program_id(0)]
+def second_kernel(core_ref, q_ref, g_ref, u_ref, d_ref, mine_ref, other_ref, out_ref):
+    head = pl.program_id(0)
     low_core = core_ref[0] == 0
     nexts = []
     for mat, ref in enumerate((g_ref, u_ref, d_ref)):
@@ -152,9 +150,17 @@
     out_ref[...] = apply_fast(q_ref[0], *nexts)
 
 
-def join_kernel(place_ref, first_ref, second_ref, out_ref):
-    out_ref[0] = first_ref[0]
-    out_ref[1] = second_ref[0]
+def lay_first_kernel(place_ref, *refs):
+    hop = pl.program_id(0)
+    for i, ref in enumerate(refs[:-1]):
+
+        @pl.when(hop == i)
+        def _(ref=ref):
+            refs[-1][0] = ref[...]
+
+
+def lay_second_kernel(buf_ref, rows_ref, out_ref):
+    out_ref[...] = rows_ref[...]
 
 
 def local(queries, key_rows, value_rows, step_rates, gate_fast, up_fast, down_fast):
@@ -196,19 +202,29 @@
 
     swap = [(0, 1), (1, 0)]
     received = lax.ppermute(send, "core", swap)
-    first = pl.pallas_call(
+    place = lax.axis_index("head").astype(jnp.int32).reshape(1)
+    part_spec = pl.BlockSpec((part, HD), lambda h, p: (0, h))
+    firsts = pl.pallas_call(
         first_kernel,
-        grid=(HEADS_HERE,),
-        in_specs=[pl.BlockSpec((1, rows, HD), lambda h: (0, 0, h)), weight_spec, weight_spec, weight_spec],
-        out_specs=rows_spec,
-        out_shape=rows_shape,
+        grid_spec=pltpu.PrefetchScalarGridSpec(
+            num_scalar_prefetch=1,
+            grid=(HEADS_HERE,),
+            in_specs=[pl.BlockSpec((1, rows, HD), lambda h, p: (0, 0, h)), weight_spec, weight_spec, weight_spec],
+            out_specs=[part_spec] * n_head,
+            scratch_shapes=[pltpu.VMEM((rows, HD), BF16)],
+        ),
+        out_shape=[jax.ShapeDtypeStruct((part, width), BF16)] * n_head,
         compiler_params=params,
         name="first",
-    )(q_hbm, g_hbm, u_hbm, d_hbm)
-    first_all = lax.all_gather(first, "head", axis=0)
+    )(place, q_hbm, g_hbm, u_hbm, d_hbm)
+    firsts = [firsts[0]] + [
+        lax.ppermute(firsts[hop], "head", [(i, (i + hop) % n_head) for i in range(n_head)])
+        for hop in range(1, n_head)
+    ]
 
     chip_sum = (keep.astype(F32) + received.astype(F32)).astype(BF16)
     by_y = lax.all_to_all(chip_sum, "y", split_axis=0, concat_axis=0, tiled=True)
+    by_y, *firsts = lax.optimization_barrier((by_y, *firsts))
     y_sum = jnp.sum(by_y.astype(F32), axis=0).astype(BF16)
     by_z = lax.all_to_all(y_sum, "z", split_axis=0, concat_axis=0, tiled=True)
     piece = jnp.sum(by_z.astype(F32), axis=0).astype(BF16)
@@ -224,59 +240,47 @@
     orth_mine = lax.all_to_all(orth, "y", split_axis=0, concat_axis=0, tiled=True).reshape(GROUP, HD, HD)
     orth_other = lax.ppermute(orth_mine, "core", swap)
 
-    def second_specs(start):
-        def at(s, heads):
-            return heads[start + s]
-
-        query = pl.BlockSpec((1, rows, HD), lambda s, c, heads: (1, 0, at(s, heads)))
-        weight = pl.BlockSpec((1, HD, HD), lambda s, c, heads: (at(s, heads), 0, 0))
-        out = pl.BlockSpec((rows, HD), lambda s, c, heads: (0, at(s, heads)))
-        return [query, weight, weight, weight], out
-
-    heads = (jnp.arange(HEADS_HERE, dtype=jnp.int32) + core * (HEADS_HERE - OWN_HEADS)) % HEADS_HERE
-    group_spec = pl.BlockSpec((GROUP, HD, HD), lambda s, c, heads: (0, 0, 0))
-    specs, out_spec = second_specs(0)
+    group_spec = pl.BlockSpec((GROUP, HD, HD), lambda h, c: (0, 0, 0))
     second = pl.pallas_call(
-        own_second_kernel,
+        second_kernel,
         grid_spec=pltpu.PrefetchScalarGridSpec(
-            num_scalar_prefetch=2, grid=(OWN_HEADS,), in_specs=specs + [group_spec], out_specs=out_spec
+            num_scalar_prefetch=1,
+            grid=(HEADS_HERE,),
+            in_specs=[pl.BlockSpec((1, rows, HD), lambda h, c: (1, 0, h))] + [weight_spec] * 3 + [group_spec] * 2,
+            out_specs=rows_spec,
         ),
         out_shape=rows_shape,
         compiler_params=params,
-        name="second_own",
-    )(core, heads, queries, gate_fast, up_fast, down_fast, orth_mine)
-    specs, out_spec = second_specs(OWN_HEADS)
-    second = pl.pallas_call(
-        rest_second_kernel,
-        grid_spec=pltpu.PrefetchScalarGridSpec(
-            num_scalar_prefetch=2,
-            grid=(HEADS_HERE - OWN_HEADS,),
-            in_specs=[pl.BlockSpec(memory_space=pl.ANY)] + specs + [group_spec, group_spec],
-            out_specs=out_spec,
-        ),
-        out_shape=rows_shape,
-        input_output_aliases={2: 0},
-        compiler_params=params,
-        name="second_rest",
-    )(core, heads, second, queries, gate_fast, up_fast, down_fast, orth_mine, orth_other)
+        name="second",
+    )(core, queries, gate_fast, up_fast, down_fast, orth_mine, orth_other)
 
     swapped = lax.all_to_all(second.reshape(n_head, part, width), "head", split_axis=0, concat_axis=0, tiled=True)
-    place = lax.axis_index("head").astype(jnp.int32).reshape(1)
-    return pl.pallas_call(
-        join_kernel,
+    out_shape = jax.ShapeDtypeStruct((2, part, n_head * width), BF16)
+    out = pl.pallas_call(
+        lay_first_kernel,
         grid_spec=pltpu.PrefetchScalarGridSpec(
             num_scalar_prefetch=1,
             grid=(n_head,),
-            in_specs=[
-                pl.BlockSpec((1, part, width), lambda s, p: (s, p[0], 0)),
-                pl.BlockSpec((1, part, width), lambda s, p: (s, 0, 0)),
-            ],
-            out_specs=pl.BlockSpec((2, part, width), lambda s, p: (0, 0, s)),
+            in_specs=[pl.BlockSpec((part, width), lambda s, p: (0, 0))] * n_head,
+            out_specs=pl.BlockSpec((1, part, width), lambda s, p: (0, 0, lax.rem(p[0] + n_head - s, n_head))),
         ),
-        out_shape=jax.ShapeDtypeStruct((2, part, n_head * width), BF16),
-        compiler_params=params,
-        name="join",
-    )(place, pltpu.with_memory_space_constraint(first_all, pltpu.HBM), swapped)
+        out_shape=out_shape,
+        compiler_params=params,
+        name="lay_first",
+    )(place, *firsts)
+    return pl.pallas_call(
+        lay_second_kernel,
+        grid=(n_head,),
+        in_specs=[
+            pl.BlockSpec(memory_space=pl.ANY),
+            pl.BlockSpec((1, part, width), lambda s: (s, 0, 0)),
+        ],
+        out_specs=pl.BlockSpec((1, part, width), lambda s: (1, 0, s)),
+        out_shape=out_shape,
+        input_output_aliases={0: 0},
+        compiler_params=params,
+        name="lay_second",
+    )(out, swapped)
 
 
 def solution(mesh):

time: 120 us -> 107 us (0.89)
  between operations: 13.5 us -> 0.07 us
  starting transfers between devices: 15.7 us -> 21 us
  Pallas kernels: 24.2 us -> 21 us
  waiting for transfers between devices: 22.2 us -> 20.2 us
    all_to_all x1, waiting for transfers between devices: 9.17 us -> 0.01 us  [local(): lax.all_to_all(chip_sum, 'y', split_axis=0, concat_axis=0, tiled=True)]
    ppermute x0 -> x3, waiting for transfers between devices: none -> 6.7 us  [local(): lax.ppermute(firsts[hop], 'head', [(i, (i + hop) % n_head) for i in range...]
    ppermute x0 -> x3, starting transfers between devices: none -> 3.79 us  [local(): lax.ppermute(firsts[hop], 'head', [(i, (i + hop) % n_head) for i in range...]
    pallas_call x4, Pallas kernels: 16.1 us -> 12.9 us  [the longest x1 5.2 us: local(): pl.pallas_call(second_kernel, grid_spec=pltpu.PrefetchScalarGridSpec(num_...]
    ppermute x1, waiting for transfers between devices: 0.01 us -> 2.29 us  [local(): orth_other = lax.ppermute(orth_mine, 'core', swap)]
    all_to_all x1, waiting for transfers between devices: 10.7 us -> 8.88 us  [local(): lax.all_to_all(second.reshape(n_head, part, width), 'head', split_axis=0,...]
  transfers between devices with their start and end apart: 5 -> 7, of which waited for: 3 -> 6; matrix products, arithmetic and copies ran while one was open for 0% -> 0% of each run, Pallas kernels for 13% -> 6%
where the time goes in v4:
time: 107 us; the launch traced here: 106 us
  blocking collectives  42.4 us (40%)
  Pallas kernels  21 us (20%)
  starting transfers between devices  21 us (20%)
  waiting for transfers between devices  20.2 us (19%)
  other arithmetic  1.61 us (2%)
    all_to_all x1, blocking collectives, local(): by_z = lax.all_to_all(y_sum, 'z', split_axis=0, concat_axis=0, tiled=True)  16.7 us
    all_to_all x1, blocking collectives, local(): lax.all_to_all(orth, 'y', split_axis=0, concat_axis=0, tiled=True)  13.3 us
    all_to_all x1, blocking collectives, local(): whole = lax.all_to_all(spread, 'z', split_axis=0, concat_axis=0, tiled=True)  12.4 us
    all_to_all x1, waiting for transfers between devices, local(): lax.all_to_all(second.reshape(n_head, part, width), 'head', split_axis=0,...  8.88 us
    ppermute x3, waiting for transfers between devices, local(): lax.ppermute(firsts[hop], 'head', [(i, (i + hop) % n_head) for i in range...  6.7 us
    ppermute x1, starting transfers between devices, local(): orth_other = lax.ppermute(orth_mine, 'core', swap)  5.99 us
    pallas_call x1, Pallas kernels, local(): pl.pallas_call(grad_kernel, grid_spec=pltpu.PrefetchScalarGridSpec(num_sc...  5.87 us
    pallas_call x1, Pallas kernels, local(): pl.pallas_call(second_kernel, grid_spec=pltpu.PrefetchScalarGridSpec(num_...  5.2 us
  transfers between devices with their start and end apart: 7, of which 6 were waited for; matrix products, arithmetic and copies ran while one was open for 0% of the time, Pallas kernels for 6%

profile of v4, /device:TPU:1, one launch (start us, length us, event | category | flops | bytes accessed | tf_op | source)
XLA Modules:
  0.0 106.3 jit_solution(5872042762299989410)
XLA Ops:
  0.0 5.9 %grads.1 = (bf16[4,8,2,64,128]{4,3,2,1,0:T(8,128)(2,1)S(1)}, bf16[4,8,2,64,128]{4,3,2,1,0:T(8,128)(2,1)S(1)}) custom-call(s32[1]{0:T(128)} %bitcast.1.core_ref, bf16[256,1280]{1,0:T(8,128)(2,1)} %k_ref.1, bf16[256,1280]{1,0:T(8,128)(2,1)} %v_ref.1, f32[5,256]{1,0:T(8,128)} %rate_ref.1, f32[5,256,256]{2,1,0:T(8,128)} %g_ref.5, f32[5,256,256]{2,1,0:T(8,128)} %u_ref.5, ...), custom_call_target="tpu_custom_call" | custom-call | tf_op jit(solution)/shard_map/grads/pallas_call | solution.py:183
  5.9 3.3 %collective-permute-start = (bf16[4,8,2,64,128]{4,3,2,1,0:T(8,128)(2,1)S(1)}, bf16[4,8,2,64,128]{4,3,2,1,0:T(8,128)(2,1)S(1)}, u32[]{:S(2)}, u32[]{:S(2)}) collective-permute-start(bf16[4,8,2,64,128]{4,3,2,1,0:T(8,128)(2,1)S(1)} %get-tuple-element.17), channel_id=1, source_target_pairs={{0,1},{1,0},{2,3},{3,2},{4,5},{5,4},{6,7},{7,6},{8,9},{9,8},{10,11... | collective-permute-start | bytes 3145736 | tf_op jit(solution)/shard_map/ppermute | solution.py:204
  9.2 2.3 %collective-permute-done = bf16[4,8,2,64,128]{4,3,2,1,0:T(8,128)(2,1)S(1)} collective-permute-done((bf16[4,8,2,64,128]{4,3,2,1,0:T(8,128)(2,1)S(1)}, bf16[4,8,2,64,128]{4,3,2,1,0:T(8,128)(2,1)S(1)}, u32[]{:S(2)}, u32[]{:S(2)}) %collective-permute-start) | collective-permute-done | bytes 1048608 | tf_op jit(solution)/shard_map/ppermute | solution.py:204
  11.5 1.4 %add_convert_fusion = bf16[4,8,2,64,128]{4,3,2,1,0:T(8,128)(2,1)} fusion(bf16[4,8,2,64,128]{4,3,2,1,0:T(8,128)(2,1)S(1)} %collective-permute-done, bf16[4,8,2,64,128]{4,3,2,1,0:T(8,128)(2,1)S(1)} %get-tuple-element.16), kind=kLoop, calls=%fused_computation | loop fusion | flops 2097152 | bytes 3145728 | tf_op jit(solution)/shard_map/convert_element_type | solution.py:225
  12.9 3.5 %all-to-all-start = ((bf16[4,8,2,64,128]{4,3,2,1,0:T(8,128)(2,1)}), bf16[4,8,2,64,128]{4,3,2,1,0:T(8,128)(2,1)S(1)}, u32[]{:S(2)}, u32[]{:S(2)}) async-start(bf16[4,8,2,64,128]{4,3,2,1,0:T(8,128)(2,1)} %add_convert_fusion), calls=%async_computation | async-start | bytes 2097152 | tf_op jit(solution)/shard_map/all_to_all | solution.py:226
  16.4 4.9 %first.1 = (bf16[64,1280]{1,0:T(8,128)(2,1)S(1)}, bf16[64,1280]{1,0:T(8,128)(2,1)S(1)}, bf16[64,1280]{1,0:T(8,128)(2,1)S(1)}, bf16[64,1280]{1,0:T(8,128)(2,1)S(1)}) custom-call(s32[1]{0:T(128)} %bitcast.place_ref, bf16[2,256,1280]{2,1,0:T(8,128)(2,1)} %q_ref.3, f32[5,256,256]{2,1,0:T(8,128)} %g_ref.5, f32[5,256,256]{2,1,0:T(8,128)} %u_ref.5, ...), custom_call_target="tpu_custom_call" | custom-call | tf_op jit(solution)/shard_map/first/pallas_call | solution.py:207
  21.3 0.2 collective-permute-start.1
  21.4 2.4 %collective-permute-start.2 = (bf16[64,1280]{1,0:T(8,128)(2,1)S(1)}, bf16[64,1280]{1,0:T(8,128)(2,1)S(1)}, u32[]{:S(2)}, u32[]{:S(2)}) collective-permute-start(bf16[64,1280]{1,0:T(8,128)(2,1)S(1)} %get-tuple-element.20), channel_id=1, source_target_pairs={{0,128},{64,192},{128,0},{192,64},{1,129},{65,193},{129,1},{193,65... | collective-permute-start | bytes 491528 | tf_op jit(solution)/shard_map/ppermute | solution.py:221
  23.9 1.2 %collective-permute-start.3 = (bf16[64,1280]{1,0:T(8,128)(2,1)S(1)}, bf16[64,1280]{1,0:T(8,128)(2,1)S(1)}, u32[]{:S(2)}, u32[]{:S(2)}) collective-permute-start(bf16[64,1280]{1,0:T(8,128)(2,1)S(1)} %get-tuple-element.21), channel_id=1, source_target_pairs={{0,192},{64,0},{128,64},{192,128},{1,193},{65,1},{129,65},{193,129... | collective-permute-start | bytes 491528 | tf_op jit(solution)/shard_map/ppermute | solution.py:221
  25.0 3.4 %collective-permute-done.1.refs_1_ = bf16[64,1280]{1,0:T(8,128)(2,1)S(1)} collective-permute-done((bf16[64,1280]{1,0:T(8,128)(2,1)S(1)}, bf16[64,1280]{1,0:T(8,128)(2,1)S(1)}, u32[]{:S(2)}, u32[]{:S(2)}) %collective-permute-start.1) | collective-permute-done | bytes 163872 | tf_op jit(solution)/shard_map/ppermute | solution.py:221
  28.4 2.7 %collective-permute-done.2.refs_2_ = bf16[64,1280]{1,0:T(8,128)(2,1)S(1)} collective-permute-done((bf16[64,1280]{1,0:T(8,128)(2,1)S(1)}, bf16[64,1280]{1,0:T(8,128)(2,1)S(1)}, u32[]{:S(2)}, u32[]{:S(2)}) %collective-permute-start.2) | collective-permute-done | bytes 163872 | tf_op jit(solution)/shard_map/ppermute | solution.py:221
  31.1 0.7 collective-permute-done.3.refs_3_
  31.7 0.0 all-to-all-done
  31.8 0.2 reduce_sum.24
  32.0 16.7 %all_to_all.25 = bf16[8,2,64,128]{3,2,1,0:T(8,128)(2,1)S(1)} all-to-all(bf16[8,2,64,128]{3,2,1,0:T(8,128)(2,1)S(1)} %reduce_sum.24), channel_id=1, replica_groups=mesh['head'=4,'z'=8,'y'=4,'core'=2] {'z'}, dimensions={0} | all-to-all | bytes 524288 | tf_op jit(solution)/shard_map/all_to_all | solution.py:229
  48.8 12.4 %all_to_all.26.rows_ref = bf16[8,2,64,128]{3,2,1,0:T(8,128)(2,1)S(1)} all-to-all(bf16[8,2,64,128]{3,2,1,0:T(8,128)(2,1)S(1)} %broadcast_in_dim.2), channel_id=1, replica_groups=mesh['head'=4,'z'=8,'y'=4,'core'=2] {'z'}, dimensions={0} | all-to-all | bytes 524288 | tf_op jit(solution)/shard_map/all_to_all | solution.py:232
  61.1 0.0 copy-start.1
  61.1 2.2 %orthogonalize.1 = bf16[4,2,256,256]{3,2,1,0:T(8,128)(2,1)S(1)} custom-call(bf16[8,2,64,128]{3,2,1,0:T(8,128)(2,1)S(1)} %all_to_all.26.rows_ref), custom_call_target="tpu_custom_call" | custom-call | tf_op jit(solution)/shard_map/orthogonalize/pallas_call | solution.py:234
  63.4 0.0 copy-start
  63.4 13.3 %all_to_all.27 = bf16[4,2,256,256]{3,2,1,0:T(8,128)(2,1)S(1)} all-to-all(bf16[4,2,256,256]{3,2,1,0:T(8,128)(2,1)S(1)} %orthogonalize.1), channel_id=1, replica_groups=mesh['head'=4,'z'=8,'y'=4,'core'=2] {'y'}, dimensions={0} | all-to-all | bytes 2097152 | tf_op jit(solution)/shard_map/all_to_all | solution.py:240
  76.7 6.0 %collective-permute-start.4 = (bf16[8,256,256]{2,1,0:T(8,128)(2,1)S(1)}, bf16[8,256,256]{2,1,0:T(8,128)(2,1)S(1)}, u32[]{:S(2)}, u32[]{:S(2)}) collective-permute-start(bf16[8,256,256]{2,1,0:T(8,128)(2,1)S(1)} %bitcast.4), channel_id=1, source_target_pairs={{0,1},{1,0},{2,3},{3,2},{4,5},{5,4},{6,7},{7,6},{8,9},{9,8},{10,11... | collective-permute-start | bytes 3145736 | tf_op jit(solution)/shard_map/ppermute | solution.py:241
  82.7 2.3 %collective-permute-done.4.other_ref = bf16[8,256,256]{2,1,0:T(8,128)(2,1)S(1)} collective-permute-done((bf16[8,256,256]{2,1,0:T(8,128)(2,1)S(1)}, bf16[8,256,256]{2,1,0:T(8,128)(2,1)S(1)}, u32[]{:S(2)}, u32[]{:S(2)}) %collective-permute-start.4) | collective-permute-done | bytes 1048608 | tf_op jit(solution)/shard_map/ppermute | solution.py:241
  85.0 0.0 copy-done.1
  85.0 0.0 copy-done
  85.0 5.2 %second.1 = bf16[256,1280]{1,0:T(8,128)(2,1)} custom-call(s32[1]{0:T(128)} %bitcast.1.core_ref, bf16[2,256,1280]{2,1,0:T(8,128)(2,1)S(1)} %copy-done.1, f32[5,256,256]{2,1,0:T(8,128)S(1)} %copy-done, f32[5,256,256]{2,1,0:T(8,128)} %u_ref.5, f32[5,256,256]{2,1,0:T(8,128)} %d_ref.5, bf16[8,256,256]{2,1,0:T(8,128)(2,1)S(1)} %bitcast.5, ...), custom_call_target="tpu_custom_call" | custom-call | tf_op jit(solution)/shard_map/second/pallas_call | solution.py:244
  90.2 4.4 %all-to-all-start.4 = ((bf16[4,64,1280]{2,1,0:T(8,128)(2,1)}), bf16[4,64,1280]{2,1,0:T(8,128)(2,1)S(1)}, u32[]{:S(2)}, u32[]{:S(2)}) async-start(bf16[4,64,1280]{2,1,0:T(8,128)(2,1)} %bitcast.3), calls=%async_computation.4 | async-start | bytes 1310720 | tf_op jit(solution)/shard_map/all_to_all | solution.py:257
  94.6 1.4 %lay_first.1.buf_ref = bf16[2,64,5120]{2,1,0:T(8,128)(2,1)} custom-call(s32[1]{0:T(128)} %bitcast.place_ref, bf16[64,1280]{1,0:T(8,128)(2,1)S(1)} %get-tuple-element.22.refs_0_, bf16[64,1280]{1,0:T(8,128)(2,1)S(1)} %collective-permute-done.1.refs_1_, bf16[64,1280]{1,0:T(8,128)(2,1)S(1)} %collective-permute-done.2.refs_2_, ...), custom_call_target="tpu_custom_call" | custom-call | tf_op jit(solution)/shard_map/lay_first/pallas_call | solution.py:259
  96.0 8.9 %all-to-all-done.4.rows_ref = bf16[4,64,1280]{2,1,0:T(8,128)(2,1)S(1)} async-done(((bf16[4,64,1280]{2,1,0:T(8,128)(2,1)}), bf16[4,64,1280]{2,1,0:T(8,128)(2,1)S(1)}, u32[]{:S(2)}, u32[]{:S(2)}) %all-to-all-start.4) | async-done | bytes 655392 | tf_op jit(solution)/shard_map/all_to_all | solution.py:257
  104.9 1.4 %lay_second.1 = bf16[2,64,5120]{2,1,0:T(8,128)(2,1)} custom-call(bf16[2,64,5120]{2,1,0:T(8,128)(2,1)} %lay_first.1.buf_ref, bf16[4,64,1280]{2,1,0:T(8,128)(2,1)S(1)} %all-to-all-done.4.rows_ref), custom_call_target="tpu_custom_call", output_to_operand_aliasing={{}: (0, {})} | custom-call | tf_op jit(solution)/shard_map/lay_second/pallas_call | solution.py:271
  (2 shorter events, 0.1 us)
Async XLA Ops:
  5.9 5.6 %collective-permute-start = (bf16[4,8,2,64,128]{4,3,2,1,0:T(8,128)(2,1)S(1)}, bf16[4,8,2,64,128]{4,3,2,1,0:T(8,128)(2,1)S(1)}, u32[]{:S(2)}, u32[]{:S(2)}) collective-permute-start(bf16[4,8,2,64,128]{4,3,2,1,0:T(8,128)(2,1)S(1)} %get-tuple-element.17), channel_id=1, source_target_pairs={{0,1},{1,0},{2,3},{3,2},{4,5},{5,4},{6,7},{7,6},{8,9},{9,8},{10,11... | collective-permute-start | bytes 3145736 | tf_op jit(solution)/shard_map/ppermute | solution.py:204
  12.9 18.9 %all-to-all-start = ((bf16[4,8,2,64,128]{4,3,2,1,0:T(8,128)(2,1)}), bf16[4,8,2,64,128]{4,3,2,1,0:T(8,128)(2,1)S(1)}, u32[]{:S(2)}, u32[]{:S(2)}) async-start(bf16[4,8,2,64,128]{4,3,2,1,0:T(8,128)(2,1)} %add_convert_fusion), calls=%async_computation | async-start | bytes 2097152 | tf_op jit(solution)/shard_map/all_to_all | solution.py:226
  21.3 7.1 %collective-permute-start.1 = (bf16[64,1280]{1,0:T(8,128)(2,1)S(1)}, bf16[64,1280]{1,0:T(8,128)(2,1)S(1)}, u32[]{:S(2)}, u32[]{:S(2)}) collective-permute-start(bf16[64,1280]{1,0:T(8,128)(2,1)S(1)} %get-tuple-element.19), channel_id=1, source_target_pairs={{0,64},{64,128},{128,192},{192,0},{1,65},{65,129},{129,193},{193,1... | collective-permute-start | bytes 491528 | tf_op jit(solution)/shard_map/ppermute | solution.py:221
  21.4 9.6 %collective-permute-start.2 = (bf16[64,1280]{1,0:T(8,128)(2,1)S(1)}, bf16[64,1280]{1,0:T(8,128)(2,1)S(1)}, u32[]{:S(2)}, u32[]{:S(2)}) collective-permute-start(bf16[64,1280]{1,0:T(8,128)(2,1)S(1)} %get-tuple-element.20), channel_id=1, source_target_pairs={{0,128},{64,192},{128,0},{192,64},{1,129},{65,193},{129,1},{193,65... | collective-permute-start | bytes 491528 | tf_op jit(solution)/shard_map/ppermute | solution.py:221
  23.9 7.9 %collective-permute-start.3 = (bf16[64,1280]{1,0:T(8,128)(2,1)S(1)}, bf16[64,1280]{1,0:T(8,128)(2,1)S(1)}, u32[]{:S(2)}, u32[]{:S(2)}) collective-permute-start(bf16[64,1280]{1,0:T(8,128)(2,1)S(1)} %get-tuple-element.21), channel_id=1, source_target_pairs={{0,192},{64,0},{128,64},{192,128},{1,193},{65,1},{129,65},{193,129... | collective-permute-start | bytes 491528 | tf_op jit(solution)/shard_map/ppermute | solution.py:221
  61.1 23.9 %copy-start.1 = (bf16[2,256,1280]{2,1,0:T(8,128)(2,1)S(1)}, bf16[2,256,1280]{2,1,0:T(8,128)(2,1)}, u32[]{:S(2)}) copy-start(bf16[2,256,1280]{2,1,0:T(8,128)(2,1)} %q_ref.3) | copy-start | bytes 3932164
  63.4 21.6 %copy-start = (f32[5,256,256]{2,1,0:T(8,128)S(1)}, f32[5,256,256]{2,1,0:T(8,128)}, u32[]{:S(2)}) copy-start(f32[5,256,256]{2,1,0:T(8,128)} %g_ref.5) | copy-start | bytes 3932164
  76.7 8.3 %collective-permute-start.4 = (bf16[8,256,256]{2,1,0:T(8,128)(2,1)S(1)}, bf16[8,256,256]{2,1,0:T(8,128)(2,1)S(1)}, u32[]{:S(2)}, u32[]{:S(2)}) collective-permute-start(bf16[8,256,256]{2,1,0:T(8,128)(2,1)S(1)} %bitcast.4), channel_id=1, source_target_pairs={{0,1},{1,0},{2,3},{3,2},{4,5},{5,4},{6,7},{7,6},{8,9},{9,8},{10,11... | collective-permute-start | bytes 3145736 | tf_op jit(solution)/shard_map/ppermute | solution.py:241
  90.2 14.7 %all-to-all-start.4 = ((bf16[4,64,1280]{2,1,0:T(8,128)(2,1)}), bf16[4,64,1280]{2,1,0:T(8,128)(2,1)S(1)}, u32[]{:S(2)}, u32[]{:S(2)}) async-start(bf16[4,64,1280]{2,1,0:T(8,128)(2,1)} %bitcast.3), calls=%async_computation.4 | async-start | bytes 1310720 | tf_op jit(solution)/shard_map/all_to_all | solution.py:257

commit v5 on v4

--- a/solution.py
+++ b/solution.py
@@ -16,10 +16,6 @@
 HEADS_HERE = 5
 MATS = 3 * HEADS_HERE
 GROUP = 8
-Y = 4
-Z = 8
-PER_Y = GROUP // Y
-ROWS = 64
 VMEM_LIMIT = 48 * 1024 * 1024
 
 
@@ -88,11 +84,7 @@
 
                 @pl.when(inside & wanted)
                 def _(ref=ref, slot=slot, grad=grad):
-                    for z in range(Z):
-                        side, block = z // 4, z % 4
-                        ref[slot // 2, z, slot % 2] = grad[
-                            block * ROWS : (block + 1) * ROWS, side * HALF : (side + 1) * HALF
-                        ]
+                    ref[slot] = grad
 
 
 def split(x):
@@ -100,37 +92,29 @@
     return high, (x - high.astype(F32)).astype(BF16)
 
 
-def orth_kernel(rows_ref, out_ref):
-    xs = []
-    for i in range(PER_Y):
-        sides = [
-            jnp.concatenate([rows_ref[side * 4 + block, i].astype(F32) for block in range(4)], axis=0)
-            for side in range(2)
-        ]
-        m = jnp.concatenate(sides, axis=1)
-        norm = jnp.sqrt(jnp.sum(m * m, keepdims=True)) + 1e-07
-        xs.append(m / norm)
+def orth_kernel(*refs):
+    out_ref = refs[-1]
+    m = refs[0][...].astype(F32)
+    for ref in refs[1:-1]:
+        m = m + ref[...].astype(F32)
+    x = m / (jnp.sqrt(jnp.sum(m * m, keepdims=True)) + 1e-07)
     for sweep in range(NS_STEPS):
         if sweep < NS_STEPS - 1:
-            lows = [x.astype(BF16) for x in xs]
-            grams = [dot_nt(x, x) for x in lows]
-            halves = [a.astype(BF16) for a in grams]
-            squares = [dot_f32(a, a) for a in halves]
-            polys = [(coef_second * a + coef_third * s).astype(BF16) for a, s in zip(grams, squares)]
-            xs = [coef_first * x + dot_f32(p, l) for x, p, l in zip(xs, polys, lows)]
+            low = x.astype(BF16)
+            gram = dot_nt(low, low)
+            half = gram.astype(BF16)
+            poly = (coef_second * gram + coef_third * dot_f32(half, half)).astype(BF16)
+            x = coef_first * x + dot_f32(poly, low)
         else:
-            parts = [split(x) for x in xs]
-            grams = [dot_nt(h, h) + (dot_nt(h, l) + dot_nt(l, h)) for h, l in parts]
-            gparts = [split(a) for a in grams]
-            squares = [dot_f32(h, h) + (dot_f32(h, l) + dot_f32(l, h)) for h, l in gparts]
-            polys = [split(coef_second * a + coef_third * s) for a, s in zip(grams, squares)]
-            xs = [
-                coef_first * x + (dot_f32(ph, h) + (dot_f32(ph, l) + dot_f32(pw, h)))
-                for x, (ph, pw), (h, l) in zip(xs, polys, parts)
-            ]
-    for i in range(PER_Y):
-        for y in range(Y):
-            out_ref[y, i] = xs[i].astype(BF16)
+            h, l = split(x)
+            gram = dot_nt(h, h) + (dot_nt(h, l) + dot_nt(l, h))
+            gh, gl = split(gram)
+            square = dot_f32(gh, gh) + (dot_f32(gh, gl) + dot_f32(gl, gh))
+            ph, pw = split(coef_second * gram + coef_third * square)
+            x = coef_first * x + (dot_f32(ph, h) + (dot_f32(ph, l) + dot_f32(pw, h)))
+    orth = x.astype(BF16)
+    for i in range(out_ref.shape[0]):
+        out_ref[i] = orth
 
 
 def next_weight(fast, orth):
@@ -174,8 +158,8 @@
     rows_spec = pl.BlockSpec((rows, HD), lambda h, *_: (0, h))
     rows_shape = jax.ShapeDtypeStruct((rows, width), BF16)
 
-    piece_shape = (Y, Z, PER_Y, ROWS, HALF)
-    piece_spec = pl.BlockSpec(piece_shape, lambda h, c: (0, 0, 0, 0, 0))
+    piece_shape = (GROUP, HD, HD)
+    piece_spec = pl.BlockSpec(piece_shape, lambda h, c: (0, 0, 0))
     args = (queries, key_rows, value_rows, step_rates, gate_fast, up_fast, down_fast)
     q_hbm, k_hbm, v_hbm, rate_hbm, g_hbm, u_hbm, d_hbm = [
         pltpu.with_memory_space_constraint(x, pltpu.HBM) for x in args
@@ -223,21 +207,21 @@
     ]
 
     chip_sum = (keep.astype(F32) + received.astype(F32)).astype(BF16)
-    by_y = lax.all_to_all(chip_sum, "y", split_axis=0, concat_axis=0, tiled=True)
-    by_y, *firsts = lax.optimization_barrier((by_y, *firsts))
-    y_sum = jnp.sum(by_y.astype(F32), axis=0).astype(BF16)
-    by_z = lax.all_to_all(y_sum, "z", split_axis=0, concat_axis=0, tiled=True)
-    piece = jnp.sum(by_z.astype(F32), axis=0).astype(BF16)
-    spread = jnp.broadcast_to(piece[None], (Z,) + piece.shape)
-    whole = lax.all_to_all(spread, "z", split_axis=0, concat_axis=0, tiled=True)
-
+    slots = ("y", "z_lo")
+    by_slot = lax.all_to_all(chip_sum, slots, split_axis=0, concat_axis=0, tiled=True)
+    by_slot, *firsts = lax.optimization_barrier((by_slot, *firsts))
+    partial = jnp.sum(by_slot.astype(F32), axis=0).astype(BF16)
+    n_far = lax.axis_size("z_hi")
+    partials = [partial] + [
+        lax.ppermute(partial, "z_hi", [(i, (i + hop) % n_far) for i in range(n_far)]) for hop in range(1, n_far)
+    ]
     orth = pl.pallas_call(
         orth_kernel,
-        out_shape=jax.ShapeDtypeStruct((Y, PER_Y, HD, HD), BF16),
+        out_shape=jax.ShapeDtypeStruct(piece_shape, BF16),
         compiler_params=pltpu.CompilerParams(vmem_limit_bytes=VMEM_LIMIT),
         name="orthogonalize",
-    )(whole)
-    orth_mine = lax.all_to_all(orth, "y", split_axis=0, concat_axis=0, tiled=True).reshape(GROUP, HD, HD)
+    )(*partials)
+    orth_mine = lax.all_to_all(orth, slots, split_axis=0, concat_axis=0, tiled=True)
     orth_other = lax.ppermute(orth_mine, "core", swap)
 
     group_spec = pl.BlockSpec((GROUP, HD, HD), lambda h, c: (0, 0, 0))
@@ -285,8 +269,8 @@
 
 def solution(mesh):
     heads = mesh.shape["head"]
-    fine = Mesh(mesh.devices.reshape(heads, 8, 4, 2), ("head", "z", "y", "core"))
-    tok = ("z", "y", "core")
+    fine = Mesh(mesh.devices.reshape(heads, 4, 2, 4, 2), ("head", "z_hi", "z_lo", "y", "core"))
+    tok = ("z_hi", "z_lo", "y", "core")
     placed = (
         P(None, tok, "head"),
         P(tok, "head"),

time: 107 us -> 97.9 us (0.915)
  blocking collectives: 42.4 us -> 23 us
  starting transfers between devices: 21 us -> 28.7 us
  waiting for transfers between devices: 20.2 us -> 23.4 us
    all_to_all x3 -> x1, blocking collectives: 42.4 us -> 23 us  [local(): lax.all_to_all(orth, slots, split_axis=0, concat_axis=0, tiled=True)]
    ppermute x0 -> x3, starting transfers between devices: none -> 9.66 us  [local(): lax.ppermute(partial, 'z_hi', [(i, (i + hop) % n_far) for i in range(n_fa...]
    ppermute x0 -> x3, waiting for transfers between devices: none -> 3.98 us  [local(): lax.ppermute(partial, 'z_hi', [(i, (i + hop) % n_far) for i in range(n_fa...]
    ppermute x1, starting transfers between devices: 5.99 us -> 3.31 us  [local(): orth_other = lax.ppermute(orth_mine, 'core', swap)]
    ppermute x3, starting transfers between devices: 3.79 us -> 4.89 us  [local(): lax.ppermute(firsts[hop], 'head', [(i, (i + hop) % n_head) for i in range...]
  transfers between devices with their start and end apart: 7 -> 10, of which waited for: 6 -> 6; matrix products, arithmetic and copies ran while one was open for 0% -> 0% of each run, Pallas kernels for 6% -> 6%
where the time goes in v5:
time: 97.9 us; the launch traced here: 97.4 us
  starting transfers between devices  28.7 us (29%)
  waiting for transfers between devices  23.4 us (24%)
  blocking collectives  23 us (23%)
  Pallas kernels  20.9 us (21%)
  other arithmetic  1.42 us (1%)
    all_to_all x1, blocking collectives, local(): lax.all_to_all(orth, slots, split_axis=0, concat_axis=0, tiled=True)  23 us
    ppermute x3, starting transfers between devices, local(): lax.ppermute(partial, 'z_hi', [(i, (i + hop) % n_far) for i in range(n_fa...  9.66 us
    all_to_all x1, waiting for transfers between devices, local(): lax.all_to_all(second.reshape(n_head, part, width), 'head', split_axis=0,...  8.87 us
    ppermute x3, waiting for transfers between devices, local(): lax.ppermute(firsts[hop], 'head', [(i, (i + hop) % n_head) for i in range...  6 us
    pallas_call x1, Pallas kernels, local(): pl.pallas_call(grad_kernel, grid_spec=pltpu.PrefetchScalarGridSpec(num_sc...  5.83 us
    pallas_call x1, Pallas kernels, local(): pl.pallas_call(second_kernel, grid_spec=pltpu.PrefetchScalarGridSpec(num_...  5.17 us
    ppermute x3, starting transfers between devices, local(): lax.ppermute(firsts[hop], 'head', [(i, (i + hop) % n_head) for i in range...  4.89 us
    pallas_call x1, Pallas kernels, local(): pl.pallas_call(first_kernel, grid_spec=pltpu.PrefetchScalarGridSpec(num_s...  4.84 us
  transfers between devices with their start and end apart: 10, of which 6 were waited for; matrix products, arithmetic and copies ran while one was open for 0% of the time, Pallas kernels for 6%

profile of v5, /device:TPU:1, one launch (start us, length us, event | category | flops | bytes accessed | tf_op | source)
XLA Modules:
  0.0 97.4 jit_solution(2983402211744012223)
XLA Ops:
  0.0 5.8 %grads.1 = (bf16[8,256,256]{2,1,0:T(8,128)(2,1)S(1)}, bf16[8,256,256]{2,1,0:T(8,128)(2,1)S(1)}) custom-call(s32[1]{0:T(128)} %bitcast.1.core_ref, bf16[256,1280]{1,0:T(8,128)(2,1)} %k_ref.1, bf16[256,1280]{1,0:T(8,128)(2,1)} %v_ref.1, f32[5,256]{1,0:T(8,128)} %rate_ref.1, f32[5,256,256]{2,1,0:T(8,128)} %g_ref.5, f32[5,256,256]{2,1,0:T(8,128)} %u_ref.5, ...), custom_call_target="tpu_custom_call" | custom-call | tf_op jit(solution)/shard_map/grads/pallas_call | solution.py:167
  5.8 3.3 %collective-permute-start = (bf16[8,256,256]{2,1,0:T(8,128)(2,1)S(1)}, bf16[8,256,256]{2,1,0:T(8,128)(2,1)S(1)}, u32[]{:S(2)}, u32[]{:S(2)}) collective-permute-start(bf16[8,256,256]{2,1,0:T(8,128)(2,1)S(1)} %get-tuple-element.17), channel_id=1, source_target_pairs={{0,1},{1,0},{2,3},{3,2},{4,5},{5,4},{6,7},{7,6},{8,9},{9,8},{10,11... | collective-permute-start | bytes 3145736 | tf_op jit(solution)/shard_map/ppermute | solution.py:188
  9.2 2.3 %collective-permute-done = bf16[8,256,256]{2,1,0:T(8,128)(2,1)S(1)} collective-permute-done((bf16[8,256,256]{2,1,0:T(8,128)(2,1)S(1)}, bf16[8,256,256]{2,1,0:T(8,128)(2,1)S(1)}, u32[]{:S(2)}, u32[]{:S(2)}) %collective-permute-start) | collective-permute-done | bytes 1048608 | tf_op jit(solution)/shard_map/ppermute | solution.py:188
  11.5 1.3 %add_convert_fusion = bf16[8,256,256]{2,1,0:T(8,128)(2,1)} fusion(bf16[8,256,256]{2,1,0:T(8,128)(2,1)S(1)} %collective-permute-done, bf16[8,256,256]{2,1,0:T(8,128)(2,1)S(1)} %get-tuple-element.16), kind=kLoop, calls=%fused_computation | loop fusion | flops 2097152 | bytes 3145728 | tf_op jit(solution)/shard_map/convert_element_type | solution.py:209
  12.7 3.8 %all-to-all-start = ((bf16[8,256,256]{2,1,0:T(8,128)(2,1)}), bf16[8,256,256]{2,1,0:T(8,128)(2,1)S(1)}, u32[]{:S(2)}, u32[]{:S(2)}) async-start(bf16[8,256,256]{2,1,0:T(8,128)(2,1)} %add_convert_fusion), calls=%async_computation | async-start | bytes 2097152 | tf_op jit(solution)/shard_map/all_to_all | solution.py:211
  16.5 4.8 %first.1 = (bf16[64,1280]{1,0:T(8,128)(2,1)S(1)}, bf16[64,1280]{1,0:T(8,128)(2,1)S(1)}, bf16[64,1280]{1,0:T(8,128)(2,1)S(1)}, bf16[64,1280]{1,0:T(8,128)(2,1)S(1)}) custom-call(s32[1]{0:T(128)} %bitcast.place_ref, bf16[2,256,1280]{2,1,0:T(8,128)(2,1)} %q_ref.3, f32[5,256,256]{2,1,0:T(8,128)} %g_ref.5, f32[5,256,256]{2,1,0:T(8,128)} %u_ref.5, ...), custom_call_target="tpu_custom_call" | custom-call | tf_op jit(solution)/shard_map/first/pallas_call | solution.py:191
  21.4 1.3 %collective-permute-start.1 = (bf16[64,1280]{1,0:T(8,128)(2,1)S(1)}, bf16[64,1280]{1,0:T(8,128)(2,1)S(1)}, u32[]{:S(2)}, u32[]{:S(2)}) collective-permute-start(bf16[64,1280]{1,0:T(8,128)(2,1)S(1)} %get-tuple-element.19), channel_id=1, source_target_pairs={{0,64},{64,128},{128,192},{192,0},{1,65},{65,129},{129,193},{193,1... | collective-permute-start | bytes 491528 | tf_op jit(solution)/shard_map/ppermute | solution.py:205
  22.7 2.5 %collective-permute-start.2 = (bf16[64,1280]{1,0:T(8,128)(2,1)S(1)}, bf16[64,1280]{1,0:T(8,128)(2,1)S(1)}, u32[]{:S(2)}, u32[]{:S(2)}) collective-permute-start(bf16[64,1280]{1,0:T(8,128)(2,1)S(1)} %get-tuple-element.20), channel_id=1, source_target_pairs={{0,128},{64,192},{128,0},{192,64},{1,129},{65,193},{129,1},{193,65... | collective-permute-start | bytes 491528 | tf_op jit(solution)/shard_map/ppermute | solution.py:205
  25.1 1.1 %collective-permute-start.3 = (bf16[64,1280]{1,0:T(8,128)(2,1)S(1)}, bf16[64,1280]{1,0:T(8,128)(2,1)S(1)}, u32[]{:S(2)}, u32[]{:S(2)}) collective-permute-start(bf16[64,1280]{1,0:T(8,128)(2,1)S(1)} %get-tuple-element.21), channel_id=1, source_target_pairs={{0,192},{64,0},{128,64},{192,128},{1,193},{65,1},{129,65},{193,129... | collective-permute-start | bytes 491528 | tf_op jit(solution)/shard_map/ppermute | solution.py:205
  26.3 1.5 %collective-permute-done.1.refs_1_ = bf16[64,1280]{1,0:T(8,128)(2,1)S(1)} collective-permute-done((bf16[64,1280]{1,0:T(8,128)(2,1)S(1)}, bf16[64,1280]{1,0:T(8,128)(2,1)S(1)}, u32[]{:S(2)}, u32[]{:S(2)}) %collective-permute-start.1) | collective-permute-done | bytes 163872 | tf_op jit(solution)/shard_map/ppermute | solution.py:205
  27.8 4.5 %collective-permute-done.2.refs_2_ = bf16[64,1280]{1,0:T(8,128)(2,1)S(1)} collective-permute-done((bf16[64,1280]{1,0:T(8,128)(2,1)S(1)}, bf16[64,1280]{1,0:T(8,128)(2,1)S(1)}, u32[]{:S(2)}, u32[]{:S(2)}) %collective-permute-start.2) | collective-permute-done | bytes 163872 | tf_op jit(solution)/shard_map/ppermute | solution.py:205
  32.3 0.0 collective-permute-done.3.refs_3_
  32.3 0.0 all-to-all-done
  32.3 0.1 reduce_sum.12.refs_0_
  32.4 3.0 %collective-permute-start.4 = (bf16[256,256]{1,0:T(8,128)(2,1)S(1)}, bf16[256,256]{1,0:T(8,128)(2,1)S(1)}, u32[]{:S(2)}, u32[]{:S(2)}) collective-permute-start(bf16[256,256]{1,0:T(8,128)(2,1)S(1)} %reduce_sum.12.refs_0_), channel_id=1, source_target_pairs={{0,16},{16,32},{32,48},{48,0},{1,17},{17,33},{33,49},{49,1},{2,18}... | collective-permute-start | bytes 393224 | tf_op jit(solution)/shard_map/ppermute | solution.py:216
  35.5 4.2 %collective-permute-start.5 = (bf16[256,256]{1,0:T(8,128)(2,1)S(1)}, bf16[256,256]{1,0:T(8,128)(2,1)S(1)}, u32[]{:S(2)}, u32[]{:S(2)}) collective-permute-start(bf16[256,256]{1,0:T(8,128)(2,1)S(1)} %reduce_sum.12.refs_0_), channel_id=1, source_target_pairs={{0,32},{16,48},{32,0},{48,16},{1,33},{17,49},{33,1},{49,17},{2,34}... | collective-permute-start | bytes 393224 | tf_op jit(solution)/shard_map/ppermute | solution.py:216
  39.7 2.4 %collective-permute-start.6 = (bf16[256,256]{1,0:T(8,128)(2,1)S(1)}, bf16[256,256]{1,0:T(8,128)(2,1)S(1)}, u32[]{:S(2)}, u32[]{:S(2)}) collective-permute-start(bf16[256,256]{1,0:T(8,128)(2,1)S(1)} %reduce_sum.12.refs_0_), channel_id=1, source_target_pairs={{0,48},{16,0},{32,16},{48,32},{1,49},{17,1},{33,17},{49,33},{2,50}... | collective-permute-start | bytes 393224 | tf_op jit(solution)/shard_map/ppermute | solution.py:216
  42.1 0.0 collective-permute-done.4.refs_1_
  42.1 4.0 %collective-permute-done.5.refs_2_ = bf16[256,256]{1,0:T(8,128)(2,1)S(1)} collective-permute-done((bf16[256,256]{1,0:T(8,128)(2,1)S(1)}, bf16[256,256]{1,0:T(8,128)(2,1)S(1)}, u32[]{:S(2)}, u32[]{:S(2)}) %collective-permute-start.5) | collective-permute-done | bytes 131104 | tf_op jit(solution)/shard_map/ppermute | solution.py:216
  46.1 0.0 collective-permute-done.6.refs_3_
  46.1 2.2 %orthogonalize.1 = bf16[8,256,256]{2,1,0:T(8,128)(2,1)S(1)} custom-call(bf16[256,256]{1,0:T(8,128)(2,1)S(1)} %reduce_sum.12.refs_0_, bf16[256,256]{1,0:T(8,128)(2,1)S(1)} %collective-permute-done.4.refs_1_, bf16[256,256]{1,0:T(8,128)(2,1)S(1)} %collective-permute-done.5.refs_2_, bf16[256,256]{1,0:T(8,128)(2,1)S(1)} %collective-permute-done.6.refs_3_), custom_call_target="tpu_custom_call" | custom-call | tf_op jit(solution)/shard_map/orthogonalize/pallas_call | solution.py:218
  48.3 0.0 copy-start
  48.3 23.0 %all_to_all.15.mine_ref = bf16[8,256,256]{2,1,0:T(8,128)(2,1)S(1)} all-to-all(bf16[8,256,256]{2,1,0:T(8,128)(2,1)S(1)} %orthogonalize.1), channel_id=1, replica_groups=mesh['head'=4,'z_hi'=4,'z_lo'=2,'y'=4,'core'=2] {'y','z_lo'}, dimensions={0} | all-to-all | bytes 2097152 | tf_op jit(solution)/shard_map/all_to_all | solution.py:224
  71.2 3.3 %collective-permute-start.7 = (bf16[8,256,256]{2,1,0:T(8,128)(2,1)S(1)}, bf16[8,256,256]{2,1,0:T(8,128)(2,1)S(1)}, u32[]{:S(2)}, u32[]{:S(2)}) collective-permute-start(bf16[8,256,256]{2,1,0:T(8,128)(2,1)S(1)} %all_to_all.15.mine_ref), channel_id=1, source_target_pairs={{0,1},{1,0},{2,3},{3,2},{4,5},{5,4},{6,7},{7,6},{8,9},{9,8},{10,11... | collective-permute-start | bytes 3145736 | tf_op jit(solution)/shard_map/ppermute | solution.py:225
  74.6 2.3 %collective-permute-done.7.other_ref = bf16[8,256,256]{2,1,0:T(8,128)(2,1)S(1)} collective-permute-done((bf16[8,256,256]{2,1,0:T(8,128)(2,1)S(1)}, bf16[8,256,256]{2,1,0:T(8,128)(2,1)S(1)}, u32[]{:S(2)}, u32[]{:S(2)}) %collective-permute-start.7) | collective-permute-done | bytes 1048608 | tf_op jit(solution)/shard_map/ppermute | solution.py:225
  76.8 0.0 copy-done.1
  76.8 0.0 copy-done
  76.9 5.2 %second.1 = bf16[256,1280]{1,0:T(8,128)(2,1)} custom-call(s32[1]{0:T(128)} %bitcast.1.core_ref, bf16[2,256,1280]{2,1,0:T(8,128)(2,1)S(1)} %copy-done.1, f32[5,256,256]{2,1,0:T(8,128)S(1)} %copy-done, f32[5,256,256]{2,1,0:T(8,128)} %u_ref.5, f32[5,256,256]{2,1,0:T(8,128)} %d_ref.5, bf16[8,256,256]{2,1,0:T(8,128)(2,1)S(1)} %all_to_all.15.mine_ref, ...), custom_call_target="tpu_custom_call" | custom-call | tf_op jit(solution)/shard_map/second/pallas_call | solution.py:228
  82.0 3.7 %all-to-all-start.2 = ((bf16[4,64,1280]{2,1,0:T(8,128)(2,1)}), bf16[4,64,1280]{2,1,0:T(8,128)(2,1)S(1)}, u32[]{:S(2)}, u32[]{:S(2)}) async-start(bf16[4,64,1280]{2,1,0:T(8,128)(2,1)} %bitcast.2), calls=%async_computation.2 | async-start | bytes 1310720 | tf_op jit(solution)/shard_map/all_to_all | solution.py:241
  85.7 1.4 %lay_first.1.buf_ref = bf16[2,64,5120]{2,1,0:T(8,128)(2,1)} custom-call(s32[1]{0:T(128)} %bitcast.place_ref, bf16[64,1280]{1,0:T(8,128)(2,1)S(1)} %get-tuple-element.22.refs_0_, bf16[64,1280]{1,0:T(8,128)(2,1)S(1)} %collective-permute-done.1.refs_1_, bf16[64,1280]{1,0:T(8,128)(2,1)S(1)} %collective-permute-done.2.refs_2_, ...), custom_call_target="tpu_custom_call" | custom-call | tf_op jit(solution)/shard_map/lay_first/pallas_call | solution.py:243
  87.2 8.9 %all-to-all-done.2.rows_ref = bf16[4,64,1280]{2,1,0:T(8,128)(2,1)S(1)} async-done(((bf16[4,64,1280]{2,1,0:T(8,128)(2,1)}), bf16[4,64,1280]{2,1,0:T(8,128)(2,1)S(1)}, u32[]{:S(2)}, u32[]{:S(2)}) %all-to-all-start.2) | async-done | bytes 655392 | tf_op jit(solution)/shard_map/all_to_all | solution.py:241
  96.0 1.4 %lay_second.1 = bf16[2,64,5120]{2,1,0:T(8,128)(2,1)} custom-call(bf16[2,64,5120]{2,1,0:T(8,128)(2,1)} %lay_first.1.buf_ref, bf16[4,64,1280]{2,1,0:T(8,128)(2,1)S(1)} %all-to-all-done.2.rows_ref), custom_call_target="tpu_custom_call", output_to_operand_aliasing={{}: (0, {})} | custom-call | tf_op jit(solution)/shard_map/lay_second/pallas_call | solution.py:255
  (1 shorter events, 0.0 us)
Async XLA Ops:
  5.8 5.6 %collective-permute-start = (bf16[8,256,256]{2,1,0:T(8,128)(2,1)S(1)}, bf16[8,256,256]{2,1,0:T(8,128)(2,1)S(1)}, u32[]{:S(2)}, u32[]{:S(2)}) collective-permute-start(bf16[8,256,256]{2,1,0:T(8,128)(2,1)S(1)} %get-tuple-element.17), channel_id=1, source_target_pairs={{0,1},{1,0},{2,3},{3,2},{4,5},{5,4},{6,7},{7,6},{8,9},{9,8},{10,11... | collective-permute-start | bytes 3145736 | tf_op jit(solution)/shard_map/ppermute | solution.py:188
  12.7 19.5 %all-to-all-start = ((bf16[8,256,256]{2,1,0:T(8,128)(2,1)}), bf16[8,256,256]{2,1,0:T(8,128)(2,1)S(1)}, u32[]{:S(2)}, u32[]{:S(2)}) async-start(bf16[8,256,256]{2,1,0:T(8,128)(2,1)} %add_convert_fusion), calls=%async_computation | async-start | bytes 2097152 | tf_op jit(solution)/shard_map/all_to_all | solution.py:211
  21.4 6.4 %collective-permute-start.1 = (bf16[64,1280]{1,0:T(8,128)(2,1)S(1)}, bf16[64,1280]{1,0:T(8,128)(2,1)S(1)}, u32[]{:S(2)}, u32[]{:S(2)}) collective-permute-start(bf16[64,1280]{1,0:T(8,128)(2,1)S(1)} %get-tuple-element.19), channel_id=1, source_target_pairs={{0,64},{64,128},{128,192},{192,0},{1,65},{65,129},{129,193},{193,1... | collective-permute-start | bytes 491528 | tf_op jit(solution)/shard_map/ppermute | solution.py:205
  22.7 9.6 %collective-permute-start.2 = (bf16[64,1280]{1,0:T(8,128)(2,1)S(1)}, bf16[64,1280]{1,0:T(8,128)(2,1)S(1)}, u32[]{:S(2)}, u32[]{:S(2)}) collective-permute-start(bf16[64,1280]{1,0:T(8,128)(2,1)S(1)} %get-tuple-element.20), channel_id=1, source_target_pairs={{0,128},{64,192},{128,0},{192,64},{1,129},{65,193},{129,1},{193,65... | collective-permute-start | bytes 491528 | tf_op jit(solution)/shard_map/ppermute | solution.py:205
  25.1 7.1 %collective-permute-start.3 = (bf16[64,1280]{1,0:T(8,128)(2,1)S(1)}, bf16[64,1280]{1,0:T(8,128)(2,1)S(1)}, u32[]{:S(2)}, u32[]{:S(2)}) collective-permute-start(bf16[64,1280]{1,0:T(8,128)(2,1)S(1)} %get-tuple-element.21), channel_id=1, source_target_pairs={{0,192},{64,0},{128,64},{192,128},{1,193},{65,1},{129,65},{193,129... | collective-permute-start | bytes 491528 | tf_op jit(solution)/shard_map/ppermute | solution.py:205
  32.4 9.7 %collective-permute-start.4 = (bf16[256,256]{1,0:T(8,128)(2,1)S(1)}, bf16[256,256]{1,0:T(8,128)(2,1)S(1)}, u32[]{:S(2)}, u32[]{:S(2)}) collective-permute-start(bf16[256,256]{1,0:T(8,128)(2,1)S(1)} %reduce_sum.12.refs_0_), channel_id=1, source_target_pairs={{0,16},{16,32},{32,48},{48,0},{1,17},{17,33},{33,49},{49,1},{2,18}... | collective-permute-start | bytes 393224 | tf_op jit(solution)/shard_map/ppermute | solution.py:216
  35.5 10.6 %collective-permute-start.5 = (bf16[256,256]{1,0:T(8,128)(2,1)S(1)}, bf16[256,256]{1,0:T(8,128)(2,1)S(1)}, u32[]{:S(2)}, u32[]{:S(2)}) collective-permute-start(bf16[256,256]{1,0:T(8,128)(2,1)S(1)} %reduce_sum.12.refs_0_), channel_id=1, source_target_pairs={{0,32},{16,48},{32,0},{48,16},{1,33},{17,49},{33,1},{49,17},{2,34}... | collective-permute-start | bytes 393224 | tf_op jit(solution)/shard_map/ppermute | solution.py:216
  39.7 6.4 %collective-permute-start.6 = (bf16[256,256]{1,0:T(8,128)(2,1)S(1)}, bf16[256,256]{1,0:T(8,128)(2,1)S(1)}, u32[]{:S(2)}, u32[]{:S(2)}) collective-permute-start(bf16[256,256]{1,0:T(8,128)(2,1)S(1)} %reduce_sum.12.refs_0_), channel_id=1, source_target_pairs={{0,48},{16,0},{32,16},{48,32},{1,49},{17,1},{33,17},{49,33},{2,50}... | collective-permute-start | bytes 393224 | tf_op jit(solution)/shard_map/ppermute | solution.py:216
  46.1 30.8 %copy-start.1 = (bf16[2,256,1280]{2,1,0:T(8,128)(2,1)S(1)}, bf16[2,256,1280]{2,1,0:T(8,128)(2,1)}, u32[]{:S(2)}) copy-start(bf16[2,256,1280]{2,1,0:T(8,128)(2,1)} %q_ref.3) | copy-start | bytes 3932164
  48.3 28.6 %copy-start = (f32[5,256,256]{2,1,0:T(8,128)S(1)}, f32[5,256,256]{2,1,0:T(8,128)}, u32[]{:S(2)}) copy-start(f32[5,256,256]{2,1,0:T(8,128)} %g_ref.5) | copy-start | bytes 3932164
  71.2 5.6 %collective-permute-start.7 = (bf16[8,256,256]{2,1,0:T(8,128)(2,1)S(1)}, bf16[8,256,256]{2,1,0:T(8,128)(2,1)S(1)}, u32[]{:S(2)}, u32[]{:S(2)}) collective-permute-start(bf16[8,256,256]{2,1,0:T(8,128)(2,1)S(1)} %all_to_all.15.mine_ref), channel_id=1, source_target_pairs={{0,1},{1,0},{2,3},{3,2},{4,5},{5,4},{6,7},{7,6},{8,9},{9,8},{10,11... | collective-permute-start | bytes 3145736 | tf_op jit(solution)/shard_map/ppermute | solution.py:225
  82.0 14.0 %all-to-all-start.2 = ((bf16[4,64,1280]{2,1,0:T(8,128)(2,1)}), bf16[4,64,1280]{2,1,0:T(8,128)(2,1)S(1)}, u32[]{:S(2)}, u32[]{:S(2)}) async-start(bf16[4,64,1280]{2,1,0:T(8,128)(2,1)} %bitcast.2), calls=%async_computation.2 | async-start | bytes 1310720 | tf_op jit(solution)/shard_map/all_to_all | solution.py:241

commit v6 on v5

--- a/solution.py
+++ b/solution.py
@@ -16,6 +16,7 @@
 HEADS_HERE = 5
 MATS = 3 * HEADS_HERE
 GROUP = 8
+N_FAR = 4
 VMEM_LIMIT = 48 * 1024 * 1024
 
 
@@ -53,9 +54,14 @@
         out_ref[...] = rows_ref[pl.ds(pl.multiple_of(to * part, part), part), :]
 
 
-def grad_kernel(core_ref, k_ref, v_ref, rate_ref, g_ref, u_ref, d_ref, keep_ref, send_ref):
+def twist_of(far_ref):
+    return jnp.where(far_ref[0] >= N_FAR // 2, 1, 0)
+
+
+def grad_kernel(core_ref, far_ref, k_ref, v_ref, rate_ref, g_ref, u_ref, d_ref, keep_ref, send_ref):
     head = pl.program_id(0)
     core = core_ref[0]
+    twist = twist_of(far_ref)
     gate = g_ref[0].astype(BF16)
     up = u_ref[0].astype(BF16)
     down = d_ref[0].astype(BF16)
@@ -84,7 +90,7 @@
 
                 @pl.when(inside & wanted)
                 def _(ref=ref, slot=slot, grad=grad):
-                    ref[slot] = grad
+                    ref[jnp.bitwise_xor(slot, twist)] = grad
 
 
 def split(x):
@@ -121,14 +127,15 @@
     return (fast - orth.astype(F32)).astype(BF16)
 
 
-def second_kernel(core_ref, q_ref, g_ref, u_ref, d_ref, mine_ref, other_ref, out_ref):
+def second_kernel(core_ref, far_ref, q_ref, g_ref, u_ref, d_ref, mine_ref, other_ref, out_ref):
     head = pl.program_id(0)
     low_core = core_ref[0] == 0
+    twist = twist_of(far_ref)
     nexts = []
     for mat, ref in enumerate((g_ref, u_ref, d_ref)):
         at = head * 3 + mat
         in_low = at < GROUP
-        index = jnp.where(in_low, at, at - (GROUP - 1))
+        index = jnp.bitwise_xor(jnp.where(in_low, at, at - (GROUP - 1)), twist)
         orth = jnp.where(in_low == low_core, mine_ref[index], other_ref[index])
         nexts.append(next_weight(ref[0], orth))
     out_ref[...] = apply_fast(q_ref[0], *nexts)
@@ -143,14 +150,23 @@
             refs[-1][0] = ref[...]
 
 
-def lay_second_kernel(buf_ref, rows_ref, out_ref):
-    out_ref[...] = rows_ref[...]
+def lay_second_kernel(buf_ref, rows_ref, out_ref, sems):
+    count, _, width = rows_ref.shape
+    copies = [
+        pltpu.make_async_copy(rows_ref.at[i], out_ref.at[1, :, pl.ds(i * width, width)], sems.at[i])
+        for i in range(count)
+    ]
+    for copy in copies:
+        copy.start()
+    for copy in copies:
+        copy.wait()
 
 
 def local(queries, key_rows, value_rows, step_rates, gate_fast, up_fast, down_fast):
     rows = key_rows.shape[0]
     width = key_rows.shape[1]
     core = lax.axis_index("core").astype(jnp.int32).reshape(1)
+    far = lax.axis_index("z_hi").astype(jnp.int32).reshape(1)
     n_head = lax.axis_size("head")
     part = rows // n_head
     params = pltpu.CompilerParams(dimension_semantics=("arbitrary",), vmem_limit_bytes=VMEM_LIMIT)
@@ -159,7 +175,7 @@
     rows_shape = jax.ShapeDtypeStruct((rows, width), BF16)
 
     piece_shape = (GROUP, HD, HD)
-    piece_spec = pl.BlockSpec(piece_shape, lambda h, c: (0, 0, 0))
+    piece_spec = pl.BlockSpec(piece_shape, lambda h, *_: (0, 0, 0))
     args = (queries, key_rows, value_rows, step_rates, gate_fast, up_fast, down_fast)
     q_hbm, k_hbm, v_hbm, rate_hbm, g_hbm, u_hbm, d_hbm = [
         pltpu.with_memory_space_constraint(x, pltpu.HBM) for x in args
@@ -167,12 +183,12 @@
     keep, send = pl.pallas_call(
         grad_kernel,
         grid_spec=pltpu.PrefetchScalarGridSpec(
-            num_scalar_prefetch=1,
+            num_scalar_prefetch=2,
             grid=(HEADS_HERE,),
             in_specs=[
                 rows_spec,
                 rows_spec,
-                pl.BlockSpec((HEADS_HERE, rows), lambda h, c: (0, 0)),
+                pl.BlockSpec((HEADS_HERE, rows), lambda h, *_: (0, 0)),
                 weight_spec,
                 weight_spec,
                 weight_spec,
@@ -182,7 +198,7 @@
         out_shape=[jax.ShapeDtypeStruct(piece_shape, BF16), jax.ShapeDtypeStruct(piece_shape, BF16)],
         compiler_params=params,
         name="grads",
-    )(core, k_hbm, v_hbm, rate_hbm, g_hbm, u_hbm, d_hbm)
+    )(core, far, k_hbm, v_hbm, rate_hbm, g_hbm, u_hbm, d_hbm)
 
     swap = [(0, 1), (1, 0)]
     received = lax.ppermute(send, "core", swap)
@@ -209,12 +225,16 @@
     chip_sum = (keep.astype(F32) + received.astype(F32)).astype(BF16)
     slots = ("y", "z_lo")
     by_slot = lax.all_to_all(chip_sum, slots, split_axis=0, concat_axis=0, tiled=True)
-    by_slot, *firsts = lax.optimization_barrier((by_slot, *firsts))
     partial = jnp.sum(by_slot.astype(F32), axis=0).astype(BF16)
-    n_far = lax.axis_size("z_hi")
+    rings = [[2 * i + (slot ^ (i >= N_FAR // 2)) for i in range(N_FAR)] for slot in range(2)]
     partials = [partial] + [
-        lax.ppermute(partial, "z_hi", [(i, (i + hop) % n_far) for i in range(n_far)]) for hop in range(1, n_far)
+        lax.ppermute(
+            partial, ("z_hi", "z_lo"), [(ring[i], ring[(i + hop) % N_FAR]) for ring in rings for i in range(N_FAR)]
+        )
+        for hop in range(1, N_FAR)
     ]
+    late = lax.optimization_barrier((*partials, *firsts))
+    partials, firsts = late[:N_FAR], late[N_FAR:]
     orth = pl.pallas_call(
         orth_kernel,
         out_shape=jax.ShapeDtypeStruct(piece_shape, BF16),
@@ -224,19 +244,19 @@
     orth_mine = lax.all_to_all(orth, slots, split_axis=0, concat_axis=0, tiled=True)
     orth_other = lax.ppermute(orth_mine, "core", swap)
 
-    group_spec = pl.BlockSpec((GROUP, HD, HD), lambda h, c: (0, 0, 0))
+    group_spec = pl.BlockSpec((GROUP, HD, HD), lambda h, *_: (0, 0, 0))
     second = pl.pallas_call(
         second_kernel,
         grid_spec=pltpu.PrefetchScalarGridSpec(
-            num_scalar_prefetch=1,
+            num_scalar_prefetch=2,
             grid=(HEADS_HERE,),
-            in_specs=[pl.BlockSpec((1, rows, HD), lambda h, c: (1, 0, h))] + [weight_spec] * 3 + [group_spec] * 2,
+            in_specs=[pl.BlockSpec((1, rows, HD), lambda h, *_: (1, 0, h))] + [weight_spec] * 3 + [group_spec] * 2,
             out_specs=rows_spec,
         ),
         out_shape=rows_shape,
         compiler_params=params,
         name="second",
-    )(core, queries, gate_fast, up_fast, down_fast, orth_mine, orth_other)
+    )(core, far, queries, gate_fast, up_fast, down_fast, orth_mine, orth_other)
 
     swapped = lax.all_to_all(second.reshape(n_head, part, width), "head", split_axis=0, concat_axis=0, tiled=True)
     out_shape = jax.ShapeDtypeStruct((2, part, n_head * width), BF16)
@@ -254,15 +274,11 @@
     )(place, *firsts)
     return pl.pallas_call(
         lay_second_kernel,
-        grid=(n_head,),
-        in_specs=[
-            pl.BlockSpec(memory_space=pl.ANY),
-            pl.BlockSpec((1, part, width), lambda s: (s, 0, 0)),
-        ],
-        out_specs=pl.BlockSpec((1, part, width), lambda s: (1, 0, s)),
+        in_specs=[pl.BlockSpec(memory_space=pl.ANY), pl.BlockSpec(memory_space=pltpu.VMEM)],
+        out_specs=pl.BlockSpec(memory_space=pl.ANY),
         out_shape=out_shape,
         input_output_aliases={0: 0},
-        compiler_params=params,
+        scratch_shapes=[pltpu.SemaphoreType.DMA((n_head,))],
         name="lay_second",
     )(out, swapped)
 

time: 97.9 us -> 97 us (level)
  blocking collectives: 23 us -> 17.7 us
  waiting for transfers between devices: 23.4 us -> 26.7 us
    ppermute x3, waiting for transfers between devices: 6 us -> 0.01 us  [local(): lax.ppermute(firsts[hop], 'head', [(i, (i + hop) % n_head) for i in range...]
    all_to_all x1, waiting for transfers between devices: 0.01 us -> 5.43 us  [local(): lax.all_to_all(chip_sum, slots, split_axis=0, concat_axis=0, tiled=True)]
    all_to_all x1, blocking collectives: 23 us -> 17.7 us  [local(): lax.all_to_all(orth, slots, split_axis=0, concat_axis=0, tiled=True)]
    ppermute x3, waiting for transfers between devices: 3.98 us -> 7.8 us  [local(): lax.ppermute(partial, ('z_hi', 'z_lo'), [(ring[i], ring[(i + hop) % N_FAR...]
  transfers between devices with their start and end apart: 10 -> 10, of which waited for: 6 -> 7; matrix products, arithmetic and copies ran while one was open for 0% -> 0% of each run, Pallas kernels for 6% -> 7%
where the time goes in v6:
time: 97 us; the launch traced here: 96.4 us
  starting transfers between devices  28.3 us (29%)
  waiting for transfers between devices  26.7 us (28%)
  Pallas kernels  21.4 us (22%)
  blocking collectives  17.7 us (18%)
  other arithmetic  1.43 us (1%)
    all_to_all x1, blocking collectives, local(): lax.all_to_all(orth, slots, split_axis=0, concat_axis=0, tiled=True)  17.7 us
    ppermute x3, starting transfers between devices, local(): lax.ppermute(partial, ('z_hi', 'z_lo'), [(ring[i], ring[(i + hop) % N_FAR...  9.01 us
    all_to_all x1, waiting for transfers between devices, local(): lax.all_to_all(second.reshape(n_head, part, width), 'head', split_axis=0,...  8.87 us
    ppermute x3, waiting for transfers between devices, local(): lax.ppermute(partial, ('z_hi', 'z_lo'), [(ring[i], ring[(i + hop) % N_FAR...  7.8 us
    pallas_call x1, Pallas kernels, local(): pl.pallas_call(grad_kernel, grid_spec=pltpu.PrefetchScalarGridSpec(num_sc...  5.83 us
    all_to_all x1, waiting for transfers between devices, local(): lax.all_to_all(chip_sum, slots, split_axis=0, concat_axis=0, tiled=True)  5.43 us
    pallas_call x1, Pallas kernels, local(): pl.pallas_call(second_kernel, grid_spec=pltpu.PrefetchScalarGridSpec(num_...  5.2 us
    ppermute x3, starting transfers between devices, local(): lax.ppermute(firsts[hop], 'head', [(i, (i + hop) % n_head) for i in range...  4.89 us
  transfers between devices with their start and end apart: 10, of which 7 were waited for; matrix products, arithmetic and copies ran while one was open for 0% of the time, Pallas kernels for 7%

profile of v6, /device:TPU:1, one launch (start us, length us, event | category | flops | bytes accessed | tf_op | source)
XLA Modules:
  0.0 96.4 jit_solution(18290989344911166680)
XLA Ops:
  0.0 5.8 %grads.1 = (bf16[8,256,256]{2,1,0:T(8,128)(2,1)S(1)}, bf16[8,256,256]{2,1,0:T(8,128)(2,1)S(1)}) custom-call(s32[1]{0:T(128)} %bitcast.1.core_ref, s32[1]{0:T(128)} %bitcast.2.far_ref, bf16[256,1280]{1,0:T(8,128)(2,1)} %k_ref.1, bf16[256,1280]{1,0:T(8,128)(2,1)} %v_ref.1, f32[5,256]{1,0:T(8,128)} %rate_ref.1, f32[5,256,256]{2,1,0:T(8,128)} %g_ref.5, ...), custom_call_target="tpu_custom_call" | custom-call | tf_op jit(solution)/shard_map/grads/pallas_call | solution.py:183
  5.8 3.3 %collective-permute-start = (bf16[8,256,256]{2,1,0:T(8,128)(2,1)S(1)}, bf16[8,256,256]{2,1,0:T(8,128)(2,1)S(1)}, u32[]{:S(2)}, u32[]{:S(2)}) collective-permute-start(bf16[8,256,256]{2,1,0:T(8,128)(2,1)S(1)} %get-tuple-element.20), channel_id=1, source_target_pairs={{0,1},{1,0},{2,3},{3,2},{4,5},{5,4},{6,7},{7,6},{8,9},{9,8},{10,11... | collective-permute-start | bytes 3145736 | tf_op jit(solution)/shard_map/ppermute | solution.py:204
  9.2 2.3 %collective-permute-done = bf16[8,256,256]{2,1,0:T(8,128)(2,1)S(1)} collective-permute-done((bf16[8,256,256]{2,1,0:T(8,128)(2,1)S(1)}, bf16[8,256,256]{2,1,0:T(8,128)(2,1)S(1)}, u32[]{:S(2)}, u32[]{:S(2)}) %collective-permute-start) | collective-permute-done | bytes 1048608 | tf_op jit(solution)/shard_map/ppermute | solution.py:204
  11.5 1.3 %add_convert_fusion = bf16[8,256,256]{2,1,0:T(8,128)(2,1)} fusion(bf16[8,256,256]{2,1,0:T(8,128)(2,1)S(1)} %collective-permute-done, bf16[8,256,256]{2,1,0:T(8,128)(2,1)S(1)} %get-tuple-element.19), kind=kLoop, calls=%fused_computation | loop fusion | flops 2097152 | bytes 3145728 | tf_op jit(solution)/shard_map/convert_element_type | solution.py:225
  12.7 3.8 %all-to-all-start = ((bf16[8,256,256]{2,1,0:T(8,128)(2,1)}), bf16[8,256,256]{2,1,0:T(8,128)(2,1)S(1)}, u32[]{:S(2)}, u32[]{:S(2)}) async-start(bf16[8,256,256]{2,1,0:T(8,128)(2,1)} %add_convert_fusion), calls=%async_computation | async-start | bytes 2097152 | tf_op jit(solution)/shard_map/all_to_all | solution.py:227
  16.5 4.8 %first.1 = (bf16[64,1280]{1,0:T(8,128)(2,1)S(1)}, bf16[64,1280]{1,0:T(8,128)(2,1)S(1)}, bf16[64,1280]{1,0:T(8,128)(2,1)S(1)}, bf16[64,1280]{1,0:T(8,128)(2,1)S(1)}) custom-call(s32[1]{0:T(128)} %bitcast.place_ref, bf16[2,256,1280]{2,1,0:T(8,128)(2,1)} %q_ref.3, f32[5,256,256]{2,1,0:T(8,128)} %g_ref.5, f32[5,256,256]{2,1,0:T(8,128)} %u_ref.5, ...), custom_call_target="tpu_custom_call" | custom-call | tf_op jit(solution)/shard_map/first/pallas_call | solution.py:207
  21.4 1.3 %collective-permute-start.4 = (bf16[64,1280]{1,0:T(8,128)(2,1)S(1)}, bf16[64,1280]{1,0:T(8,128)(2,1)S(1)}, u32[]{:S(2)}, u32[]{:S(2)}) collective-permute-start(bf16[64,1280]{1,0:T(8,128)(2,1)S(1)} %get-tuple-element.22), channel_id=1, source_target_pairs={{0,64},{64,128},{128,192},{192,0},{1,65},{65,129},{129,193},{193,1... | collective-permute-start | bytes 491528 | tf_op jit(solution)/shard_map/ppermute | solution.py:221
  22.7 2.5 %collective-permute-start.5 = (bf16[64,1280]{1,0:T(8,128)(2,1)S(1)}, bf16[64,1280]{1,0:T(8,128)(2,1)S(1)}, u32[]{:S(2)}, u32[]{:S(2)}) collective-permute-start(bf16[64,1280]{1,0:T(8,128)(2,1)S(1)} %get-tuple-element.23), channel_id=1, source_target_pairs={{0,128},{64,192},{128,0},{192,64},{1,129},{65,193},{129,1},{193,65... | collective-permute-start | bytes 491528 | tf_op jit(solution)/shard_map/ppermute | solution.py:221
  25.1 1.1 %collective-permute-start.6 = (bf16[64,1280]{1,0:T(8,128)(2,1)S(1)}, bf16[64,1280]{1,0:T(8,128)(2,1)S(1)}, u32[]{:S(2)}, u32[]{:S(2)}) collective-permute-start(bf16[64,1280]{1,0:T(8,128)(2,1)S(1)} %get-tuple-element.24), channel_id=1, source_target_pairs={{0,192},{64,0},{128,64},{192,128},{1,193},{65,1},{129,65},{193,129... | collective-permute-start | bytes 491528 | tf_op jit(solution)/shard_map/ppermute | solution.py:221
  26.3 5.4 %all-to-all-done = bf16[8,256,256]{2,1,0:T(8,128)(2,1)S(1)} async-done(((bf16[8,256,256]{2,1,0:T(8,128)(2,1)}), bf16[8,256,256]{2,1,0:T(8,128)(2,1)S(1)}, u32[]{:S(2)}, u32[]{:S(2)}) %all-to-all-start) | async-done | bytes 1048608 | tf_op jit(solution)/shard_map/all_to_all | solution.py:227
  31.7 0.1 reduce_sum.12.refs_0_
  31.9 3.1 %collective-permute-start.1 = (bf16[256,256]{1,0:T(8,128)(2,1)S(1)}, bf16[256,256]{1,0:T(8,128)(2,1)S(1)}, u32[]{:S(2)}, u32[]{:S(2)}) collective-permute-start(bf16[256,256]{1,0:T(8,128)(2,1)S(1)} %reduce_sum.12.refs_0_), channel_id=1, source_target_pairs={{0,16},{16,40},{40,56},{56,0},{8,24},{24,32},{32,48},{48,8},{1,17}... | collective-permute-start | bytes 393224 | tf_op jit(solution)/shard_map/ppermute | solution.py:231
  34.9 3.6 %collective-permute-start.2 = (bf16[256,256]{1,0:T(8,128)(2,1)S(1)}, bf16[256,256]{1,0:T(8,128)(2,1)S(1)}, u32[]{:S(2)}, u32[]{:S(2)}) collective-permute-start(bf16[256,256]{1,0:T(8,128)(2,1)S(1)} %reduce_sum.12.refs_0_), channel_id=1, source_target_pairs={{0,40},{16,56},{40,0},{56,16},{8,32},{24,48},{32,8},{48,24},{1,41}... | collective-permute-start | bytes 393224 | tf_op jit(solution)/shard_map/ppermute | solution.py:231
  38.5 0.0 collective-permute-done.4.refs_1_
  38.5 2.4 %collective-permute-start.3 = (bf16[256,256]{1,0:T(8,128)(2,1)S(1)}, bf16[256,256]{1,0:T(8,128)(2,1)S(1)}, u32[]{:S(2)}, u32[]{:S(2)}) collective-permute-start(bf16[256,256]{1,0:T(8,128)(2,1)S(1)} %reduce_sum.12.refs_0_), channel_id=1, source_target_pairs={{0,56},{16,0},{40,16},{56,40},{8,48},{24,8},{32,24},{48,32},{1,57}... | collective-permute-start | bytes 393224 | tf_op jit(solution)/shard_map/ppermute | solution.py:231
  40.9 0.0 collective-permute-done.5.refs_2_
  40.9 0.0 collective-permute-done.6.refs_3_
  40.9 1.6 %collective-permute-done.1.refs_1_ = bf16[256,256]{1,0:T(8,128)(2,1)S(1)} collective-permute-done((bf16[256,256]{1,0:T(8,128)(2,1)S(1)}, bf16[256,256]{1,0:T(8,128)(2,1)S(1)}, u32[]{:S(2)}, u32[]{:S(2)}) %collective-permute-start.1) | collective-permute-done | bytes 131104 | tf_op jit(solution)/shard_map/ppermute | solution.py:231
  42.5 6.0 %collective-permute-done.2.refs_2_ = bf16[256,256]{1,0:T(8,128)(2,1)S(1)} collective-permute-done((bf16[256,256]{1,0:T(8,128)(2,1)S(1)}, bf16[256,256]{1,0:T(8,128)(2,1)S(1)}, u32[]{:S(2)}, u32[]{:S(2)}) %collective-permute-start.2) | collective-permute-done | bytes 131104 | tf_op jit(solution)/shard_map/ppermute | solution.py:231
  48.5 0.2 collective-permute-done.3.refs_3_
  48.7 2.2 %orthogonalize.1 = bf16[8,256,256]{2,1,0:T(8,128)(2,1)S(1)} custom-call(bf16[256,256]{1,0:T(8,128)(2,1)S(1)} %reduce_sum.12.refs_0_, bf16[256,256]{1,0:T(8,128)(2,1)S(1)} %collective-permute-done.1.refs_1_, bf16[256,256]{1,0:T(8,128)(2,1)S(1)} %collective-permute-done.2.refs_2_, bf16[256,256]{1,0:T(8,128)(2,1)S(1)} %collective-permute-done.3.refs_3_), custom_call_target="tpu_custom_call" | custom-call | tf_op jit(solution)/shard_map/orthogonalize/pallas_call | solution.py:238
  50.9 0.0 copy-start
  50.9 17.7 %all_to_all.15.mine_ref = bf16[8,256,256]{2,1,0:T(8,128)(2,1)S(1)} all-to-all(bf16[8,256,256]{2,1,0:T(8,128)(2,1)S(1)} %orthogonalize.1), channel_id=1, replica_groups=mesh['head'=4,'z_hi'=4,'z_lo'=2,'y'=4,'core'=2] {'y','z_lo'}, dimensions={0} | all-to-all | bytes 2097152 | tf_op jit(solution)/shard_map/all_to_all | solution.py:244
  68.6 3.2 %collective-permute-start.7 = (bf16[8,256,256]{2,1,0:T(8,128)(2,1)S(1)}, bf16[8,256,256]{2,1,0:T(8,128)(2,1)S(1)}, u32[]{:S(2)}, u32[]{:S(2)}) collective-permute-start(bf16[8,256,256]{2,1,0:T(8,128)(2,1)S(1)} %all_to_all.15.mine_ref), channel_id=1, source_target_pairs={{0,1},{1,0},{2,3},{3,2},{4,5},{5,4},{6,7},{7,6},{8,9},{9,8},{10,11... | collective-permute-start | bytes 3145736 | tf_op jit(solution)/shard_map/ppermute | solution.py:245
  71.8 2.3 %collective-permute-done.7.other_ref = bf16[8,256,256]{2,1,0:T(8,128)(2,1)S(1)} collective-permute-done((bf16[8,256,256]{2,1,0:T(8,128)(2,1)S(1)}, bf16[8,256,256]{2,1,0:T(8,128)(2,1)S(1)}, u32[]{:S(2)}, u32[]{:S(2)}) %collective-permute-start.7) | collective-permute-done | bytes 1048608 | tf_op jit(solution)/shard_map/ppermute | solution.py:245
  74.1 0.0 copy-done.1
  74.1 5.2 %second.1 = bf16[256,1280]{1,0:T(8,128)(2,1)} custom-call(s32[1]{0:T(128)} %bitcast.1.core_ref, s32[1]{0:T(128)} %bitcast.2.far_ref, bf16[2,256,1280]{2,1,0:T(8,128)(2,1)S(1)} %copy-done.1, f32[5,256,256]{2,1,0:T(8,128)S(1)} %copy-done, f32[5,256,256]{2,1,0:T(8,128)} %u_ref.5, f32[5,256,256]{2,1,0:T(8,128)} %d_ref.5, ...), custom_call_target="tpu_custom_call" | custom-call | tf_op jit(solution)/shard_map/second/pallas_call | solution.py:248
  79.3 4.0 %all-to-all-start.2 = ((bf16[4,64,1280]{2,1,0:T(8,128)(2,1)}), bf16[4,64,1280]{2,1,0:T(8,128)(2,1)S(1)}, u32[]{:S(2)}, u32[]{:S(2)}) async-start(bf16[4,64,1280]{2,1,0:T(8,128)(2,1)} %bitcast.3), calls=%async_computation.2 | async-start | bytes 1310720 | tf_op jit(solution)/shard_map/all_to_all | solution.py:261
  83.4 1.4 %lay_first.1.buf_ref = bf16[2,64,5120]{2,1,0:T(8,128)(2,1)} custom-call(s32[1]{0:T(128)} %bitcast.place_ref, bf16[64,1280]{1,0:T(8,128)(2,1)S(1)} %get-tuple-element.25.refs_0_, bf16[64,1280]{1,0:T(8,128)(2,1)S(1)} %collective-permute-done.4.refs_1_, bf16[64,1280]{1,0:T(8,128)(2,1)S(1)} %collective-permute-done.5.refs_2_, ...), custom_call_target="tpu_custom_call" | custom-call | tf_op jit(solution)/shard_map/lay_first/pallas_call | solution.py:263
  84.8 8.9 %all-to-all-done.2.rows_ref = bf16[4,64,1280]{2,1,0:T(8,128)(2,1)S(1)} async-done(((bf16[4,64,1280]{2,1,0:T(8,128)(2,1)}), bf16[4,64,1280]{2,1,0:T(8,128)(2,1)S(1)}, u32[]{:S(2)}, u32[]{:S(2)}) %all-to-all-start.2) | async-done | bytes 655392 | tf_op jit(solution)/shard_map/all_to_all | solution.py:261
  93.7 0.8 copy-done.2
  94.5 1.9 %lay_second.1 = bf16[2,64,5120]{2,1,0:T(8,128)(2,1)} custom-call(bf16[2,64,5120]{2,1,0:T(8,128)(2,1)} %lay_first.1.buf_ref, bf16[4,64,1280]{2,1,0:T(8,128)(2,1)} %copy-done.2), custom_call_target="tpu_custom_call", output_to_operand_aliasing={{}: (0, {})} | custom-call | tf_op jit(solution)/shard_map/lay_second/pallas_call | solution.py:275
  (3 shorter events, 0.0 us)
Async XLA Ops:
  5.8 5.6 %collective-permute-start = (bf16[8,256,256]{2,1,0:T(8,128)(2,1)S(1)}, bf16[8,256,256]{2,1,0:T(8,128)(2,1)S(1)}, u32[]{:S(2)}, u32[]{:S(2)}) collective-permute-start(bf16[8,256,256]{2,1,0:T(8,128)(2,1)S(1)} %get-tuple-element.20), channel_id=1, source_target_pairs={{0,1},{1,0},{2,3},{3,2},{4,5},{5,4},{6,7},{7,6},{8,9},{9,8},{10,11... | collective-permute-start | bytes 3145736 | tf_op jit(solution)/shard_map/ppermute | solution.py:204
  12.7 19.0 %all-to-all-start = ((bf16[8,256,256]{2,1,0:T(8,128)(2,1)}), bf16[8,256,256]{2,1,0:T(8,128)(2,1)S(1)}, u32[]{:S(2)}, u32[]{:S(2)}) async-start(bf16[8,256,256]{2,1,0:T(8,128)(2,1)} %add_convert_fusion), calls=%async_computation | async-start | bytes 2097152 | tf_op jit(solution)/shard_map/all_to_all | solution.py:227
  21.4 17.1 %collective-permute-start.4 = (bf16[64,1280]{1,0:T(8,128)(2,1)S(1)}, bf16[64,1280]{1,0:T(8,128)(2,1)S(1)}, u32[]{:S(2)}, u32[]{:S(2)}) collective-permute-start(bf16[64,1280]{1,0:T(8,128)(2,1)S(1)} %get-tuple-element.22), channel_id=1, source_target_pairs={{0,64},{64,128},{128,192},{192,0},{1,65},{65,129},{129,193},{193,1... | collective-permute-start | bytes 491528 | tf_op jit(solution)/shard_map/ppermute | solution.py:221
  22.7 18.2 %collective-permute-start.5 = (bf16[64,1280]{1,0:T(8,128)(2,1)S(1)}, bf16[64,1280]{1,0:T(8,128)(2,1)S(1)}, u32[]{:S(2)}, u32[]{:S(2)}) collective-permute-start(bf16[64,1280]{1,0:T(8,128)(2,1)S(1)} %get-tuple-element.23), channel_id=1, source_target_pairs={{0,128},{64,192},{128,0},{192,64},{1,129},{65,193},{129,1},{193,65... | collective-permute-start | bytes 491528 | tf_op jit(solution)/shard_map/ppermute | solution.py:221
  25.1 15.7 %collective-permute-start.6 = (bf16[64,1280]{1,0:T(8,128)(2,1)S(1)}, bf16[64,1280]{1,0:T(8,128)(2,1)S(1)}, u32[]{:S(2)}, u32[]{:S(2)}) collective-permute-start(bf16[64,1280]{1,0:T(8,128)(2,1)S(1)} %get-tuple-element.24), channel_id=1, source_target_pairs={{0,192},{64,0},{128,64},{192,128},{1,193},{65,1},{129,65},{193,129... | collective-permute-start | bytes 491528 | tf_op jit(solution)/shard_map/ppermute | solution.py:221
  31.9 10.6 %collective-permute-start.1 = (bf16[256,256]{1,0:T(8,128)(2,1)S(1)}, bf16[256,256]{1,0:T(8,128)(2,1)S(1)}, u32[]{:S(2)}, u32[]{:S(2)}) collective-permute-start(bf16[256,256]{1,0:T(8,128)(2,1)S(1)} %reduce_sum.12.refs_0_), channel_id=1, source_target_pairs={{0,16},{16,40},{40,56},{56,0},{8,24},{24,32},{32,48},{48,8},{1,17}... | collective-permute-start | bytes 393224 | tf_op jit(solution)/shard_map/ppermute | solution.py:231
  34.9 13.6 %collective-permute-start.2 = (bf16[256,256]{1,0:T(8,128)(2,1)S(1)}, bf16[256,256]{1,0:T(8,128)(2,1)S(1)}, u32[]{:S(2)}, u32[]{:S(2)}) collective-permute-start(bf16[256,256]{1,0:T(8,128)(2,1)S(1)} %reduce_sum.12.refs_0_), channel_id=1, source_target_pairs={{0,40},{16,56},{40,0},{56,16},{8,32},{24,48},{32,8},{48,24},{1,41}... | collective-permute-start | bytes 393224 | tf_op jit(solution)/shard_map/ppermute | solution.py:231
  38.5 10.2 %collective-permute-start.3 = (bf16[256,256]{1,0:T(8,128)(2,1)S(1)}, bf16[256,256]{1,0:T(8,128)(2,1)S(1)}, u32[]{:S(2)}, u32[]{:S(2)}) collective-permute-start(bf16[256,256]{1,0:T(8,128)(2,1)S(1)} %reduce_sum.12.refs_0_), channel_id=1, source_target_pairs={{0,56},{16,0},{40,16},{56,40},{8,48},{24,8},{32,24},{48,32},{1,57}... | collective-permute-start | bytes 393224 | tf_op jit(solution)/shard_map/ppermute | solution.py:231
  48.7 25.4 %copy-start.1 = (bf16[2,256,1280]{2,1,0:T(8,128)(2,1)S(1)}, bf16[2,256,1280]{2,1,0:T(8,128)(2,1)}, u32[]{:S(2)}) copy-start(bf16[2,256,1280]{2,1,0:T(8,128)(2,1)} %q_ref.3) | copy-start | bytes 3932164
  50.9 23.2 %copy-start = (f32[5,256,256]{2,1,0:T(8,128)S(1)}, f32[5,256,256]{2,1,0:T(8,128)}, u32[]{:S(2)}) copy-start(f32[5,256,256]{2,1,0:T(8,128)} %g_ref.5) | copy-start | bytes 3932164
  68.6 5.5 %collective-permute-start.7 = (bf16[8,256,256]{2,1,0:T(8,128)(2,1)S(1)}, bf16[8,256,256]{2,1,0:T(8,128)(2,1)S(1)}, u32[]{:S(2)}, u32[]{:S(2)}) collective-permute-start(bf16[8,256,256]{2,1,0:T(8,128)(2,1)S(1)} %all_to_all.15.mine_ref), channel_id=1, source_target_pairs={{0,1},{1,0},{2,3},{3,2},{4,5},{5,4},{6,7},{7,6},{8,9},{9,8},{10,11... | collective-permute-start | bytes 3145736 | tf_op jit(solution)/shard_map/ppermute | solution.py:245
  79.3 14.3 %all-to-all-start.2 = ((bf16[4,64,1280]{2,1,0:T(8,128)(2,1)}), bf16[4,64,1280]{2,1,0:T(8,128)(2,1)S(1)}, u32[]{:S(2)}, u32[]{:S(2)}) async-start(bf16[4,64,1280]{2,1,0:T(8,128)(2,1)} %bitcast.3), calls=%async_computation.2 | async-start | bytes 1310720 | tf_op jit(solution)/shard_map/all_to_all | solution.py:261
  93.7 0.8 copy-start.2

commit v7 on v6

--- a/solution.py
+++ b/solution.py
@@ -58,39 +58,67 @@
     return jnp.where(far_ref[0] >= N_FAR // 2, 1, 0)
 
 
-def grad_kernel(core_ref, far_ref, k_ref, v_ref, rate_ref, g_ref, u_ref, d_ref, keep_ref, send_ref):
-    head = pl.program_id(0)
-    core = core_ref[0]
+def grad_kernel(core_ref, far_ref, k_ref, v_ref, rate_ref, g_ref, u_ref, d_ref, keep_ref, send_ref, *scratch):
+    rates, keys, values, gates, ups, downs, rate_sem, sems = scratch
     twist = twist_of(far_ref)
-    gate = g_ref[0].astype(BF16)
-    up = u_ref[0].astype(BF16)
-    down = d_ref[0].astype(BF16)
-    keys = k_ref[...]
+    rate_copy = pltpu.make_async_copy(rate_ref, rates, rate_sem)
+    rate_copy.start()
+    copies = []
+    for head in range(HEADS_HERE):
+        cols = pl.ds(head * HD, HD)
+        pairs = (
+            (k_ref.at[:, cols], keys),
+            (v_ref.at[:, cols], values),
+            (g_ref.at[head], gates),
+            (u_ref.at[head], ups),
+            (d_ref.at[head], downs),
+        )
+        copies.append([pltpu.make_async_copy(src, dst.at[head], sems.at[head, i]) for i, (src, dst) in enumerate(pairs)])
+        for copy in copies[-1]:
+            copy.start()
+    rate_copy.wait()
+
+    def all_heads(group_refs):
+        for head in range(HEADS_HERE):
+            for copy in copies[head]:
+                copy.wait()
+            grads = head_grads(
+                keys[head],
+                values[head],
+                rates[head : head + 1, :],
+                gates[head].astype(BF16),
+                ups[head].astype(BF16),
+                downs[head].astype(BF16),
+            )
+            for mat, grad in enumerate(grads):
+                for group, ref in enumerate(group_refs):
+                    slot = head * 3 + mat - group * (GROUP - 1)
+                    if 0 <= slot < GROUP:
+                        ref[jnp.bitwise_xor(slot, twist)] = grad
+
+    @pl.when(core_ref[0] == 0)
+    def _():
+        all_heads((keep_ref, send_ref))
+
+    @pl.when(core_ref[0] != 0)
+    def _():
+        all_heads((send_ref, keep_ref))
+
+
+def head_grads(keys, values, rate, gate, up, down):
     zg = dot_f32(keys, gate)
     zu = dot_f32(keys, up)
     sig = sigmoid(zg)
     silu = zg * sig
     hidden = (silu * zu).astype(BF16)
-    rate = rate_ref[pl.ds(head, 1), :]
     rate = jnp.transpose(jnp.broadcast_to(rate, (HALF, rate.shape[1])))
     rate = jnp.concatenate([rate, rate], axis=1)
-    dout = (-(rate * v_ref[...].astype(F32))).astype(BF16)
+    dout = (-(rate * values.astype(F32))).astype(BF16)
     dh = dot_nt(dout, down)
     dzu = (dh * silu).astype(BF16)
     dzg = (dh * zu * sig * (1.0 + zg * (1.0 - sig))).astype(BF16)
     pair = dot_tn(keys, jnp.concatenate([dzg, dzu], axis=1)).astype(BF16)
-    grads = (pair[:, :HD], pair[:, HD:], dot_tn(hidden, dout).astype(BF16))
-    for mat in range(3):
-        grad = grads[mat]
-        at = head * 3 + mat
-        for group in range(2):
-            slot = at - group * (GROUP - 1)
-            inside = (slot >= 0) & (slot < GROUP)
-            for ref, wanted in ((keep_ref, core == group), (send_ref, core != group)):
-
-                @pl.when(inside & wanted)
-                def _(ref=ref, slot=slot, grad=grad):
-                    ref[jnp.bitwise_xor(slot, twist)] = grad
+    return pair[:, :HD], pair[:, HD:], dot_tn(hidden, dout).astype(BF16)
 
 
 def split(x):
@@ -128,17 +156,19 @@
 
 
 def second_kernel(core_ref, far_ref, q_ref, g_ref, u_ref, d_ref, mine_ref, other_ref, out_ref):
-    head = pl.program_id(0)
     low_core = core_ref[0] == 0
     twist = twist_of(far_ref)
-    nexts = []
-    for mat, ref in enumerate((g_ref, u_ref, d_ref)):
-        at = head * 3 + mat
-        in_low = at < GROUP
-        index = jnp.bitwise_xor(jnp.where(in_low, at, at - (GROUP - 1)), twist)
-        orth = jnp.where(in_low == low_core, mine_ref[index], other_ref[index])
-        nexts.append(next_weight(ref[0], orth))
-    out_ref[...] = apply_fast(q_ref[0], *nexts)
+    for head in range(HEADS_HERE):
+        nexts = []
+        for mat, ref in enumerate((g_ref, u_ref, d_ref)):
+            at = head * 3 + mat
+            in_low = at < GROUP
+            index = jnp.bitwise_xor(at if in_low else at - (GROUP - 1), twist)
+            pair = (mine_ref[index], other_ref[index])
+            orth = jnp.where(low_core, *(pair if in_low else pair[::-1]))
+            nexts.append(next_weight(ref[head], orth))
+        cols = slice(head * HD, (head + 1) * HD)
+        out_ref[:, cols] = apply_fast(q_ref[0, :, cols], *nexts)
 
 
 def lay_first_kernel(place_ref, *refs):
@@ -150,16 +180,8 @@
             refs[-1][0] = ref[...]
 
 
-def lay_second_kernel(buf_ref, rows_ref, out_ref, sems):
-    count, _, width = rows_ref.shape
-    copies = [
-        pltpu.make_async_copy(rows_ref.at[i], out_ref.at[1, :, pl.ds(i * width, width)], sems.at[i])
-        for i in range(count)
-    ]
-    for copy in copies:
-        copy.start()
-    for copy in copies:
-        copy.wait()
+def lay_second_kernel(buf_ref, rows_ref, out_ref):
+    out_ref[...] = rows_ref[...]
 
 
 def local(queries, key_rows, value_rows, step_rates, gate_fast, up_fast, down_fast):
@@ -171,7 +193,6 @@
     part = rows // n_head
     params = pltpu.CompilerParams(dimension_semantics=("arbitrary",), vmem_limit_bytes=VMEM_LIMIT)
     weight_spec = pl.BlockSpec((1, HD, HD), lambda h, *_: (h, 0, 0))
-    rows_spec = pl.BlockSpec((rows, HD), lambda h, *_: (0, h))
     rows_shape = jax.ShapeDtypeStruct((rows, width), BF16)
 
     piece_shape = (GROUP, HD, HD)
@@ -180,20 +201,24 @@
     q_hbm, k_hbm, v_hbm, rate_hbm, g_hbm, u_hbm, d_hbm = [
         pltpu.with_memory_space_constraint(x, pltpu.HBM) for x in args
     ]
+    any_spec = pl.BlockSpec(memory_space=pl.ANY)
     keep, send = pl.pallas_call(
         grad_kernel,
         grid_spec=pltpu.PrefetchScalarGridSpec(
             num_scalar_prefetch=2,
-            grid=(HEADS_HERE,),
-            in_specs=[
-                rows_spec,
-                rows_spec,
-                pl.BlockSpec((HEADS_HERE, rows), lambda h, *_: (0, 0)),
-                weight_spec,
-                weight_spec,
-                weight_spec,
+            grid=(1,),
+            in_specs=[any_spec] * 6,
+            out_specs=[piece_spec, piece_spec],
+            scratch_shapes=[
+                pltpu.VMEM((HEADS_HERE, rows), F32),
+                pltpu.VMEM((HEADS_HERE, rows, HD), BF16),
+                pltpu.VMEM((HEADS_HERE, rows, HD), BF16),
+                pltpu.VMEM((HEADS_HERE, HD, HD), F32),
+                pltpu.VMEM((HEADS_HERE, HD, HD), F32),
+                pltpu.VMEM((HEADS_HERE, HD, HD), F32),
+                pltpu.SemaphoreType.DMA(()),
+                pltpu.SemaphoreType.DMA((HEADS_HERE, 5)),
             ],
-            out_specs=[piece_spec, piece_spec],
         ),
         out_shape=[jax.ShapeDtypeStruct(piece_shape, BF16), jax.ShapeDtypeStruct(piece_shape, BF16)],
         compiler_params=params,
@@ -244,14 +269,15 @@
     orth_mine = lax.all_to_all(orth, slots, split_axis=0, concat_axis=0, tiled=True)
     orth_other = lax.ppermute(orth_mine, "core", swap)
 
-    group_spec = pl.BlockSpec((GROUP, HD, HD), lambda h, *_: (0, 0, 0))
+    group_spec = pl.BlockSpec((GROUP, HD, HD), lambda i, *_: (0, 0, 0))
+    fast_spec = pl.BlockSpec((HEADS_HERE, HD, HD), lambda i, *_: (0, 0, 0))
     second = pl.pallas_call(
         second_kernel,
         grid_spec=pltpu.PrefetchScalarGridSpec(
             num_scalar_prefetch=2,
-            grid=(HEADS_HERE,),
-            in_specs=[pl.BlockSpec((1, rows, HD), lambda h, *_: (1, 0, h))] + [weight_spec] * 3 + [group_spec] * 2,
-            out_specs=rows_spec,
+            grid=(1,),
+            in_specs=[pl.BlockSpec((1, rows, width), lambda i, *_: (1, 0, 0))] + [fast_spec] * 3 + [group_spec] * 2,
+            out_specs=pl.BlockSpec((rows, width), lambda i, *_: (0, 0)),
         ),
         out_shape=rows_shape,
         compiler_params=params,
@@ -274,11 +300,15 @@
     )(place, *firsts)
     return pl.pallas_call(
         lay_second_kernel,
-        in_specs=[pl.BlockSpec(memory_space=pl.ANY), pl.BlockSpec(memory_space=pltpu.VMEM)],
-        out_specs=pl.BlockSpec(memory_space=pl.ANY),
+        grid=(n_head,),
+        in_specs=[
+            pl.BlockSpec(memory_space=pl.ANY),
+            pl.BlockSpec((1, part, width), lambda s: (s, 0, 0)),
+        ],
+        out_specs=pl.BlockSpec((1, part, width), lambda s: (1, 0, s)),
         out_shape=out_shape,
         input_output_aliases={0: 0},
-        scratch_shapes=[pltpu.SemaphoreType.DMA((n_head,))],
+        compiler_params=params,
         name="lay_second",
     )(out, swapped)
 

time: 97 us -> 93.7 us (0.966)
  Pallas kernels: 21.4 us -> 19.2 us
    pallas_call x1, Pallas kernels: 5.2 us -> 3.81 us  [local(): pl.pallas_call(second_kernel, grid_spec=pltpu.PrefetchScalarGridSpec(num_...]
where the time goes in v7:
time: 93.7 us; the launch traced here: 93.4 us
  starting transfers between devices  28.3 us (30%)
  waiting for transfers between devices  26.7 us (28%)
  Pallas kernels  19.2 us (20%)
  blocking collectives  17.7 us (19%)
  other arithmetic  1.43 us (2%)
    all_to_all x1, blocking collectives, local(): lax.all_to_all(orth, slots, split_axis=0, concat_axis=0, tiled=True)  17.7 us
    ppermute x3, starting transfers between devices, local(): lax.ppermute(partial, ('z_hi', 'z_lo'), [(ring[i], ring[(i + hop) % N_FAR...  9.01 us
    all_to_all x1, waiting for transfers between devices, local(): lax.all_to_all(second.reshape(n_head, part, width), 'head', split_axis=0,...  8.88 us
    ppermute x3, waiting for transfers between devices, local(): lax.ppermute(partial, ('z_hi', 'z_lo'), [(ring[i], ring[(i + hop) % N_FAR...  7.79 us
    pallas_call x1, Pallas kernels, local(): pl.pallas_call(grad_kernel, grid_spec=pltpu.PrefetchScalarGridSpec(num_sc...  5.48 us
    all_to_all x1, waiting for transfers between devices, local(): lax.all_to_all(chip_sum, slots, split_axis=0, concat_axis=0, tiled=True)  5.43 us
    ppermute x3, starting transfers between devices, local(): lax.ppermute(firsts[hop], 'head', [(i, (i + hop) % n_head) for i in range...  4.89 us
    pallas_call x1, Pallas kernels, local(): pl.pallas_call(first_kernel, grid_spec=pltpu.PrefetchScalarGridSpec(num_s...  4.84 us
  transfers between devices with their start and end apart: 10, of which 7 were waited for; matrix products, arithmetic and copies ran while one was open for 0% of the time, Pallas kernels for 7%

profile of v7, /device:TPU:1, one launch (start us, length us, event | category | flops | bytes accessed | tf_op | source)
XLA Modules:
  0.0 93.4 jit_solution(7526304214688318980)
XLA Ops:
  0.0 5.5 %grads.1 = (bf16[8,256,256]{2,1,0:T(8,128)(2,1)S(1)}, bf16[8,256,256]{2,1,0:T(8,128)(2,1)S(1)}) custom-call(s32[1]{0:T(128)} %bitcast.1.core_ref, s32[1]{0:T(128)} %bitcast.2.far_ref, bf16[256,1280]{1,0:T(8,128)(2,1)} %k_ref.1, bf16[256,1280]{1,0:T(8,128)(2,1)} %v_ref.1, f32[5,256]{1,0:T(8,128)} %rate_ref.1, f32[5,256,256]{2,1,0:T(8,128)} %g_ref.5, ...), custom_call_target="tpu_custom_call" | custom-call | tf_op jit(solution)/shard_map/grads/pallas_call | solution.py:205
  5.5 3.3 %collective-permute-start = (bf16[8,256,256]{2,1,0:T(8,128)(2,1)S(1)}, bf16[8,256,256]{2,1,0:T(8,128)(2,1)S(1)}, u32[]{:S(2)}, u32[]{:S(2)}) collective-permute-start(bf16[8,256,256]{2,1,0:T(8,128)(2,1)S(1)} %get-tuple-element.20), channel_id=1, source_target_pairs={{0,1},{1,0},{2,3},{3,2},{4,5},{5,4},{6,7},{7,6},{8,9},{9,8},{10,11... | collective-permute-start | bytes 3145736 | tf_op jit(solution)/shard_map/ppermute | solution.py:229
  8.8 2.3 %collective-permute-done = bf16[8,256,256]{2,1,0:T(8,128)(2,1)S(1)} collective-permute-done((bf16[8,256,256]{2,1,0:T(8,128)(2,1)S(1)}, bf16[8,256,256]{2,1,0:T(8,128)(2,1)S(1)}, u32[]{:S(2)}, u32[]{:S(2)}) %collective-permute-start) | collective-permute-done | bytes 1048608 | tf_op jit(solution)/shard_map/ppermute | solution.py:229
  11.1 1.3 %add_convert_fusion = bf16[8,256,256]{2,1,0:T(8,128)(2,1)} fusion(bf16[8,256,256]{2,1,0:T(8,128)(2,1)S(1)} %collective-permute-done, bf16[8,256,256]{2,1,0:T(8,128)(2,1)S(1)} %get-tuple-element.19), kind=kLoop, calls=%fused_computation | loop fusion | flops 2097152 | bytes 3145728 | tf_op jit(solution)/shard_map/convert_element_type | solution.py:250
  12.4 3.8 %all-to-all-start = ((bf16[8,256,256]{2,1,0:T(8,128)(2,1)}), bf16[8,256,256]{2,1,0:T(8,128)(2,1)S(1)}, u32[]{:S(2)}, u32[]{:S(2)}) async-start(bf16[8,256,256]{2,1,0:T(8,128)(2,1)} %add_convert_fusion), calls=%async_computation | async-start | bytes 2097152 | tf_op jit(solution)/shard_map/all_to_all | solution.py:252
  16.2 4.8 %first.1 = (bf16[64,1280]{1,0:T(8,128)(2,1)S(1)}, bf16[64,1280]{1,0:T(8,128)(2,1)S(1)}, bf16[64,1280]{1,0:T(8,128)(2,1)S(1)}, bf16[64,1280]{1,0:T(8,128)(2,1)S(1)}) custom-call(s32[1]{0:T(128)} %bitcast.place_ref, bf16[2,256,1280]{2,1,0:T(8,128)(2,1)} %q_ref.3, f32[5,256,256]{2,1,0:T(8,128)} %g_ref.5, f32[5,256,256]{2,1,0:T(8,128)} %u_ref.5, ...), custom_call_target="tpu_custom_call" | custom-call | tf_op jit(solution)/shard_map/first/pallas_call | solution.py:232
  21.1 1.3 %collective-permute-start.4 = (bf16[64,1280]{1,0:T(8,128)(2,1)S(1)}, bf16[64,1280]{1,0:T(8,128)(2,1)S(1)}, u32[]{:S(2)}, u32[]{:S(2)}) collective-permute-start(bf16[64,1280]{1,0:T(8,128)(2,1)S(1)} %get-tuple-element.22), channel_id=1, source_target_pairs={{0,64},{64,128},{128,192},{192,0},{1,65},{65,129},{129,193},{193,1... | collective-permute-start | bytes 491528 | tf_op jit(solution)/shard_map/ppermute | solution.py:246
  22.3 2.5 %collective-permute-start.5 = (bf16[64,1280]{1,0:T(8,128)(2,1)S(1)}, bf16[64,1280]{1,0:T(8,128)(2,1)S(1)}, u32[]{:S(2)}, u32[]{:S(2)}) collective-permute-start(bf16[64,1280]{1,0:T(8,128)(2,1)S(1)} %get-tuple-element.23), channel_id=1, source_target_pairs={{0,128},{64,192},{128,0},{192,64},{1,129},{65,193},{129,1},{193,65... | collective-permute-start | bytes 491528 | tf_op jit(solution)/shard_map/ppermute | solution.py:246
  24.8 1.2 %collective-permute-start.6 = (bf16[64,1280]{1,0:T(8,128)(2,1)S(1)}, bf16[64,1280]{1,0:T(8,128)(2,1)S(1)}, u32[]{:S(2)}, u32[]{:S(2)}) collective-permute-start(bf16[64,1280]{1,0:T(8,128)(2,1)S(1)} %get-tuple-element.24), channel_id=1, source_target_pairs={{0,192},{64,0},{128,64},{192,128},{1,193},{65,1},{129,65},{193,129... | collective-permute-start | bytes 491528 | tf_op jit(solution)/shard_map/ppermute | solution.py:246
  25.9 5.4 %all-to-all-done = bf16[8,256,256]{2,1,0:T(8,128)(2,1)S(1)} async-done(((bf16[8,256,256]{2,1,0:T(8,128)(2,1)}), bf16[8,256,256]{2,1,0:T(8,128)(2,1)S(1)}, u32[]{:S(2)}, u32[]{:S(2)}) %all-to-all-start) | async-done | bytes 1048608 | tf_op jit(solution)/shard_map/all_to_all | solution.py:252
  31.4 0.1 reduce_sum.12.refs_0_
  31.5 3.1 %collective-permute-start.1 = (bf16[256,256]{1,0:T(8,128)(2,1)S(1)}, bf16[256,256]{1,0:T(8,128)(2,1)S(1)}, u32[]{:S(2)}, u32[]{:S(2)}) collective-permute-start(bf16[256,256]{1,0:T(8,128)(2,1)S(1)} %reduce_sum.12.refs_0_), channel_id=1, source_target_pairs={{0,16},{16,40},{40,56},{56,0},{8,24},{24,32},{32,48},{48,8},{1,17}... | collective-permute-start | bytes 393224 | tf_op jit(solution)/shard_map/ppermute | solution.py:256
  34.6 3.6 %collective-permute-start.2 = (bf16[256,256]{1,0:T(8,128)(2,1)S(1)}, bf16[256,256]{1,0:T(8,128)(2,1)S(1)}, u32[]{:S(2)}, u32[]{:S(2)}) collective-permute-start(bf16[256,256]{1,0:T(8,128)(2,1)S(1)} %reduce_sum.12.refs_0_), channel_id=1, source_target_pairs={{0,40},{16,56},{40,0},{56,16},{8,32},{24,48},{32,8},{48,24},{1,41}... | collective-permute-start | bytes 393224 | tf_op jit(solution)/shard_map/ppermute | solution.py:256
  38.2 0.0 collective-permute-done.4.refs_1_
  38.2 2.4 %collective-permute-start.3 = (bf16[256,256]{1,0:T(8,128)(2,1)S(1)}, bf16[256,256]{1,0:T(8,128)(2,1)S(1)}, u32[]{:S(2)}, u32[]{:S(2)}) collective-permute-start(bf16[256,256]{1,0:T(8,128)(2,1)S(1)} %reduce_sum.12.refs_0_), channel_id=1, source_target_pairs={{0,56},{16,0},{40,16},{56,40},{8,48},{24,8},{32,24},{48,32},{1,57}... | collective-permute-start | bytes 393224 | tf_op jit(solution)/shard_map/ppermute | solution.py:256
  40.5 0.0 collective-permute-done.5.refs_2_
  40.5 0.0 collective-permute-done.6.refs_3_
  40.5 1.6 %collective-permute-done.1.refs_1_ = bf16[256,256]{1,0:T(8,128)(2,1)S(1)} collective-permute-done((bf16[256,256]{1,0:T(8,128)(2,1)S(1)}, bf16[256,256]{1,0:T(8,128)(2,1)S(1)}, u32[]{:S(2)}, u32[]{:S(2)}) %collective-permute-start.1) | collective-permute-done | bytes 131104 | tf_op jit(solution)/shard_map/ppermute | solution.py:256
  42.1 6.0 %collective-permute-done.2.refs_2_ = bf16[256,256]{1,0:T(8,128)(2,1)S(1)} collective-permute-done((bf16[256,256]{1,0:T(8,128)(2,1)S(1)}, bf16[256,256]{1,0:T(8,128)(2,1)S(1)}, u32[]{:S(2)}, u32[]{:S(2)}) %collective-permute-start.2) | collective-permute-done | bytes 131104 | tf_op jit(solution)/shard_map/ppermute | solution.py:256
  48.2 0.2 collective-permute-done.3.refs_3_
  48.3 2.2 %orthogonalize.1 = bf16[8,256,256]{2,1,0:T(8,128)(2,1)S(1)} custom-call(bf16[256,256]{1,0:T(8,128)(2,1)S(1)} %reduce_sum.12.refs_0_, bf16[256,256]{1,0:T(8,128)(2,1)S(1)} %collective-permute-done.1.refs_1_, bf16[256,256]{1,0:T(8,128)(2,1)S(1)} %collective-permute-done.2.refs_2_, bf16[256,256]{1,0:T(8,128)(2,1)S(1)} %collective-permute-done.3.refs_3_), custom_call_target="tpu_custom_call" | custom-call | tf_op jit(solution)/shard_map/orthogonalize/pallas_call | solution.py:263
  50.5 0.0 copy-start
  50.6 17.7 %all_to_all.15.mine_ref = bf16[8,256,256]{2,1,0:T(8,128)(2,1)S(1)} all-to-all(bf16[8,256,256]{2,1,0:T(8,128)(2,1)S(1)} %orthogonalize.1), channel_id=1, replica_groups=mesh['head'=4,'z_hi'=4,'z_lo'=2,'y'=4,'core'=2] {'y','z_lo'}, dimensions={0} | all-to-all | bytes 2097152 | tf_op jit(solution)/shard_map/all_to_all | solution.py:269
  68.3 3.2 %collective-permute-start.7 = (bf16[8,256,256]{2,1,0:T(8,128)(2,1)S(1)}, bf16[8,256,256]{2,1,0:T(8,128)(2,1)S(1)}, u32[]{:S(2)}, u32[]{:S(2)}) collective-permute-start(bf16[8,256,256]{2,1,0:T(8,128)(2,1)S(1)} %all_to_all.15.mine_ref), channel_id=1, source_target_pairs={{0,1},{1,0},{2,3},{3,2},{4,5},{5,4},{6,7},{7,6},{8,9},{9,8},{10,11... | collective-permute-start | bytes 3145736 | tf_op jit(solution)/shard_map/ppermute | solution.py:270
  71.5 2.3 %collective-permute-done.7.other_ref = bf16[8,256,256]{2,1,0:T(8,128)(2,1)S(1)} collective-permute-done((bf16[8,256,256]{2,1,0:T(8,128)(2,1)S(1)}, bf16[8,256,256]{2,1,0:T(8,128)(2,1)S(1)}, u32[]{:S(2)}, u32[]{:S(2)}) %collective-permute-start.7) | collective-permute-done | bytes 1048608 | tf_op jit(solution)/shard_map/ppermute | solution.py:270
  73.8 0.0 copy-done.1
  73.8 0.0 copy-done
  73.8 3.8 %second.1 = bf16[256,1280]{1,0:T(8,128)(2,1)} custom-call(s32[1]{0:T(128)} %bitcast.1.core_ref, s32[1]{0:T(128)} %bitcast.2.far_ref, bf16[2,256,1280]{2,1,0:T(8,128)(2,1)S(1)} %copy-done.1, f32[5,256,256]{2,1,0:T(8,128)S(1)} %copy-done, f32[5,256,256]{2,1,0:T(8,128)} %u_ref.5, f32[5,256,256]{2,1,0:T(8,128)} %d_ref.5, ...), custom_call_target="tpu_custom_call" | custom-call | tf_op jit(solution)/shard_map/second/pallas_call | solution.py:274
  77.6 4.0 %all-to-all-start.2 = ((bf16[4,64,1280]{2,1,0:T(8,128)(2,1)}), bf16[4,64,1280]{2,1,0:T(8,128)(2,1)S(1)}, u32[]{:S(2)}, u32[]{:S(2)}) async-start(bf16[4,64,1280]{2,1,0:T(8,128)(2,1)} %bitcast.3), calls=%async_computation.2 | async-start | bytes 1310720 | tf_op jit(solution)/shard_map/all_to_all | solution.py:287
  81.6 1.4 %lay_first.1.buf_ref = bf16[2,64,5120]{2,1,0:T(8,128)(2,1)} custom-call(s32[1]{0:T(128)} %bitcast.place_ref, bf16[64,1280]{1,0:T(8,128)(2,1)S(1)} %get-tuple-element.25.refs_0_, bf16[64,1280]{1,0:T(8,128)(2,1)S(1)} %collective-permute-done.4.refs_1_, bf16[64,1280]{1,0:T(8,128)(2,1)S(1)} %collective-permute-done.5.refs_2_, ...), custom_call_target="tpu_custom_call" | custom-call | tf_op jit(solution)/shard_map/lay_first/pallas_call | solution.py:289
  83.1 8.9 %all-to-all-done.2.rows_ref = bf16[4,64,1280]{2,1,0:T(8,128)(2,1)S(1)} async-done(((bf16[4,64,1280]{2,1,0:T(8,128)(2,1)}), bf16[4,64,1280]{2,1,0:T(8,128)(2,1)S(1)}, u32[]{:S(2)}, u32[]{:S(2)}) %all-to-all-start.2) | async-done | bytes 655392 | tf_op jit(solution)/shard_map/all_to_all | solution.py:287
  92.0 1.4 %lay_second.1 = bf16[2,64,5120]{2,1,0:T(8,128)(2,1)} custom-call(bf16[2,64,5120]{2,1,0:T(8,128)(2,1)} %lay_first.1.buf_ref, bf16[4,64,1280]{2,1,0:T(8,128)(2,1)S(1)} %all-to-all-done.2.rows_ref), custom_call_target="tpu_custom_call", output_to_operand_aliasing={{}: (0, {})} | custom-call | tf_op jit(solution)/shard_map/lay_second/pallas_call | solution.py:301
  (1 shorter events, 0.0 us)
Async XLA Ops:
  5.5 5.6 %collective-permute-start = (bf16[8,256,256]{2,1,0:T(8,128)(2,1)S(1)}, bf16[8,256,256]{2,1,0:T(8,128)(2,1)S(1)}, u32[]{:S(2)}, u32[]{:S(2)}) collective-permute-start(bf16[8,256,256]{2,1,0:T(8,128)(2,1)S(1)} %get-tuple-element.20), channel_id=1, source_target_pairs={{0,1},{1,0},{2,3},{3,2},{4,5},{5,4},{6,7},{7,6},{8,9},{9,8},{10,11... | collective-permute-start | bytes 3145736 | tf_op jit(solution)/shard_map/ppermute | solution.py:229
  12.4 19.0 %all-to-all-start = ((bf16[8,256,256]{2,1,0:T(8,128)(2,1)}), bf16[8,256,256]{2,1,0:T(8,128)(2,1)S(1)}, u32[]{:S(2)}, u32[]{:S(2)}) async-start(bf16[8,256,256]{2,1,0:T(8,128)(2,1)} %add_convert_fusion), calls=%async_computation | async-start | bytes 2097152 | tf_op jit(solution)/shard_map/all_to_all | solution.py:252
  21.1 17.1 %collective-permute-start.4 = (bf16[64,1280]{1,0:T(8,128)(2,1)S(1)}, bf16[64,1280]{1,0:T(8,128)(2,1)S(1)}, u32[]{:S(2)}, u32[]{:S(2)}) collective-permute-start(bf16[64,1280]{1,0:T(8,128)(2,1)S(1)} %get-tuple-element.22), channel_id=1, source_target_pairs={{0,64},{64,128},{128,192},{192,0},{1,65},{65,129},{129,193},{193,1... | collective-permute-start | bytes 491528 | tf_op jit(solution)/shard_map/ppermute | solution.py:246
  22.3 18.2 %collective-permute-start.5 = (bf16[64,1280]{1,0:T(8,128)(2,1)S(1)}, bf16[64,1280]{1,0:T(8,128)(2,1)S(1)}, u32[]{:S(2)}, u32[]{:S(2)}) collective-permute-start(bf16[64,1280]{1,0:T(8,128)(2,1)S(1)} %get-tuple-element.23), channel_id=1, source_target_pairs={{0,128},{64,192},{128,0},{192,64},{1,129},{65,193},{129,1},{193,65... | collective-permute-start | bytes 491528 | tf_op jit(solution)/shard_map/ppermute | solution.py:246
  24.8 15.8 %collective-permute-start.6 = (bf16[64,1280]{1,0:T(8,128)(2,1)S(1)}, bf16[64,1280]{1,0:T(8,128)(2,1)S(1)}, u32[]{:S(2)}, u32[]{:S(2)}) collective-permute-start(bf16[64,1280]{1,0:T(8,128)(2,1)S(1)} %get-tuple-element.24), channel_id=1, source_target_pairs={{0,192},{64,0},{128,64},{192,128},{1,193},{65,1},{129,65},{193,129... | collective-permute-start | bytes 491528 | tf_op jit(solution)/shard_map/ppermute | solution.py:246
  31.5 10.6 %collective-permute-start.1 = (bf16[256,256]{1,0:T(8,128)(2,1)S(1)}, bf16[256,256]{1,0:T(8,128)(2,1)S(1)}, u32[]{:S(2)}, u32[]{:S(2)}) collective-permute-start(bf16[256,256]{1,0:T(8,128)(2,1)S(1)} %reduce_sum.12.refs_0_), channel_id=1, source_target_pairs={{0,16},{16,40},{40,56},{56,0},{8,24},{24,32},{32,48},{48,8},{1,17}... | collective-permute-start | bytes 393224 | tf_op jit(solution)/shard_map/ppermute | solution.py:256
  34.6 13.6 %collective-permute-start.2 = (bf16[256,256]{1,0:T(8,128)(2,1)S(1)}, bf16[256,256]{1,0:T(8,128)(2,1)S(1)}, u32[]{:S(2)}, u32[]{:S(2)}) collective-permute-start(bf16[256,256]{1,0:T(8,128)(2,1)S(1)} %reduce_sum.12.refs_0_), channel_id=1, source_target_pairs={{0,40},{16,56},{40,0},{56,16},{8,32},{24,48},{32,8},{48,24},{1,41}... | collective-permute-start | bytes 393224 | tf_op jit(solution)/shard_map/ppermute | solution.py:256
  38.2 10.2 %collective-permute-start.3 = (bf16[256,256]{1,0:T(8,128)(2,1)S(1)}, bf16[256,256]{1,0:T(8,128)(2,1)S(1)}, u32[]{:S(2)}, u32[]{:S(2)}) collective-permute-start(bf16[256,256]{1,0:T(8,128)(2,1)S(1)} %reduce_sum.12.refs_0_), channel_id=1, source_target_pairs={{0,56},{16,0},{40,16},{56,40},{8,48},{24,8},{32,24},{48,32},{1,57}... | collective-permute-start | bytes 393224 | tf_op jit(solution)/shard_map/ppermute | solution.py:256
  48.3 25.4 %copy-start.1 = (bf16[2,256,1280]{2,1,0:T(8,128)(2,1)S(1)}, bf16[2,256,1280]{2,1,0:T(8,128)(2,1)}, u32[]{:S(2)}) copy-start(bf16[2,256,1280]{2,1,0:T(8,128)(2,1)} %q_ref.3) | copy-start | bytes 3932164
  50.5 23.2 %copy-start = (f32[5,256,256]{2,1,0:T(8,128)S(1)}, f32[5,256,256]{2,1,0:T(8,128)}, u32[]{:S(2)}) copy-start(f32[5,256,256]{2,1,0:T(8,128)} %g_ref.5) | copy-start | bytes 3932164
  68.3 5.5 %collective-permute-start.7 = (bf16[8,256,256]{2,1,0:T(8,128)(2,1)S(1)}, bf16[8,256,256]{2,1,0:T(8,128)(2,1)S(1)}, u32[]{:S(2)}, u32[]{:S(2)}) collective-permute-start(bf16[8,256,256]{2,1,0:T(8,128)(2,1)S(1)} %all_to_all.15.mine_ref), channel_id=1, source_target_pairs={{0,1},{1,0},{2,3},{3,2},{4,5},{5,4},{6,7},{7,6},{8,9},{9,8},{10,11... | collective-permute-start | bytes 3145736 | tf_op jit(solution)/shard_map/ppermute | solution.py:270
  77.6 14.4 %all-to-all-start.2 = ((bf16[4,64,1280]{2,1,0:T(8,128)(2,1)}), bf16[4,64,1280]{2,1,0:T(8,128)(2,1)S(1)}, u32[]{:S(2)}, u32[]{:S(2)}) async-start(bf16[4,64,1280]{2,1,0:T(8,128)(2,1)} %bitcast.3), calls=%async_computation.2 | async-start | bytes 1310720 | tf_op jit(solution)/shard_map/all_to_all | solution.py:287

commit v8 on v7

--- a/solution.py
+++ b/solution.py
@@ -58,13 +58,13 @@
     return jnp.where(far_ref[0] >= N_FAR // 2, 1, 0)
 
 
-def grad_kernel(core_ref, far_ref, k_ref, v_ref, rate_ref, g_ref, u_ref, d_ref, keep_ref, send_ref, *scratch):
+def heads_of(heads, in_refs, scratch):
+    k_ref, v_ref, rate_ref, g_ref, u_ref, d_ref = in_refs
     rates, keys, values, gates, ups, downs, rate_sem, sems = scratch
-    twist = twist_of(far_ref)
     rate_copy = pltpu.make_async_copy(rate_ref, rates, rate_sem)
     rate_copy.start()
     copies = []
-    for head in range(HEADS_HERE):
+    for at, head in enumerate(heads):
         cols = pl.ds(head * HD, HD)
         pairs = (
             (k_ref.at[:, cols], keys),
@@ -73,36 +73,66 @@
             (u_ref.at[head], ups),
             (d_ref.at[head], downs),
         )
-        copies.append([pltpu.make_async_copy(src, dst.at[head], sems.at[head, i]) for i, (src, dst) in enumerate(pairs)])
+        copies.append([pltpu.make_async_copy(src, dst.at[at], sems.at[at, i]) for i, (src, dst) in enumerate(pairs)])
         for copy in copies[-1]:
             copy.start()
     rate_copy.wait()
-
-    def all_heads(group_refs):
-        for head in range(HEADS_HERE):
-            for copy in copies[head]:
-                copy.wait()
-            grads = head_grads(
-                keys[head],
-                values[head],
+    for at, head in enumerate(heads):
+        for copy in copies[at]:
+            copy.wait()
+        yield (
+            head,
+            head_grads(
+                keys[at],
+                values[at],
                 rates[head : head + 1, :],
-                gates[head].astype(BF16),
-                ups[head].astype(BF16),
-                downs[head].astype(BF16),
-            )
+                gates[at].astype(BF16),
+                ups[at].astype(BF16),
+                downs[at].astype(BF16),
+            ),
+        )
+
+
+def sent_kernel(core_ref, far_ref, *refs):
+    in_refs, (send_ref, shared_ref), scratch = refs[:6], refs[6:8], refs[8:]
+    twist = twist_of(far_ref)
+
+    def run(heads, send_from, keep_from):
+        for head, grads in heads_of(heads, in_refs, scratch):
             for mat, grad in enumerate(grads):
-                for group, ref in enumerate(group_refs):
-                    slot = head * 3 + mat - group * (GROUP - 1)
-                    if 0 <= slot < GROUP:
-                        ref[jnp.bitwise_xor(slot, twist)] = grad
+                at = head * 3 + mat
+                if 0 <= at - send_from < GROUP:
+                    send_ref[jnp.bitwise_xor(at - send_from, twist)] = grad
+                if 0 <= at - keep_from < 2:
+                    shared_ref[at - keep_from] = grad
 
     @pl.when(core_ref[0] == 0)
     def _():
-        all_heads((keep_ref, send_ref))
+        run((2, 3, 4), GROUP - 1, 6)
 
     @pl.when(core_ref[0] != 0)
     def _():
-        all_heads((send_ref, keep_ref))
+        run((0, 1, 2), 0, GROUP - 1)
+
+
+def kept_kernel(core_ref, far_ref, *refs):
+    in_refs, shared_ref, keep_ref, scratch = refs[:6], refs[6], refs[7], refs[8:]
+    twist = twist_of(far_ref)
+
+    def run(heads, keep_from, shared_from):
+        for i in range(2):
+            keep_ref[jnp.bitwise_xor(shared_from - keep_from + i, twist)] = shared_ref[i]
+        for head, grads in heads_of(heads, in_refs, scratch):
+            for mat, grad in enumerate(grads):
+                keep_ref[jnp.bitwise_xor(head * 3 + mat - keep_from, twist)] = grad
+
+    @pl.when(core_ref[0] == 0)
+    def _():
+        run((0, 1), 0, 6)
+
+    @pl.when(core_ref[0] != 0)
+    def _():
+        run((3, 4), GROUP - 1, GROUP - 1)
 
 
 def head_grads(keys, values, rate, gate, up, down):
@@ -202,31 +232,52 @@
         pltpu.with_memory_space_constraint(x, pltpu.HBM) for x in args
     ]
     any_spec = pl.BlockSpec(memory_space=pl.ANY)
-    keep, send = pl.pallas_call(
-        grad_kernel,
+    piece_array = jax.ShapeDtypeStruct(piece_shape, BF16)
+    shared_shape = (2, HD, HD)
+    shared_spec = pl.BlockSpec(shared_shape, lambda h, *_: (0, 0, 0))
+
+    def copy_scratch(heads):
+        return [
+            pltpu.VMEM((HEADS_HERE, rows), F32),
+            pltpu.VMEM((heads, rows, HD), BF16),
+            pltpu.VMEM((heads, rows, HD), BF16),
+            pltpu.VMEM((heads, HD, HD), F32),
+            pltpu.VMEM((heads, HD, HD), F32),
+            pltpu.VMEM((heads, HD, HD), F32),
+            pltpu.SemaphoreType.DMA(()),
+            pltpu.SemaphoreType.DMA((heads, 5)),
+        ]
+
+    grad_inputs = (k_hbm, v_hbm, rate_hbm, g_hbm, u_hbm, d_hbm)
+    send, shared = pl.pallas_call(
+        sent_kernel,
         grid_spec=pltpu.PrefetchScalarGridSpec(
             num_scalar_prefetch=2,
             grid=(1,),
             in_specs=[any_spec] * 6,
-            out_specs=[piece_spec, piece_spec],
-            scratch_shapes=[
-                pltpu.VMEM((HEADS_HERE, rows), F32),
-                pltpu.VMEM((HEADS_HERE, rows, HD), BF16),
-                pltpu.VMEM((HEADS_HERE, rows, HD), BF16),
-                pltpu.VMEM((HEADS_HERE, HD, HD), F32),
-                pltpu.VMEM((HEADS_HERE, HD, HD), F32),
-                pltpu.VMEM((HEADS_HERE, HD, HD), F32),
-                pltpu.SemaphoreType.DMA(()),
-                pltpu.SemaphoreType.DMA((HEADS_HERE, 5)),
-            ],
-        ),
-        out_shape=[jax.ShapeDtypeStruct(piece_shape, BF16), jax.ShapeDtypeStruct(piece_shape, BF16)],
-        compiler_params=params,
-        name="grads",
-    )(core, far, k_hbm, v_hbm, rate_hbm, g_hbm, u_hbm, d_hbm)
+            out_specs=[piece_spec, shared_spec],
+            scratch_shapes=copy_scratch(3),
+        ),
+        out_shape=[piece_array, jax.ShapeDtypeStruct(shared_shape, BF16)],
+        compiler_params=params,
+        name="grads_sent",
+    )(core, far, *grad_inputs)
 
     swap = [(0, 1), (1, 0)]
     received = lax.ppermute(send, "core", swap)
+    keep = pl.pallas_call(
+        kept_kernel,
+        grid_spec=pltpu.PrefetchScalarGridSpec(
+            num_scalar_prefetch=2,
+            grid=(1,),
+            in_specs=[any_spec] * 6 + [shared_spec],
+            out_specs=piece_spec,
+            scratch_shapes=copy_scratch(2),
+        ),
+        out_shape=piece_array,
+        compiler_params=params,
+        name="grads_kept",
+    )(core, far, *grad_inputs, shared)
     place = lax.axis_index("head").astype(jnp.int32).reshape(1)
     part_spec = pl.BlockSpec((part, HD), lambda h, p: (0, h))
     firsts = pl.pallas_call(

time: 93.7 us -> 92.5 us (0.987)
  waiting for transfers between devices: 26.7 us -> 25.1 us
    ppermute x1, waiting for transfers between devices: 2.29 us -> 0.01 us  [local(): received = lax.ppermute(send, 'core', swap)]
    pallas_call x1 -> x2, Pallas kernels: 5.48 us -> 6.15 us  [the longest x1 3.55 us: local(): pl.pallas_call(sent_kernel, grid_spec=pltpu.PrefetchScalarGridSpec(num_sc...]
  transfers between devices with their start and end apart: 10 -> 10, of which waited for: 7 -> 6; matrix products, arithmetic and copies ran while one was open for 0% -> 0% of each run, Pallas kernels for 7% -> 10%
where the time goes in v8:
time: 92.5 us; the launch traced here: 92.1 us
  starting transfers between devices  27.6 us (30%)
  waiting for transfers between devices  25.1 us (27%)
  Pallas kernels  19.8 us (21%)
  blocking collectives  18.1 us (20%)
  other arithmetic  1.41 us (2%)
    all_to_all x1, blocking collectives, local(): lax.all_to_all(orth, slots, split_axis=0, concat_axis=0, tiled=True)  18.1 us
    ppermute x3, starting transfers between devices, local(): lax.ppermute(partial, ('z_hi', 'z_lo'), [(ring[i], ring[(i + hop) % N_FAR...  9.01 us
    all_to_all x1, waiting for transfers between devices, local(): lax.all_to_all(second.reshape(n_head, part, width), 'head', split_axis=0,...  8.88 us
    ppermute x3, waiting for transfers between devices, local(): lax.ppermute(partial, ('z_hi', 'z_lo'), [(ring[i], ring[(i + hop) % N_FAR...  8.08 us
    all_to_all x1, waiting for transfers between devices, local(): lax.all_to_all(chip_sum, slots, split_axis=0, concat_axis=0, tiled=True)  5.8 us
    ppermute x3, starting transfers between devices, local(): lax.ppermute(firsts[hop], 'head', [(i, (i + hop) % n_head) for i in range...  4.9 us
    pallas_call x1, Pallas kernels, local(): pl.pallas_call(first_kernel, grid_spec=pltpu.PrefetchScalarGridSpec(num_s...  4.84 us
    all_to_all x1, starting transfers between devices, local(): lax.all_to_all(second.reshape(n_head, part, width), 'head', split_axis=0,...  4 us
  transfers between devices with their start and end apart: 10, of which 6 were waited for; matrix products, arithmetic and copies ran while one was open for 0% of the time, Pallas kernels for 10%

profile of v8, /device:TPU:1, one launch (start us, length us, event | category | flops | bytes accessed | tf_op | source)
XLA Modules:
  0.0 92.1 jit_solution(10125295138320931914)
XLA Ops:
  0.0 3.6 %grads_sent.1 = (bf16[8,256,256]{2,1,0:T(8,128)(2,1)S(1)}, bf16[2,256,256]{2,1,0:T(8,128)(2,1)S(1)}) custom-call(s32[1]{0:T(128)} %bitcast.1.core_ref, s32[1]{0:T(128)} %bitcast.2.far_ref, bf16[256,1280]{1,0:T(8,128)(2,1)} %refs_0_.3, bf16[256,1280]{1,0:T(8,128)(2,1)} %refs_1_.3, f32[5,256]{1,0:T(8,128)} %refs_2_.3, f32[5,256,256]{2,1,0:T(8,128)} %g_ref.3, ...), custom_call_target="tpu_custom_call" | custom-call | tf_op jit(solution)/shard_map/grads_sent/pallas_call | solution.py:252
  3.6 3.4 %collective-permute-start = (bf16[8,256,256]{2,1,0:T(8,128)(2,1)S(1)}, bf16[8,256,256]{2,1,0:T(8,128)(2,1)S(1)}, u32[]{:S(2)}, u32[]{:S(2)}) collective-permute-start(bf16[8,256,256]{2,1,0:T(8,128)(2,1)S(1)} %get-tuple-element.20), channel_id=1, source_target_pairs={{0,1},{1,0},{2,3},{3,2},{4,5},{5,4},{6,7},{7,6},{8,9},{9,8},{10,11... | collective-permute-start | bytes 3145736 | tf_op jit(solution)/shard_map/ppermute | solution.py:267
  6.9 2.6 %grads_kept.1 = bf16[8,256,256]{2,1,0:T(8,128)(2,1)S(1)} custom-call(s32[1]{0:T(128)} %bitcast.1.core_ref, s32[1]{0:T(128)} %bitcast.2.far_ref, bf16[256,1280]{1,0:T(8,128)(2,1)} %refs_0_.3, bf16[256,1280]{1,0:T(8,128)(2,1)} %refs_1_.3, f32[5,256]{1,0:T(8,128)} %refs_2_.3, f32[5,256,256]{2,1,0:T(8,128)} %g_ref.3, f32[5,256,256]{2,1,0:T(8,128)} %u_ref.3, ...), custom_call_target="tpu_custom_call" | custom-call | tf_op jit(solution)/shard_map/grads_kept/pallas_call | solution.py:268
  9.5 0.0 collective-permute-done
  9.5 1.3 %add_convert_fusion = bf16[8,256,256]{2,1,0:T(8,128)(2,1)} fusion(bf16[8,256,256]{2,1,0:T(8,128)(2,1)S(1)} %collective-permute-done, bf16[8,256,256]{2,1,0:T(8,128)(2,1)S(1)} %grads_kept.1), kind=kLoop, calls=%fused_computation | loop fusion | flops 2097152 | bytes 3145728 | tf_op jit(solution)/shard_map/convert_element_type | solution.py:301
  10.8 3.8 %all-to-all-start = ((bf16[8,256,256]{2,1,0:T(8,128)(2,1)}), bf16[8,256,256]{2,1,0:T(8,128)(2,1)S(1)}, u32[]{:S(2)}, u32[]{:S(2)}) async-start(bf16[8,256,256]{2,1,0:T(8,128)(2,1)} %add_convert_fusion), calls=%async_computation | async-start | bytes 2097152 | tf_op jit(solution)/shard_map/all_to_all | solution.py:303
  14.6 4.8 %first.1 = (bf16[64,1280]{1,0:T(8,128)(2,1)S(1)}, bf16[64,1280]{1,0:T(8,128)(2,1)S(1)}, bf16[64,1280]{1,0:T(8,128)(2,1)S(1)}, bf16[64,1280]{1,0:T(8,128)(2,1)S(1)}) custom-call(s32[1]{0:T(128)} %bitcast.place_ref, bf16[2,256,1280]{2,1,0:T(8,128)(2,1)} %q_ref.3, f32[5,256,256]{2,1,0:T(8,128)} %g_ref.3, f32[5,256,256]{2,1,0:T(8,128)} %u_ref.3, ...), custom_call_target="tpu_custom_call" | custom-call | tf_op jit(solution)/shard_map/first/pallas_call | solution.py:283
  19.5 1.3 %collective-permute-start.4 = (bf16[64,1280]{1,0:T(8,128)(2,1)S(1)}, bf16[64,1280]{1,0:T(8,128)(2,1)S(1)}, u32[]{:S(2)}, u32[]{:S(2)}) collective-permute-start(bf16[64,1280]{1,0:T(8,128)(2,1)S(1)} %get-tuple-element.22), channel_id=1, source_target_pairs={{0,64},{64,128},{128,192},{192,0},{1,65},{65,129},{129,193},{193,1... | collective-permute-start | bytes 491528 | tf_op jit(solution)/shard_map/ppermute | solution.py:297
  20.8 2.5 %collective-permute-start.5 = (bf16[64,1280]{1,0:T(8,128)(2,1)S(1)}, bf16[64,1280]{1,0:T(8,128)(2,1)S(1)}, u32[]{:S(2)}, u32[]{:S(2)}) collective-permute-start(bf16[64,1280]{1,0:T(8,128)(2,1)S(1)} %get-tuple-element.23), channel_id=1, source_target_pairs={{0,128},{64,192},{128,0},{192,64},{1,129},{65,193},{129,1},{193,65... | collective-permute-start | bytes 491528 | tf_op jit(solution)/shard_map/ppermute | solution.py:297
  23.2 1.1 %collective-permute-start.6 = (bf16[64,1280]{1,0:T(8,128)(2,1)S(1)}, bf16[64,1280]{1,0:T(8,128)(2,1)S(1)}, u32[]{:S(2)}, u32[]{:S(2)}) collective-permute-start(bf16[64,1280]{1,0:T(8,128)(2,1)S(1)} %get-tuple-element.24), channel_id=1, source_target_pairs={{0,192},{64,0},{128,64},{192,128},{1,193},{65,1},{129,65},{193,129... | collective-permute-start | bytes 491528 | tf_op jit(solution)/shard_map/ppermute | solution.py:297
  24.4 5.8 %all-to-all-done = bf16[8,256,256]{2,1,0:T(8,128)(2,1)S(1)} async-done(((bf16[8,256,256]{2,1,0:T(8,128)(2,1)}), bf16[8,256,256]{2,1,0:T(8,128)(2,1)S(1)}, u32[]{:S(2)}, u32[]{:S(2)}) %all-to-all-start) | async-done | bytes 1048608 | tf_op jit(solution)/shard_map/all_to_all | solution.py:303
  30.2 0.1 reduce_sum.12.refs_0_
  30.3 3.1 %collective-permute-start.1 = (bf16[256,256]{1,0:T(8,128)(2,1)S(1)}, bf16[256,256]{1,0:T(8,128)(2,1)S(1)}, u32[]{:S(2)}, u32[]{:S(2)}) collective-permute-start(bf16[256,256]{1,0:T(8,128)(2,1)S(1)} %reduce_sum.12.refs_0_), channel_id=1, source_target_pairs={{0,16},{16,40},{40,56},{56,0},{8,24},{24,32},{32,48},{48,8},{1,17}... | collective-permute-start | bytes 393224 | tf_op jit(solution)/shard_map/ppermute | solution.py:307
  33.4 3.5 %collective-permute-start.2 = (bf16[256,256]{1,0:T(8,128)(2,1)S(1)}, bf16[256,256]{1,0:T(8,128)(2,1)S(1)}, u32[]{:S(2)}, u32[]{:S(2)}) collective-permute-start(bf16[256,256]{1,0:T(8,128)(2,1)S(1)} %reduce_sum.12.refs_0_), channel_id=1, source_target_pairs={{0,40},{16,56},{40,0},{56,16},{8,32},{24,48},{32,8},{48,24},{1,41}... | collective-permute-start | bytes 393224 | tf_op jit(solution)/shard_map/ppermute | solution.py:307
  37.0 0.0 collective-permute-done.4.refs_1_
  37.0 2.4 %collective-permute-start.3 = (bf16[256,256]{1,0:T(8,128)(2,1)S(1)}, bf16[256,256]{1,0:T(8,128)(2,1)S(1)}, u32[]{:S(2)}, u32[]{:S(2)}) collective-permute-start(bf16[256,256]{1,0:T(8,128)(2,1)S(1)} %reduce_sum.12.refs_0_), channel_id=1, source_target_pairs={{0,56},{16,0},{40,16},{56,40},{8,48},{24,8},{32,24},{48,32},{1,57}... | collective-permute-start | bytes 393224 | tf_op jit(solution)/shard_map/ppermute | solution.py:307
  39.3 0.0 collective-permute-done.5.refs_2_
  39.3 0.0 collective-permute-done.6.refs_3_
  39.3 1.6 %collective-permute-done.1.refs_1_ = bf16[256,256]{1,0:T(8,128)(2,1)S(1)} collective-permute-done((bf16[256,256]{1,0:T(8,128)(2,1)S(1)}, bf16[256,256]{1,0:T(8,128)(2,1)S(1)}, u32[]{:S(2)}, u32[]{:S(2)}) %collective-permute-start.1) | collective-permute-done | bytes 131104 | tf_op jit(solution)/shard_map/ppermute | solution.py:307
  40.9 5.7 %collective-permute-done.2.refs_2_ = bf16[256,256]{1,0:T(8,128)(2,1)S(1)} collective-permute-done((bf16[256,256]{1,0:T(8,128)(2,1)S(1)}, bf16[256,256]{1,0:T(8,128)(2,1)S(1)}, u32[]{:S(2)}, u32[]{:S(2)}) %collective-permute-start.2) | collective-permute-done | bytes 131104 | tf_op jit(solution)/shard_map/ppermute | solution.py:307
  46.7 0.7 collective-permute-done.3.refs_3_
  47.4 2.2 %orthogonalize.1 = bf16[8,256,256]{2,1,0:T(8,128)(2,1)S(1)} custom-call(bf16[256,256]{1,0:T(8,128)(2,1)S(1)} %reduce_sum.12.refs_0_, bf16[256,256]{1,0:T(8,128)(2,1)S(1)} %collective-permute-done.1.refs_1_, bf16[256,256]{1,0:T(8,128)(2,1)S(1)} %collective-permute-done.2.refs_2_, bf16[256,256]{1,0:T(8,128)(2,1)S(1)} %collective-permute-done.3.refs_3_), custom_call_target="tpu_custom_call" | custom-call | tf_op jit(solution)/shard_map/orthogonalize/pallas_call | solution.py:314
  49.6 0.0 copy-start
  49.6 18.1 %all_to_all.15.mine_ref = bf16[8,256,256]{2,1,0:T(8,128)(2,1)S(1)} all-to-all(bf16[8,256,256]{2,1,0:T(8,128)(2,1)S(1)} %orthogonalize.1), channel_id=1, replica_groups=mesh['head'=4,'z_hi'=4,'z_lo'=2,'y'=4,'core'=2] {'y','z_lo'}, dimensions={0} | all-to-all | bytes 2097152 | tf_op jit(solution)/shard_map/all_to_all | solution.py:320
  67.7 2.5 %collective-permute-start.7 = (bf16[8,256,256]{2,1,0:T(8,128)(2,1)S(1)}, bf16[8,256,256]{2,1,0:T(8,128)(2,1)S(1)}, u32[]{:S(2)}, u32[]{:S(2)}) collective-permute-start(bf16[8,256,256]{2,1,0:T(8,128)(2,1)S(1)} %all_to_all.15.mine_ref), channel_id=1, source_target_pairs={{0,1},{1,0},{2,3},{3,2},{4,5},{5,4},{6,7},{7,6},{8,9},{9,8},{10,11... | collective-permute-start | bytes 3145736 | tf_op jit(solution)/shard_map/ppermute | solution.py:321
  70.2 2.3 %collective-permute-done.7.other_ref = bf16[8,256,256]{2,1,0:T(8,128)(2,1)S(1)} collective-permute-done((bf16[8,256,256]{2,1,0:T(8,128)(2,1)S(1)}, bf16[8,256,256]{2,1,0:T(8,128)(2,1)S(1)}, u32[]{:S(2)}, u32[]{:S(2)}) %collective-permute-start.7) | collective-permute-done | bytes 1048608 | tf_op jit(solution)/shard_map/ppermute | solution.py:321
  72.5 0.0 copy-done.1
  72.5 3.8 %second.1 = bf16[256,1280]{1,0:T(8,128)(2,1)} custom-call(s32[1]{0:T(128)} %bitcast.1.core_ref, s32[1]{0:T(128)} %bitcast.2.far_ref, bf16[2,256,1280]{2,1,0:T(8,128)(2,1)S(1)} %copy-done.1, f32[5,256,256]{2,1,0:T(8,128)S(1)} %copy-done, f32[5,256,256]{2,1,0:T(8,128)} %u_ref.3, f32[5,256,256]{2,1,0:T(8,128)} %d_ref.3, ...), custom_call_target="tpu_custom_call" | custom-call | tf_op jit(solution)/shard_map/second/pallas_call | solution.py:325
  76.3 4.0 %all-to-all-start.2 = ((bf16[4,64,1280]{2,1,0:T(8,128)(2,1)}), bf16[4,64,1280]{2,1,0:T(8,128)(2,1)S(1)}, u32[]{:S(2)}, u32[]{:S(2)}) async-start(bf16[4,64,1280]{2,1,0:T(8,128)(2,1)} %bitcast.3), calls=%async_computation.2 | async-start | bytes 1310720 | tf_op jit(solution)/shard_map/all_to_all | solution.py:338
  80.3 1.4 %lay_first.1.buf_ref = bf16[2,64,5120]{2,1,0:T(8,128)(2,1)} custom-call(s32[1]{0:T(128)} %bitcast.place_ref, bf16[64,1280]{1,0:T(8,128)(2,1)S(1)} %get-tuple-element.25.refs_0_, bf16[64,1280]{1,0:T(8,128)(2,1)S(1)} %collective-permute-done.4.refs_1_, bf16[64,1280]{1,0:T(8,128)(2,1)S(1)} %collective-permute-done.5.refs_2_, ...), custom_call_target="tpu_custom_call" | custom-call | tf_op jit(solution)/shard_map/lay_first/pallas_call | solution.py:340
  81.8 8.9 %all-to-all-done.2.rows_ref = bf16[4,64,1280]{2,1,0:T(8,128)(2,1)S(1)} async-done(((bf16[4,64,1280]{2,1,0:T(8,128)(2,1)}), bf16[4,64,1280]{2,1,0:T(8,128)(2,1)S(1)}, u32[]{:S(2)}, u32[]{:S(2)}) %all-to-all-start.2) | async-done | bytes 655392 | tf_op jit(solution)/shard_map/all_to_all | solution.py:338
  90.7 1.4 %lay_second.1 = bf16[2,64,5120]{2,1,0:T(8,128)(2,1)} custom-call(bf16[2,64,5120]{2,1,0:T(8,128)(2,1)} %lay_first.1.buf_ref, bf16[4,64,1280]{2,1,0:T(8,128)(2,1)S(1)} %all-to-all-done.2.rows_ref), custom_call_target="tpu_custom_call", output_to_operand_aliasing={{}: (0, {})} | custom-call | tf_op jit(solution)/shard_map/lay_second/pallas_call | solution.py:352
  (2 shorter events, 0.0 us)
Async XLA Ops:
  3.6 6.0 %collective-permute-start = (bf16[8,256,256]{2,1,0:T(8,128)(2,1)S(1)}, bf16[8,256,256]{2,1,0:T(8,128)(2,1)S(1)}, u32[]{:S(2)}, u32[]{:S(2)}) collective-permute-start(bf16[8,256,256]{2,1,0:T(8,128)(2,1)S(1)} %get-tuple-element.20), channel_id=1, source_target_pairs={{0,1},{1,0},{2,3},{3,2},{4,5},{5,4},{6,7},{7,6},{8,9},{9,8},{10,11... | collective-permute-start | bytes 3145736 | tf_op jit(solution)/shard_map/ppermute | solution.py:267
  10.8 19.4 %all-to-all-start = ((bf16[8,256,256]{2,1,0:T(8,128)(2,1)}), bf16[8,256,256]{2,1,0:T(8,128)(2,1)S(1)}, u32[]{:S(2)}, u32[]{:S(2)}) async-start(bf16[8,256,256]{2,1,0:T(8,128)(2,1)} %add_convert_fusion), calls=%async_computation | async-start | bytes 2097152 | tf_op jit(solution)/shard_map/all_to_all | solution.py:303
  19.5 17.5 %collective-permute-start.4 = (bf16[64,1280]{1,0:T(8,128)(2,1)S(1)}, bf16[64,1280]{1,0:T(8,128)(2,1)S(1)}, u32[]{:S(2)}, u32[]{:S(2)}) collective-permute-start(bf16[64,1280]{1,0:T(8,128)(2,1)S(1)} %get-tuple-element.22), channel_id=1, source_target_pairs={{0,64},{64,128},{128,192},{192,0},{1,65},{65,129},{129,193},{193,1... | collective-permute-start | bytes 491528 | tf_op jit(solution)/shard_map/ppermute | solution.py:297
  20.8 18.6 %collective-permute-start.5 = (bf16[64,1280]{1,0:T(8,128)(2,1)S(1)}, bf16[64,1280]{1,0:T(8,128)(2,1)S(1)}, u32[]{:S(2)}, u32[]{:S(2)}) collective-permute-start(bf16[64,1280]{1,0:T(8,128)(2,1)S(1)} %get-tuple-element.23), channel_id=1, source_target_pairs={{0,128},{64,192},{128,0},{192,64},{1,129},{65,193},{129,1},{193,65... | collective-permute-start | bytes 491528 | tf_op jit(solution)/shard_map/ppermute | solution.py:297
  23.2 16.1 %collective-permute-start.6 = (bf16[64,1280]{1,0:T(8,128)(2,1)S(1)}, bf16[64,1280]{1,0:T(8,128)(2,1)S(1)}, u32[]{:S(2)}, u32[]{:S(2)}) collective-permute-start(bf16[64,1280]{1,0:T(8,128)(2,1)S(1)} %get-tuple-element.24), channel_id=1, source_target_pairs={{0,192},{64,0},{128,64},{192,128},{1,193},{65,1},{129,65},{193,129... | collective-permute-start | bytes 491528 | tf_op jit(solution)/shard_map/ppermute | solution.py:297
  30.3 10.6 %collective-permute-start.1 = (bf16[256,256]{1,0:T(8,128)(2,1)S(1)}, bf16[256,256]{1,0:T(8,128)(2,1)S(1)}, u32[]{:S(2)}, u32[]{:S(2)}) collective-permute-start(bf16[256,256]{1,0:T(8,128)(2,1)S(1)} %reduce_sum.12.refs_0_), channel_id=1, source_target_pairs={{0,16},{16,40},{40,56},{56,0},{8,24},{24,32},{32,48},{48,8},{1,17}... | collective-permute-start | bytes 393224 | tf_op jit(solution)/shard_map/ppermute | solution.py:307
  33.4 13.3 %collective-permute-start.2 = (bf16[256,256]{1,0:T(8,128)(2,1)S(1)}, bf16[256,256]{1,0:T(8,128)(2,1)S(1)}, u32[]{:S(2)}, u32[]{:S(2)}) collective-permute-start(bf16[256,256]{1,0:T(8,128)(2,1)S(1)} %reduce_sum.12.refs_0_), channel_id=1, source_target_pairs={{0,40},{16,56},{40,0},{56,16},{8,32},{24,48},{32,8},{48,24},{1,41}... | collective-permute-start | bytes 393224 | tf_op jit(solution)/shard_map/ppermute | solution.py:307
  37.0 10.5 %collective-permute-start.3 = (bf16[256,256]{1,0:T(8,128)(2,1)S(1)}, bf16[256,256]{1,0:T(8,128)(2,1)S(1)}, u32[]{:S(2)}, u32[]{:S(2)}) collective-permute-start(bf16[256,256]{1,0:T(8,128)(2,1)S(1)} %reduce_sum.12.refs_0_), channel_id=1, source_target_pairs={{0,56},{16,0},{40,16},{56,40},{8,48},{24,8},{32,24},{48,32},{1,57}... | collective-permute-start | bytes 393224 | tf_op jit(solution)/shard_map/ppermute | solution.py:307
  47.4 25.1 %copy-start.1 = (bf16[2,256,1280]{2,1,0:T(8,128)(2,1)S(1)}, bf16[2,256,1280]{2,1,0:T(8,128)(2,1)}, u32[]{:S(2)}) copy-start(bf16[2,256,1280]{2,1,0:T(8,128)(2,1)} %q_ref.3) | copy-start | bytes 3932164
  49.6 22.9 %copy-start = (f32[5,256,256]{2,1,0:T(8,128)S(1)}, f32[5,256,256]{2,1,0:T(8,128)}, u32[]{:S(2)}) copy-start(f32[5,256,256]{2,1,0:T(8,128)} %g_ref.3) | copy-start | bytes 3932164
  67.7 4.8 %collective-permute-start.7 = (bf16[8,256,256]{2,1,0:T(8,128)(2,1)S(1)}, bf16[8,256,256]{2,1,0:T(8,128)(2,1)S(1)}, u32[]{:S(2)}, u32[]{:S(2)}) collective-permute-start(bf16[8,256,256]{2,1,0:T(8,128)(2,1)S(1)} %all_to_all.15.mine_ref), channel_id=1, source_target_pairs={{0,1},{1,0},{2,3},{3,2},{4,5},{5,4},{6,7},{7,6},{8,9},{9,8},{10,11... | collective-permute-start | bytes 3145736 | tf_op jit(solution)/shard_map/ppermute | solution.py:321
  76.3 14.3 %all-to-all-start.2 = ((bf16[4,64,1280]{2,1,0:T(8,128)(2,1)}), bf16[4,64,1280]{2,1,0:T(8,128)(2,1)S(1)}, u32[]{:S(2)}, u32[]{:S(2)}) async-start(bf16[4,64,1280]{2,1,0:T(8,128)(2,1)} %bitcast.3), calls=%async_computation.2 | async-start | bytes 1310720 | tf_op jit(solution)/shard_map/all_to_all | solution.py:338

commit v9 on v8

--- a/solution.py
+++ b/solution.py
@@ -185,20 +185,63 @@
     return (fast - orth.astype(F32)).astype(BF16)
 
 
-def second_kernel(core_ref, far_ref, q_ref, g_ref, u_ref, d_ref, mine_ref, other_ref, out_ref):
-    low_core = core_ref[0] == 0
+def own_second_kernel(core_ref, far_ref, q_ref, g_ref, u_ref, d_ref, mine_ref, out_ref, *refs):
+    g_rest, u_rest, d_rest, u_own, d_own, sems = refs
     twist = twist_of(far_ref)
-    for head in range(HEADS_HERE):
-        nexts = []
-        for mat, ref in enumerate((g_ref, u_ref, d_ref)):
-            at = head * 3 + mat
-            in_low = at < GROUP
-            index = jnp.bitwise_xor(at if in_low else at - (GROUP - 1), twist)
-            pair = (mine_ref[index], other_ref[index])
-            orth = jnp.where(low_core, *(pair if in_low else pair[::-1]))
-            nexts.append(next_weight(ref[head], orth))
-        cols = slice(head * HD, (head + 1) * HD)
-        out_ref[:, cols] = apply_fast(q_ref[0, :, cols], *nexts)
+
+    def run(own_from, rest_from, base):
+        pairs = [(ref.at[pl.ds(own_from, 2)], own) for ref, own in ((u_ref, u_own), (d_ref, d_own))]
+        pairs += [(ref.at[pl.ds(rest_from, 3)], rest) for ref, rest in ((g_ref, g_rest), (u_ref, u_rest), (d_ref, d_rest))]
+        copies = [pltpu.make_async_copy(src, dst, sems.at[i]) for i, (src, dst) in enumerate(pairs)]
+        for copy in copies:
+            copy.start()
+        for copy in copies[:2]:
+            copy.wait()
+        for i in range(2):
+            head = own_from + i
+            fasts = (g_ref[head], u_own[i], d_own[i])
+            nexts = [
+                next_weight(fast, mine_ref[jnp.bitwise_xor(head * 3 + mat - base, twist)])
+                for mat, fast in enumerate(fasts)
+            ]
+            out_ref[:, i * HD : (i + 1) * HD] = apply_fast(q_ref[0, :, head * HD : (head + 1) * HD], *nexts)
+        for copy in copies[2:]:
+            copy.wait()
+
+    @pl.when(core_ref[0] == 0)
+    def _():
+        run(0, 2, 0)
+
+    @pl.when(core_ref[0] != 0)
+    def _():
+        run(3, 0, GROUP - 1)
+
+
+def rest_second_kernel(core_ref, far_ref, q_ref, g_rest, u_rest, d_rest, mine_ref, other_ref, own_ref, out_ref):
+    twist = twist_of(far_ref)
+
+    def run(own_from, rest_from, base, other_base):
+        out_ref[:, own_from * HD : (own_from + 2) * HD] = own_ref[...]
+        for i in range(3):
+            head = rest_from + i
+            nexts = []
+            for mat, fast in enumerate((g_rest[i], u_rest[i], d_rest[i])):
+                at = head * 3 + mat
+                if 0 <= at - base < GROUP:
+                    orth = mine_ref[jnp.bitwise_xor(at - base, twist)]
+                else:
+                    orth = other_ref[jnp.bitwise_xor(at - other_base, twist)]
+                nexts.append(next_weight(fast, orth))
+            cols = slice(head * HD, (head + 1) * HD)
+            out_ref[:, cols] = apply_fast(q_ref[0, :, cols], *nexts)
+
+    @pl.when(core_ref[0] == 0)
+    def _():
+        run(0, 2, 0, GROUP - 1)
+
+    @pl.when(core_ref[0] != 0)
+    def _():
+        run(3, 0, GROUP - 1, 0)
 
 
 def lay_first_kernel(place_ref, *refs):
@@ -322,18 +365,39 @@
 
     group_spec = pl.BlockSpec((GROUP, HD, HD), lambda i, *_: (0, 0, 0))
     fast_spec = pl.BlockSpec((HEADS_HERE, HD, HD), lambda i, *_: (0, 0, 0))
-    second = pl.pallas_call(
-        second_kernel,
+    query_spec = pl.BlockSpec((1, rows, width), lambda i, *_: (1, 0, 0))
+    own_spec = pl.BlockSpec((rows, 2 * HD), lambda i, *_: (0, 0))
+    rest_spec = pl.BlockSpec((3, HD, HD), lambda i, *_: (0, 0, 0))
+    rest_array = jax.ShapeDtypeStruct((3, HD, HD), F32)
+    own, *rest = pl.pallas_call(
+        own_second_kernel,
         grid_spec=pltpu.PrefetchScalarGridSpec(
             num_scalar_prefetch=2,
             grid=(1,),
-            in_specs=[pl.BlockSpec((1, rows, width), lambda i, *_: (1, 0, 0))] + [fast_spec] * 3 + [group_spec] * 2,
+            in_specs=[query_spec, fast_spec, any_spec, any_spec, group_spec],
+            out_specs=[own_spec, rest_spec, rest_spec, rest_spec],
+            scratch_shapes=[
+                pltpu.VMEM((2, HD, HD), F32),
+                pltpu.VMEM((2, HD, HD), F32),
+                pltpu.SemaphoreType.DMA((5,)),
+            ],
+        ),
+        out_shape=[jax.ShapeDtypeStruct((rows, 2 * HD), BF16), rest_array, rest_array, rest_array],
+        compiler_params=params,
+        name="second_own",
+    )(core, far, queries, gate_fast, u_hbm, d_hbm, orth_mine)
+    second = pl.pallas_call(
+        rest_second_kernel,
+        grid_spec=pltpu.PrefetchScalarGridSpec(
+            num_scalar_prefetch=2,
+            grid=(1,),
+            in_specs=[query_spec, rest_spec, rest_spec, rest_spec, group_spec, group_spec, own_spec],
             out_specs=pl.BlockSpec((rows, width), lambda i, *_: (0, 0)),
         ),
         out_shape=rows_shape,
         compiler_params=params,
-        name="second",
-    )(core, far, queries, gate_fast, up_fast, down_fast, orth_mine, orth_other)
+        name="second_rest",
+    )(core, far, queries, *rest, orth_mine, orth_other, own)
 
     swapped = lax.all_to_all(second.reshape(n_head, part, width), "head", split_axis=0, concat_axis=0, tiled=True)
     out_shape = jax.ShapeDtypeStruct((2, part, n_head * width), BF16)

time: 92.5 us -> 92.8 us (level)
  Pallas kernels: 19.8 us -> 21.9 us
  waiting for transfers between devices: 25.1 us -> 23.2 us
    ppermute x1, waiting for transfers between devices: 2.29 us -> 0.01 us  [local(): orth_other = lax.ppermute(orth_mine, 'core', swap)]
    pallas_call x1 -> x2, Pallas kernels: 3.81 us -> 5.92 us  [the longest x1 3.17 us: local(): pl.pallas_call(own_second_kernel, grid_spec=pltpu.PrefetchScalarGridSpec(...]
  transfers between devices with their start and end apart: 10 -> 10, of which waited for: 6 -> 5; matrix products, arithmetic and copies ran while one was open for 0% -> 0% of each run, Pallas kernels for 10% -> 13%
where the time goes in v9:
time: 92.8 us; the launch traced here: 92.3 us
  starting transfers between devices  27.6 us (30%)
  waiting for transfers between devices  23.2 us (25%)
  Pallas kernels  21.9 us (24%)
  blocking collectives  18.1 us (20%)
  other arithmetic  1.41 us (2%)
    all_to_all x1, blocking collectives, local(): lax.all_to_all(orth, slots, split_axis=0, concat_axis=0, tiled=True)  18.1 us
    all_to_all x1, waiting for transfers between devices, local(): lax.all_to_all(second.reshape(n_head, part, width), 'head', split_axis=0,...  9.3 us
    ppermute x3, starting transfers between devices, local(): lax.ppermute(partial, ('z_hi', 'z_lo'), [(ring[i], ring[(i + hop) % N_FAR...  9.01 us
    ppermute x3, waiting for transfers between devices, local(): lax.ppermute(partial, ('z_hi', 'z_lo'), [(ring[i], ring[(i + hop) % N_FAR...  8.03 us
    all_to_all x1, waiting for transfers between devices, local(): lax.all_to_all(chip_sum, slots, split_axis=0, concat_axis=0, tiled=True)  5.81 us
    ppermute x3, starting transfers between devices, local(): lax.ppermute(firsts[hop], 'head', [(i, (i + hop) % n_head) for i in range...  4.89 us
    pallas_call x1, Pallas kernels, local(): pl.pallas_call(first_kernel, grid_spec=pltpu.PrefetchScalarGridSpec(num_s...  4.84 us
    all_to_all x1, starting transfers between devices, local(): lax.all_to_all(second.reshape(n_head, part, width), 'head', split_axis=0,...  4.01 us
  transfers between devices with their start and end apart: 10, of which 5 were waited for; matrix products, arithmetic and copies ran while one was open for 0% of the time, Pallas kernels for 13%

profile of v9, /device:TPU:1, one launch (start us, length us, event | category | flops | bytes accessed | tf_op | source)
XLA Modules:
  0.0 92.3 jit_solution(6805130648588131140)
XLA Ops:
  0.0 3.6 %grads_sent.1 = (bf16[8,256,256]{2,1,0:T(8,128)(2,1)S(1)}, bf16[2,256,256]{2,1,0:T(8,128)(2,1)S(1)}) custom-call(s32[1]{0:T(128)} %bitcast.1.core_ref, s32[1]{0:T(128)} %bitcast.2.far_ref, bf16[256,1280]{1,0:T(8,128)(2,1)} %refs_0_.3, bf16[256,1280]{1,0:T(8,128)(2,1)} %refs_1_.3, f32[5,256]{1,0:T(8,128)} %refs_2_.3, f32[5,256,256]{2,1,0:T(8,128)} %g_ref.3, ...), custom_call_target="tpu_custom_call" | custom-call | tf_op jit(solution)/shard_map/grads_sent/pallas_call | solution.py:295
  3.6 3.4 %collective-permute-start = (bf16[8,256,256]{2,1,0:T(8,128)(2,1)S(1)}, bf16[8,256,256]{2,1,0:T(8,128)(2,1)S(1)}, u32[]{:S(2)}, u32[]{:S(2)}) collective-permute-start(bf16[8,256,256]{2,1,0:T(8,128)(2,1)S(1)} %get-tuple-element.24), channel_id=1, source_target_pairs={{0,1},{1,0},{2,3},{3,2},{4,5},{5,4},{6,7},{7,6},{8,9},{9,8},{10,11... | collective-permute-start | bytes 3145736 | tf_op jit(solution)/shard_map/ppermute | solution.py:310
  6.9 2.6 %grads_kept.1 = bf16[8,256,256]{2,1,0:T(8,128)(2,1)S(1)} custom-call(s32[1]{0:T(128)} %bitcast.1.core_ref, s32[1]{0:T(128)} %bitcast.2.far_ref, bf16[256,1280]{1,0:T(8,128)(2,1)} %refs_0_.3, bf16[256,1280]{1,0:T(8,128)(2,1)} %refs_1_.3, f32[5,256]{1,0:T(8,128)} %refs_2_.3, f32[5,256,256]{2,1,0:T(8,128)} %g_ref.3, f32[5,256,256]{2,1,0:T(8,128)} %u_ref.3, ...), custom_call_target="tpu_custom_call" | custom-call | tf_op jit(solution)/shard_map/grads_kept/pallas_call | solution.py:311
  9.5 0.0 collective-permute-done
  9.5 1.3 %add_convert_fusion = bf16[8,256,256]{2,1,0:T(8,128)(2,1)} fusion(bf16[8,256,256]{2,1,0:T(8,128)(2,1)S(1)} %collective-permute-done, bf16[8,256,256]{2,1,0:T(8,128)(2,1)S(1)} %grads_kept.1), kind=kLoop, calls=%fused_computation | loop fusion | flops 2097152 | bytes 3145728 | tf_op jit(solution)/shard_map/convert_element_type | solution.py:344
  10.8 3.8 %all-to-all-start = ((bf16[8,256,256]{2,1,0:T(8,128)(2,1)}), bf16[8,256,256]{2,1,0:T(8,128)(2,1)S(1)}, u32[]{:S(2)}, u32[]{:S(2)}) async-start(bf16[8,256,256]{2,1,0:T(8,128)(2,1)} %add_convert_fusion), calls=%async_computation | async-start | bytes 2097152 | tf_op jit(solution)/shard_map/all_to_all | solution.py:346
  14.6 4.8 %first.1 = (bf16[64,1280]{1,0:T(8,128)(2,1)S(1)}, bf16[64,1280]{1,0:T(8,128)(2,1)S(1)}, bf16[64,1280]{1,0:T(8,128)(2,1)S(1)}, bf16[64,1280]{1,0:T(8,128)(2,1)S(1)}) custom-call(s32[1]{0:T(128)} %bitcast.place_ref, bf16[2,256,1280]{2,1,0:T(8,128)(2,1)} %q_ref.5, f32[5,256,256]{2,1,0:T(8,128)} %g_ref.3, f32[5,256,256]{2,1,0:T(8,128)} %u_ref.3, ...), custom_call_target="tpu_custom_call" | custom-call | tf_op jit(solution)/shard_map/first/pallas_call | solution.py:326
  19.5 1.3 %collective-permute-start.4 = (bf16[64,1280]{1,0:T(8,128)(2,1)S(1)}, bf16[64,1280]{1,0:T(8,128)(2,1)S(1)}, u32[]{:S(2)}, u32[]{:S(2)}) collective-permute-start(bf16[64,1280]{1,0:T(8,128)(2,1)S(1)} %get-tuple-element.26), channel_id=1, source_target_pairs={{0,64},{64,128},{128,192},{192,0},{1,65},{65,129},{129,193},{193,1... | collective-permute-start | bytes 491528 | tf_op jit(solution)/shard_map/ppermute | solution.py:340
  20.8 2.4 %collective-permute-start.5 = (bf16[64,1280]{1,0:T(8,128)(2,1)S(1)}, bf16[64,1280]{1,0:T(8,128)(2,1)S(1)}, u32[]{:S(2)}, u32[]{:S(2)}) collective-permute-start(bf16[64,1280]{1,0:T(8,128)(2,1)S(1)} %get-tuple-element.27), channel_id=1, source_target_pairs={{0,128},{64,192},{128,0},{192,64},{1,129},{65,193},{129,1},{193,65... | collective-permute-start | bytes 491528 | tf_op jit(solution)/shard_map/ppermute | solution.py:340
  23.2 1.2 %collective-permute-start.6 = (bf16[64,1280]{1,0:T(8,128)(2,1)S(1)}, bf16[64,1280]{1,0:T(8,128)(2,1)S(1)}, u32[]{:S(2)}, u32[]{:S(2)}) collective-permute-start(bf16[64,1280]{1,0:T(8,128)(2,1)S(1)} %get-tuple-element.28), channel_id=1, source_target_pairs={{0,192},{64,0},{128,64},{192,128},{1,193},{65,1},{129,65},{193,129... | collective-permute-start | bytes 491528 | tf_op jit(solution)/shard_map/ppermute | solution.py:340
  24.4 5.8 %all-to-all-done = bf16[8,256,256]{2,1,0:T(8,128)(2,1)S(1)} async-done(((bf16[8,256,256]{2,1,0:T(8,128)(2,1)}), bf16[8,256,256]{2,1,0:T(8,128)(2,1)S(1)}, u32[]{:S(2)}, u32[]{:S(2)}) %all-to-all-start) | async-done | bytes 1048608 | tf_op jit(solution)/shard_map/all_to_all | solution.py:346
  30.2 0.1 reduce_sum.12.refs_0_
  30.3 3.1 %collective-permute-start.1 = (bf16[256,256]{1,0:T(8,128)(2,1)S(1)}, bf16[256,256]{1,0:T(8,128)(2,1)S(1)}, u32[]{:S(2)}, u32[]{:S(2)}) collective-permute-start(bf16[256,256]{1,0:T(8,128)(2,1)S(1)} %reduce_sum.12.refs_0_), channel_id=1, source_target_pairs={{0,16},{16,40},{40,56},{56,0},{8,24},{24,32},{32,48},{48,8},{1,17}... | collective-permute-start | bytes 393224 | tf_op jit(solution)/shard_map/ppermute | solution.py:350
  33.4 3.6 %collective-permute-start.2 = (bf16[256,256]{1,0:T(8,128)(2,1)S(1)}, bf16[256,256]{1,0:T(8,128)(2,1)S(1)}, u32[]{:S(2)}, u32[]{:S(2)}) collective-permute-start(bf16[256,256]{1,0:T(8,128)(2,1)S(1)} %reduce_sum.12.refs_0_), channel_id=1, source_target_pairs={{0,40},{16,56},{40,0},{56,16},{8,32},{24,48},{32,8},{48,24},{1,41}... | collective-permute-start | bytes 393224 | tf_op jit(solution)/shard_map/ppermute | solution.py:350
  36.9 0.0 collective-permute-done.4.refs_1_
  36.9 2.4 %collective-permute-start.3 = (bf16[256,256]{1,0:T(8,128)(2,1)S(1)}, bf16[256,256]{1,0:T(8,128)(2,1)S(1)}, u32[]{:S(2)}, u32[]{:S(2)}) collective-permute-start(bf16[256,256]{1,0:T(8,128)(2,1)S(1)} %reduce_sum.12.refs_0_), channel_id=1, source_target_pairs={{0,56},{16,0},{40,16},{56,40},{8,48},{24,8},{32,24},{48,32},{1,57}... | collective-permute-start | bytes 393224 | tf_op jit(solution)/shard_map/ppermute | solution.py:350
  39.3 0.0 collective-permute-done.5.refs_2_
  39.3 0.0 collective-permute-done.6.refs_3_
  39.3 1.6 %collective-permute-done.1.refs_1_ = bf16[256,256]{1,0:T(8,128)(2,1)S(1)} collective-permute-done((bf16[256,256]{1,0:T(8,128)(2,1)S(1)}, bf16[256,256]{1,0:T(8,128)(2,1)S(1)}, u32[]{:S(2)}, u32[]{:S(2)}) %collective-permute-start.1) | collective-permute-done | bytes 131104 | tf_op jit(solution)/shard_map/ppermute | solution.py:350
  40.9 5.7 %collective-permute-done.2.refs_2_ = bf16[256,256]{1,0:T(8,128)(2,1)S(1)} collective-permute-done((bf16[256,256]{1,0:T(8,128)(2,1)S(1)}, bf16[256,256]{1,0:T(8,128)(2,1)S(1)}, u32[]{:S(2)}, u32[]{:S(2)}) %collective-permute-start.2) | collective-permute-done | bytes 131104 | tf_op jit(solution)/shard_map/ppermute | solution.py:350
  46.7 0.7 collective-permute-done.3.refs_3_
  47.4 2.2 %orthogonalize.1 = bf16[8,256,256]{2,1,0:T(8,128)(2,1)S(1)} custom-call(bf16[256,256]{1,0:T(8,128)(2,1)S(1)} %reduce_sum.12.refs_0_, bf16[256,256]{1,0:T(8,128)(2,1)S(1)} %collective-permute-done.1.refs_1_, bf16[256,256]{1,0:T(8,128)(2,1)S(1)} %collective-permute-done.2.refs_2_, bf16[256,256]{1,0:T(8,128)(2,1)S(1)} %collective-permute-done.3.refs_3_), custom_call_target="tpu_custom_call" | custom-call | tf_op jit(solution)/shard_map/orthogonalize/pallas_call | solution.py:357
  49.6 0.0 copy-start
  49.6 18.1 %all_to_all.15.mine_ref = bf16[8,256,256]{2,1,0:T(8,128)(2,1)S(1)} all-to-all(bf16[8,256,256]{2,1,0:T(8,128)(2,1)S(1)} %orthogonalize.1), channel_id=1, replica_groups=mesh['head'=4,'z_hi'=4,'z_lo'=2,'y'=4,'core'=2] {'y','z_lo'}, dimensions={0} | all-to-all | bytes 2097152 | tf_op jit(solution)/shard_map/all_to_all | solution.py:363
  67.7 2.5 %collective-permute-start.7 = (bf16[8,256,256]{2,1,0:T(8,128)(2,1)S(1)}, bf16[8,256,256]{2,1,0:T(8,128)(2,1)S(1)}, u32[]{:S(2)}, u32[]{:S(2)}) collective-permute-start(bf16[8,256,256]{2,1,0:T(8,128)(2,1)S(1)} %all_to_all.15.mine_ref), channel_id=1, source_target_pairs={{0,1},{1,0},{2,3},{3,2},{4,5},{5,4},{6,7},{7,6},{8,9},{9,8},{10,11... | collective-permute-start | bytes 3145736 | tf_op jit(solution)/shard_map/ppermute | solution.py:364
  70.2 3.2 %second_own.1 = (bf16[256,512]{1,0:T(8,128)(2,1)S(1)}, f32[3,256,256]{2,1,0:T(8,128)S(1)}, f32[3,256,256]{2,1,0:T(8,128)S(1)}, f32[3,256,256]{2,1,0:T(8,128)S(1)}) custom-call(s32[1]{0:T(128)} %bitcast.1.core_ref, s32[1]{0:T(128)} %bitcast.2.far_ref, bf16[2,256,1280]{2,1,0:T(8,128)(2,1)S(1)} %copy-done, f32[5,256,256]{2,1,0:T(8,128)} %g_ref.3, ...), custom_call_target="tpu_custom_call" | custom-call | tf_op jit(solution)/shard_map/second_own/pallas_call | solution.py:372
  73.4 0.0 collective-permute-done.7.other_ref
  73.4 2.8 %second_rest.1 = bf16[256,1280]{1,0:T(8,128)(2,1)} custom-call(s32[1]{0:T(128)} %bitcast.1.core_ref, s32[1]{0:T(128)} %bitcast.2.far_ref, bf16[2,256,1280]{2,1,0:T(8,128)(2,1)} %q_ref.5, f32[3,256,256]{2,1,0:T(8,128)S(1)} %get-tuple-element.37.g_rest, f32[3,256,256]{2,1,0:T(8,128)S(1)} %get-tuple-element.38.u_rest, ...), custom_call_target="tpu_custom_call" | custom-call | tf_op jit(solution)/shard_map/second_rest/pallas_call | solution.py:389
  76.2 4.0 %all-to-all-start.2 = ((bf16[4,64,1280]{2,1,0:T(8,128)(2,1)}), bf16[4,64,1280]{2,1,0:T(8,128)(2,1)S(1)}, u32[]{:S(2)}, u32[]{:S(2)}) async-start(bf16[4,64,1280]{2,1,0:T(8,128)(2,1)} %bitcast.3), calls=%async_computation.2 | async-start | bytes 1310720 | tf_op jit(solution)/shard_map/all_to_all | solution.py:402
  80.2 1.4 %lay_first.1.buf_ref = bf16[2,64,5120]{2,1,0:T(8,128)(2,1)} custom-call(s32[1]{0:T(128)} %bitcast.place_ref, bf16[64,1280]{1,0:T(8,128)(2,1)S(1)} %get-tuple-element.29.refs_0_, bf16[64,1280]{1,0:T(8,128)(2,1)S(1)} %collective-permute-done.4.refs_1_, bf16[64,1280]{1,0:T(8,128)(2,1)S(1)} %collective-permute-done.5.refs_2_, ...), custom_call_target="tpu_custom_call" | custom-call | tf_op jit(solution)/shard_map/lay_first/pallas_call | solution.py:404
  81.6 9.3 %all-to-all-done.2.rows_ref = bf16[4,64,1280]{2,1,0:T(8,128)(2,1)S(1)} async-done(((bf16[4,64,1280]{2,1,0:T(8,128)(2,1)}), bf16[4,64,1280]{2,1,0:T(8,128)(2,1)S(1)}, u32[]{:S(2)}, u32[]{:S(2)}) %all-to-all-start.2) | async-done | bytes 655392 | tf_op jit(solution)/shard_map/all_to_all | solution.py:402
  90.9 1.4 %lay_second.1 = bf16[2,64,5120]{2,1,0:T(8,128)(2,1)} custom-call(bf16[2,64,5120]{2,1,0:T(8,128)(2,1)} %lay_first.1.buf_ref, bf16[4,64,1280]{2,1,0:T(8,128)(2,1)S(1)} %all-to-all-done.2.rows_ref), custom_call_target="tpu_custom_call", output_to_operand_aliasing={{}: (0, {})} | custom-call | tf_op jit(solution)/shard_map/lay_second/pallas_call | solution.py:416
  (1 shorter events, 0.0 us)
Async XLA Ops:
  3.6 6.0 %collective-permute-start = (bf16[8,256,256]{2,1,0:T(8,128)(2,1)S(1)}, bf16[8,256,256]{2,1,0:T(8,128)(2,1)S(1)}, u32[]{:S(2)}, u32[]{:S(2)}) collective-permute-start(bf16[8,256,256]{2,1,0:T(8,128)(2,1)S(1)} %get-tuple-element.24), channel_id=1, source_target_pairs={{0,1},{1,0},{2,3},{3,2},{4,5},{5,4},{6,7},{7,6},{8,9},{9,8},{10,11... | collective-permute-start | bytes 3145736 | tf_op jit(solution)/shard_map/ppermute | solution.py:310
  10.8 19.4 %all-to-all-start = ((bf16[8,256,256]{2,1,0:T(8,128)(2,1)}), bf16[8,256,256]{2,1,0:T(8,128)(2,1)S(1)}, u32[]{:S(2)}, u32[]{:S(2)}) async-start(bf16[8,256,256]{2,1,0:T(8,128)(2,1)} %add_convert_fusion), calls=%async_computation | async-start | bytes 2097152 | tf_op jit(solution)/shard_map/all_to_all | solution.py:346
  19.5 17.5 %collective-permute-start.4 = (bf16[64,1280]{1,0:T(8,128)(2,1)S(1)}, bf16[64,1280]{1,0:T(8,128)(2,1)S(1)}, u32[]{:S(2)}, u32[]{:S(2)}) collective-permute-start(bf16[64,1280]{1,0:T(8,128)(2,1)S(1)} %get-tuple-element.26), channel_id=1, source_target_pairs={{0,64},{64,128},{128,192},{192,0},{1,65},{65,129},{129,193},{193,1... | collective-permute-start | bytes 491528 | tf_op jit(solution)/shard_map/ppermute | solution.py:340
  20.8 18.6 %collective-permute-start.5 = (bf16[64,1280]{1,0:T(8,128)(2,1)S(1)}, bf16[64,1280]{1,0:T(8,128)(2,1)S(1)}, u32[]{:S(2)}, u32[]{:S(2)}) collective-permute-start(bf16[64,1280]{1,0:T(8,128)(2,1)S(1)} %get-tuple-element.27), channel_id=1, source_target_pairs={{0,128},{64,192},{128,0},{192,64},{1,129},{65,193},{129,1},{193,65... | collective-permute-start | bytes 491528 | tf_op jit(solution)/shard_map/ppermute | solution.py:340
  23.2 16.1 %collective-permute-start.6 = (bf16[64,1280]{1,0:T(8,128)(2,1)S(1)}, bf16[64,1280]{1,0:T(8,128)(2,1)S(1)}, u32[]{:S(2)}, u32[]{:S(2)}) collective-permute-start(bf16[64,1280]{1,0:T(8,128)(2,1)S(1)} %get-tuple-element.28), channel_id=1, source_target_pairs={{0,192},{64,0},{128,64},{192,128},{1,193},{65,1},{129,65},{193,129... | collective-permute-start | bytes 491528 | tf_op jit(solution)/shard_map/ppermute | solution.py:340
  30.3 10.6 %collective-permute-start.1 = (bf16[256,256]{1,0:T(8,128)(2,1)S(1)}, bf16[256,256]{1,0:T(8,128)(2,1)S(1)}, u32[]{:S(2)}, u32[]{:S(2)}) collective-permute-start(bf16[256,256]{1,0:T(8,128)(2,1)S(1)} %reduce_sum.12.refs_0_), channel_id=1, source_target_pairs={{0,16},{16,40},{40,56},{56,0},{8,24},{24,32},{32,48},{48,8},{1,17}... | collective-permute-start | bytes 393224 | tf_op jit(solution)/shard_map/ppermute | solution.py:350
  33.4 13.3 %collective-permute-start.2 = (bf16[256,256]{1,0:T(8,128)(2,1)S(1)}, bf16[256,256]{1,0:T(8,128)(2,1)S(1)}, u32[]{:S(2)}, u32[]{:S(2)}) collective-permute-start(bf16[256,256]{1,0:T(8,128)(2,1)S(1)} %reduce_sum.12.refs_0_), channel_id=1, source_target_pairs={{0,40},{16,56},{40,0},{56,16},{8,32},{24,48},{32,8},{48,24},{1,41}... | collective-permute-start | bytes 393224 | tf_op jit(solution)/shard_map/ppermute | solution.py:350
  36.9 10.4 %collective-permute-start.3 = (bf16[256,256]{1,0:T(8,128)(2,1)S(1)}, bf16[256,256]{1,0:T(8,128)(2,1)S(1)}, u32[]{:S(2)}, u32[]{:S(2)}) collective-permute-start(bf16[256,256]{1,0:T(8,128)(2,1)S(1)} %reduce_sum.12.refs_0_), channel_id=1, source_target_pairs={{0,56},{16,0},{40,16},{56,40},{8,48},{24,8},{32,24},{48,32},{1,57}... | collective-permute-start | bytes 393224 | tf_op jit(solution)/shard_map/ppermute | solution.py:350
  49.6 20.7 %copy-start = (bf16[2,256,1280]{2,1,0:T(8,128)(2,1)S(1)}, bf16[2,256,1280]{2,1,0:T(8,128)(2,1)}, u32[]{:S(2)}) copy-start(bf16[2,256,1280]{2,1,0:T(8,128)(2,1)} %q_ref.5) | copy-start | bytes 3932164
  67.7 5.7 %collective-permute-start.7 = (bf16[8,256,256]{2,1,0:T(8,128)(2,1)S(1)}, bf16[8,256,256]{2,1,0:T(8,128)(2,1)S(1)}, u32[]{:S(2)}, u32[]{:S(2)}) collective-permute-start(bf16[8,256,256]{2,1,0:T(8,128)(2,1)S(1)} %all_to_all.15.mine_ref), channel_id=1, source_target_pairs={{0,1},{1,0},{2,3},{3,2},{4,5},{5,4},{6,7},{7,6},{8,9},{9,8},{10,11... | collective-permute-start | bytes 3145736 | tf_op jit(solution)/shard_map/ppermute | solution.py:364
  76.2 14.7 %all-to-all-start.2 = ((bf16[4,64,1280]{2,1,0:T(8,128)(2,1)}), bf16[4,64,1280]{2,1,0:T(8,128)(2,1)S(1)}, u32[]{:S(2)}, u32[]{:S(2)}) async-start(bf16[4,64,1280]{2,1,0:T(8,128)(2,1)} %bitcast.3), calls=%async_computation.2 | async-start | bytes 1310720 | tf_op jit(solution)/shard_map/all_to_all | solution.py:402

commit v10 on v8

--- a/solution.py
+++ b/solution.py
@@ -17,7 +17,7 @@
 MATS = 3 * HEADS_HERE
 GROUP = 8
 N_FAR = 4
-VMEM_LIMIT = 48 * 1024 * 1024
+VMEM_LIMIT = 24 * 1024 * 1024
 
 
 def dot_f32(a, b):
@@ -185,20 +185,62 @@
     return (fast - orth.astype(F32)).astype(BF16)
 
 
-def second_kernel(core_ref, far_ref, q_ref, g_ref, u_ref, d_ref, mine_ref, other_ref, out_ref):
-    low_core = core_ref[0] == 0
+def stage_kernel(q_ref, g_ref, u_ref, d_ref, q_out, g_out, u_out, d_out, sems):
+    pairs = ((q_ref.at[1], q_out), (g_ref, g_out), (u_ref, u_out), (d_ref, d_out))
+    copies = [pltpu.make_async_copy(src, dst, sems.at[i]) for i, (src, dst) in enumerate(pairs)]
+    for copy in copies:
+        copy.start()
+    for copy in copies:
+        copy.wait()
+
+
+def second_head(head, base, twist, q_ref, fast_refs, mine_ref, other_ref=None, other_base=0):
+    nexts = []
+    for mat, ref in enumerate(fast_refs):
+        at = head * 3 + mat
+        if 0 <= at - base < GROUP:
+            orth = mine_ref[jnp.bitwise_xor(at - base, twist)]
+        else:
+            orth = other_ref[jnp.bitwise_xor(at - other_base, twist)]
+        nexts.append(next_weight(ref[head], orth))
+    return apply_fast(q_ref[:, head * HD : (head + 1) * HD], *nexts)
+
+
+def own_second_kernel(core_ref, far_ref, q_ref, g_ref, u_ref, d_ref, mine_ref, out_ref):
     twist = twist_of(far_ref)
-    for head in range(HEADS_HERE):
-        nexts = []
-        for mat, ref in enumerate((g_ref, u_ref, d_ref)):
-            at = head * 3 + mat
-            in_low = at < GROUP
-            index = jnp.bitwise_xor(at if in_low else at - (GROUP - 1), twist)
-            pair = (mine_ref[index], other_ref[index])
-            orth = jnp.where(low_core, *(pair if in_low else pair[::-1]))
-            nexts.append(next_weight(ref[head], orth))
-        cols = slice(head * HD, (head + 1) * HD)
-        out_ref[:, cols] = apply_fast(q_ref[0, :, cols], *nexts)
+
+    def run(own_from, base):
+        for i in range(2):
+            out_ref[:, i * HD : (i + 1) * HD] = second_head(
+                own_from + i, base, twist, q_ref, (g_ref, u_ref, d_ref), mine_ref
+            )
+
+    @pl.when(core_ref[0] == 0)
+    def _():
+        run(0, 0)
+
+    @pl.when(core_ref[0] != 0)
+    def _():
+        run(3, GROUP - 1)
+
+
+def rest_second_kernel(core_ref, far_ref, q_ref, g_ref, u_ref, d_ref, mine_ref, other_ref, own_ref, out_ref):
+    twist = twist_of(far_ref)
+
+    def run(own_from, rest_from, base, other_base):
+        out_ref[:, own_from * HD : (own_from + 2) * HD] = own_ref[...]
+        for head in range(rest_from, rest_from + 3):
+            out_ref[:, head * HD : (head + 1) * HD] = second_head(
+                head, base, twist, q_ref, (g_ref, u_ref, d_ref), mine_ref, other_ref, other_base
+            )
+
+    @pl.when(core_ref[0] == 0)
+    def _():
+        run(0, 2, 0, GROUP - 1)
+
+    @pl.when(core_ref[0] != 0)
+    def _():
+        run(3, 0, GROUP - 1, 0)
 
 
 def lay_first_kernel(place_ref, *refs):
@@ -309,8 +351,20 @@
         )
         for hop in range(1, N_FAR)
     ]
-    late = lax.optimization_barrier((*partials, *firsts))
-    partials, firsts = late[:N_FAR], late[N_FAR:]
+    rows_full = pl.BlockSpec((rows, width), lambda *_: (0, 0))
+    fast_spec = pl.BlockSpec((HEADS_HERE, HD, HD), lambda *_: (0, 0, 0))
+    staged = pl.pallas_call(
+        stage_kernel,
+        grid=(1,),
+        in_specs=[any_spec] * 4,
+        out_specs=[rows_full] + [fast_spec] * 3,
+        out_shape=[rows_shape] + [jax.ShapeDtypeStruct((HEADS_HERE, HD, HD), F32)] * 3,
+        scratch_shapes=[pltpu.SemaphoreType.DMA((4,))],
+        compiler_params=params,
+        name="stage",
+    )(q_hbm, g_hbm, u_hbm, d_hbm)
+    late = lax.optimization_barrier((*partials, *firsts, *staged))
+    partials, firsts, staged = late[:N_FAR], late[N_FAR : N_FAR + n_head], late[N_FAR + n_head :]
     orth = pl.pallas_call(
         orth_kernel,
         out_shape=jax.ShapeDtypeStruct(piece_shape, BF16),
@@ -321,19 +375,31 @@
     orth_other = lax.ppermute(orth_mine, "core", swap)
 
     group_spec = pl.BlockSpec((GROUP, HD, HD), lambda i, *_: (0, 0, 0))
-    fast_spec = pl.BlockSpec((HEADS_HERE, HD, HD), lambda i, *_: (0, 0, 0))
-    second = pl.pallas_call(
-        second_kernel,
+    own_spec = pl.BlockSpec((rows, 2 * HD), lambda *_: (0, 0))
+    own = pl.pallas_call(
+        own_second_kernel,
         grid_spec=pltpu.PrefetchScalarGridSpec(
             num_scalar_prefetch=2,
             grid=(1,),
-            in_specs=[pl.BlockSpec((1, rows, width), lambda i, *_: (1, 0, 0))] + [fast_spec] * 3 + [group_spec] * 2,
-            out_specs=pl.BlockSpec((rows, width), lambda i, *_: (0, 0)),
+            in_specs=[rows_full] + [fast_spec] * 3 + [group_spec],
+            out_specs=own_spec,
+        ),
+        out_shape=jax.ShapeDtypeStruct((rows, 2 * HD), BF16),
+        compiler_params=params,
+        name="second_own",
+    )(core, far, *staged, orth_mine)
+    second = pl.pallas_call(
+        rest_second_kernel,
+        grid_spec=pltpu.PrefetchScalarGridSpec(
+            num_scalar_prefetch=2,
+            grid=(1,),
+            in_specs=[rows_full] + [fast_spec] * 3 + [group_spec] * 2 + [own_spec],
+            out_specs=rows_full,
         ),
         out_shape=rows_shape,
         compiler_params=params,
-        name="second",
-    )(core, far, queries, gate_fast, up_fast, down_fast, orth_mine, orth_other)
+        name="second_rest",
+    )(core, far, *staged, orth_mine, orth_other, own)
 
     swapped = lax.all_to_all(second.reshape(n_head, part, width), "head", split_axis=0, concat_axis=0, tiled=True)
     out_shape = jax.ShapeDtypeStruct((2, part, n_head * width), BF16)

time: 92.5 us -> 90.1 us (0.974)
  waiting for transfers between devices: 25.1 us -> 22.1 us
    ppermute x3, waiting for transfers between devices: 8.08 us -> 5.66 us  [local(): lax.ppermute(partial, ('z_hi', 'z_lo'), [(ring[i], ring[(i + hop) % N_FAR...]
    pallas_call x1 -> x3, Pallas kernels: 3.81 us -> 4.59 us  [the longest x1 2.34 us: local(): pl.pallas_call(stage_kernel, grid=(1,), in_specs=[any_spec] * 4, out_spec...]
  transfers between devices with their start and end apart: 10 -> 10, of which waited for: 6 -> 5; matrix products, arithmetic and copies ran while one was open for 0% -> 0% of each run, Pallas kernels for 10% -> 13%
where the time goes in v10:
time: 90.1 us; the launch traced here: 89.8 us
  starting transfers between devices  27.6 us (31%)
  waiting for transfers between devices  22.1 us (25%)
  Pallas kernels  20.6 us (23%)
  blocking collectives  18 us (20%)
  other arithmetic  1.41 us (2%)
    all_to_all x1, blocking collectives, local(): lax.all_to_all(orth, slots, split_axis=0, concat_axis=0, tiled=True)  18 us
    ppermute x3, starting transfers between devices, local(): lax.ppermute(partial, ('z_hi', 'z_lo'), [(ring[i], ring[(i + hop) % N_FAR...  9.01 us
    all_to_all x1, waiting for transfers between devices, local(): lax.all_to_all(second.reshape(n_head, part, width), 'head', split_axis=0,...  8.89 us
    all_to_all x1, waiting for transfers between devices, local(): lax.all_to_all(chip_sum, slots, split_axis=0, concat_axis=0, tiled=True)  5.81 us
    ppermute x3, waiting for transfers between devices, local(): lax.ppermute(partial, ('z_hi', 'z_lo'), [(ring[i], ring[(i + hop) % N_FAR...  5.66 us
    ppermute x3, starting transfers between devices, local(): lax.ppermute(firsts[hop], 'head', [(i, (i + hop) % n_head) for i in range...  4.89 us
    pallas_call x1, Pallas kernels, local(): pl.pallas_call(first_kernel, grid_spec=pltpu.PrefetchScalarGridSpec(num_s...  4.84 us
    all_to_all x1, starting transfers between devices, local(): lax.all_to_all(second.reshape(n_head, part, width), 'head', split_axis=0,...  4.01 us
  transfers between devices with their start and end apart: 10, of which 5 were waited for; matrix products, arithmetic and copies ran while one was open for 0% of the time, Pallas kernels for 13%

profile of v10, /device:TPU:1, one launch (start us, length us, event | category | flops | bytes accessed | tf_op | source)
XLA Modules:
  0.0 89.8 jit_solution(14277300545346911390)
XLA Ops:
  0.0 3.6 %grads_sent.1 = (bf16[8,256,256]{2,1,0:T(8,128)(2,1)S(1)}, bf16[2,256,256]{2,1,0:T(8,128)(2,1)S(1)}) custom-call(s32[1]{0:T(128)} %bitcast.1.core_ref, s32[1]{0:T(128)} %bitcast.2.far_ref, bf16[256,1280]{1,0:T(8,128)(2,1)} %refs_0_.3, bf16[256,1280]{1,0:T(8,128)(2,1)} %refs_1_.3, f32[5,256]{1,0:T(8,128)} %refs_2_.3, f32[5,256,256]{2,1,0:T(8,128)} %g_ref.3, ...), custom_call_target="tpu_custom_call" | custom-call | tf_op jit(solution)/shard_map/grads_sent/pallas_call | solution.py:294
  3.6 3.4 %collective-permute-start = (bf16[8,256,256]{2,1,0:T(8,128)(2,1)S(1)}, bf16[8,256,256]{2,1,0:T(8,128)(2,1)S(1)}, u32[]{:S(2)}, u32[]{:S(2)}) collective-permute-start(bf16[8,256,256]{2,1,0:T(8,128)(2,1)S(1)} %get-tuple-element.28), channel_id=1, source_target_pairs={{0,1},{1,0},{2,3},{3,2},{4,5},{5,4},{6,7},{7,6},{8,9},{9,8},{10,11... | collective-permute-start | bytes 3145736 | tf_op jit(solution)/shard_map/ppermute | solution.py:309
  6.9 2.6 %grads_kept.1 = bf16[8,256,256]{2,1,0:T(8,128)(2,1)S(1)} custom-call(s32[1]{0:T(128)} %bitcast.1.core_ref, s32[1]{0:T(128)} %bitcast.2.far_ref, bf16[256,1280]{1,0:T(8,128)(2,1)} %refs_0_.3, bf16[256,1280]{1,0:T(8,128)(2,1)} %refs_1_.3, f32[5,256]{1,0:T(8,128)} %refs_2_.3, f32[5,256,256]{2,1,0:T(8,128)} %g_ref.3, f32[5,256,256]{2,1,0:T(8,128)} %u_ref.3, ...), custom_call_target="tpu_custom_call" | custom-call | tf_op jit(solution)/shard_map/grads_kept/pallas_call | solution.py:310
  9.5 0.0 collective-permute-done
  9.5 1.3 %add_convert_fusion = bf16[8,256,256]{2,1,0:T(8,128)(2,1)} fusion(bf16[8,256,256]{2,1,0:T(8,128)(2,1)S(1)} %collective-permute-done, bf16[8,256,256]{2,1,0:T(8,128)(2,1)S(1)} %grads_kept.1), kind=kLoop, calls=%fused_computation | loop fusion | flops 2097152 | bytes 3145728 | tf_op jit(solution)/shard_map/convert_element_type | solution.py:343
  10.8 3.8 %all-to-all-start = ((bf16[8,256,256]{2,1,0:T(8,128)(2,1)}), bf16[8,256,256]{2,1,0:T(8,128)(2,1)S(1)}, u32[]{:S(2)}, u32[]{:S(2)}) async-start(bf16[8,256,256]{2,1,0:T(8,128)(2,1)} %add_convert_fusion), calls=%async_computation | async-start | bytes 2097152 | tf_op jit(solution)/shard_map/all_to_all | solution.py:345
  14.6 4.8 %first.1 = (bf16[64,1280]{1,0:T(8,128)(2,1)S(1)}, bf16[64,1280]{1,0:T(8,128)(2,1)S(1)}, bf16[64,1280]{1,0:T(8,128)(2,1)S(1)}, bf16[64,1280]{1,0:T(8,128)(2,1)S(1)}) custom-call(s32[1]{0:T(128)} %bitcast.place_ref, bf16[2,256,1280]{2,1,0:T(8,128)(2,1)} %q_ref.3, f32[5,256,256]{2,1,0:T(8,128)} %g_ref.3, f32[5,256,256]{2,1,0:T(8,128)} %u_ref.3, ...), custom_call_target="tpu_custom_call" | custom-call | tf_op jit(solution)/shard_map/first/pallas_call | solution.py:325
  19.5 1.3 %collective-permute-start.4 = (bf16[64,1280]{1,0:T(8,128)(2,1)S(1)}, bf16[64,1280]{1,0:T(8,128)(2,1)S(1)}, u32[]{:S(2)}, u32[]{:S(2)}) collective-permute-start(bf16[64,1280]{1,0:T(8,128)(2,1)S(1)} %get-tuple-element.30), channel_id=1, source_target_pairs={{0,64},{64,128},{128,192},{192,0},{1,65},{65,129},{129,193},{193,1... | collective-permute-start | bytes 491528 | tf_op jit(solution)/shard_map/ppermute | solution.py:339
  20.8 2.4 %collective-permute-start.5 = (bf16[64,1280]{1,0:T(8,128)(2,1)S(1)}, bf16[64,1280]{1,0:T(8,128)(2,1)S(1)}, u32[]{:S(2)}, u32[]{:S(2)}) collective-permute-start(bf16[64,1280]{1,0:T(8,128)(2,1)S(1)} %get-tuple-element.31), channel_id=1, source_target_pairs={{0,128},{64,192},{128,0},{192,64},{1,129},{65,193},{129,1},{193,65... | collective-permute-start | bytes 491528 | tf_op jit(solution)/shard_map/ppermute | solution.py:339
  23.2 1.2 %collective-permute-start.6 = (bf16[64,1280]{1,0:T(8,128)(2,1)S(1)}, bf16[64,1280]{1,0:T(8,128)(2,1)S(1)}, u32[]{:S(2)}, u32[]{:S(2)}) collective-permute-start(bf16[64,1280]{1,0:T(8,128)(2,1)S(1)} %get-tuple-element.32), channel_id=1, source_target_pairs={{0,192},{64,0},{128,64},{192,128},{1,193},{65,1},{129,65},{193,129... | collective-permute-start | bytes 491528 | tf_op jit(solution)/shard_map/ppermute | solution.py:339
  24.4 5.8 %all-to-all-done = bf16[8,256,256]{2,1,0:T(8,128)(2,1)S(1)} async-done(((bf16[8,256,256]{2,1,0:T(8,128)(2,1)}), bf16[8,256,256]{2,1,0:T(8,128)(2,1)S(1)}, u32[]{:S(2)}, u32[]{:S(2)}) %all-to-all-start) | async-done | bytes 1048608 | tf_op jit(solution)/shard_map/all_to_all | solution.py:345
  30.2 0.1 reduce_sum.12.refs_0_
  30.3 3.1 %collective-permute-start.1 = (bf16[256,256]{1,0:T(8,128)(2,1)S(1)}, bf16[256,256]{1,0:T(8,128)(2,1)S(1)}, u32[]{:S(2)}, u32[]{:S(2)}) collective-permute-start(bf16[256,256]{1,0:T(8,128)(2,1)S(1)} %reduce_sum.12.refs_0_), channel_id=1, source_target_pairs={{0,16},{16,40},{40,56},{56,0},{8,24},{24,32},{32,48},{48,8},{1,17}... | collective-permute-start | bytes 393224 | tf_op jit(solution)/shard_map/ppermute | solution.py:349
  33.4 3.6 %collective-permute-start.2 = (bf16[256,256]{1,0:T(8,128)(2,1)S(1)}, bf16[256,256]{1,0:T(8,128)(2,1)S(1)}, u32[]{:S(2)}, u32[]{:S(2)}) collective-permute-start(bf16[256,256]{1,0:T(8,128)(2,1)S(1)} %reduce_sum.12.refs_0_), channel_id=1, source_target_pairs={{0,40},{16,56},{40,0},{56,16},{8,32},{24,48},{32,8},{48,24},{1,41}... | collective-permute-start | bytes 393224 | tf_op jit(solution)/shard_map/ppermute | solution.py:349
  36.9 0.0 collective-permute-done.4.refs_1_
  36.9 2.4 %collective-permute-start.3 = (bf16[256,256]{1,0:T(8,128)(2,1)S(1)}, bf16[256,256]{1,0:T(8,128)(2,1)S(1)}, u32[]{:S(2)}, u32[]{:S(2)}) collective-permute-start(bf16[256,256]{1,0:T(8,128)(2,1)S(1)} %reduce_sum.12.refs_0_), channel_id=1, source_target_pairs={{0,56},{16,0},{40,16},{56,40},{8,48},{24,8},{32,24},{48,32},{1,57}... | collective-permute-start | bytes 393224 | tf_op jit(solution)/shard_map/ppermute | solution.py:349
  39.3 2.3 %stage.1 = (bf16[256,1280]{1,0:T(8,128)(2,1)S(1)}, f32[5,256,256]{2,1,0:T(8,128)S(1)}, f32[5,256,256]{2,1,0:T(8,128)S(1)}, f32[5,256,256]{2,1,0:T(8,128)S(1)}) custom-call(bf16[2,256,1280]{2,1,0:T(8,128)(2,1)} %q_ref.3, f32[5,256,256]{2,1,0:T(8,128)} %g_ref.3, f32[5,256,256]{2,1,0:T(8,128)} %u_ref.3, f32[5,256,256]{2,1,0:T(8,128)} %d_ref.3), custom_call_target="tpu_custom_call" | custom-call | tf_op jit(solution)/shard_map/stage/pallas_call | solution.py:356
  41.7 0.0 collective-permute-done.5.refs_2_
  41.7 0.0 collective-permute-done.6.refs_3_
  41.7 0.0 collective-permute-done.1.refs_1_
  41.7 4.9 %collective-permute-done.2.refs_2_ = bf16[256,256]{1,0:T(8,128)(2,1)S(1)} collective-permute-done((bf16[256,256]{1,0:T(8,128)(2,1)S(1)}, bf16[256,256]{1,0:T(8,128)(2,1)S(1)}, u32[]{:S(2)}, u32[]{:S(2)}) %collective-permute-start.2) | collective-permute-done | bytes 131104 | tf_op jit(solution)/shard_map/ppermute | solution.py:349
  46.7 0.7 collective-permute-done.3.refs_3_
  47.4 2.2 %orthogonalize.1 = bf16[8,256,256]{2,1,0:T(8,128)(2,1)S(1)} custom-call(bf16[256,256]{1,0:T(8,128)(2,1)S(1)} %reduce_sum.12.refs_0_, bf16[256,256]{1,0:T(8,128)(2,1)S(1)} %collective-permute-done.1.refs_1_, bf16[256,256]{1,0:T(8,128)(2,1)S(1)} %collective-permute-done.2.refs_2_, bf16[256,256]{1,0:T(8,128)(2,1)S(1)} %collective-permute-done.3.refs_3_), custom_call_target="tpu_custom_call" | custom-call | tf_op jit(solution)/shard_map/orthogonalize/pallas_call | solution.py:368
  49.6 18.0 %all_to_all.15.mine_ref = bf16[8,256,256]{2,1,0:T(8,128)(2,1)S(1)} all-to-all(bf16[8,256,256]{2,1,0:T(8,128)(2,1)S(1)} %orthogonalize.1), channel_id=1, replica_groups=mesh['head'=4,'z_hi'=4,'z_lo'=2,'y'=4,'core'=2] {'y','z_lo'}, dimensions={0} | all-to-all | bytes 2097152 | tf_op jit(solution)/shard_map/all_to_all | solution.py:374
  67.6 2.5 %collective-permute-start.7 = (bf16[8,256,256]{2,1,0:T(8,128)(2,1)S(1)}, bf16[8,256,256]{2,1,0:T(8,128)(2,1)S(1)}, u32[]{:S(2)}, u32[]{:S(2)}) collective-permute-start(bf16[8,256,256]{2,1,0:T(8,128)(2,1)S(1)} %all_to_all.15.mine_ref), channel_id=1, source_target_pairs={{0,1},{1,0},{2,3},{3,2},{4,5},{5,4},{6,7},{7,6},{8,9},{9,8},{10,11... | collective-permute-start | bytes 3145736 | tf_op jit(solution)/shard_map/ppermute | solution.py:375
  70.1 0.6 second_own.1.own_ref
  70.7 1.7 %collective-permute-done.7.other_ref = bf16[8,256,256]{2,1,0:T(8,128)(2,1)S(1)} collective-permute-done((bf16[8,256,256]{2,1,0:T(8,128)(2,1)S(1)}, bf16[8,256,256]{2,1,0:T(8,128)(2,1)S(1)}, u32[]{:S(2)}, u32[]{:S(2)}) %collective-permute-start.7) | collective-permute-done | bytes 1048608 | tf_op jit(solution)/shard_map/ppermute | solution.py:375
  72.4 1.7 %second_rest.1 = bf16[256,1280]{1,0:T(8,128)(2,1)} custom-call(s32[1]{0:T(128)} %bitcast.1.core_ref, s32[1]{0:T(128)} %bitcast.2.far_ref, bf16[256,1280]{1,0:T(8,128)(2,1)S(1)} %get-tuple-element.41.q_ref, f32[5,256,256]{2,1,0:T(8,128)S(1)} %get-tuple-element.42.g_ref, f32[5,256,256]{2,1,0:T(8,128)S(1)} %get-tuple-element.43.u_ref, ...), custom_call_target="tpu_custom_call" | custom-call | tf_op jit(solution)/shard_map/second_rest/pallas_call | solution.py:391
  74.0 4.0 %all-to-all-start.2 = ((bf16[4,64,1280]{2,1,0:T(8,128)(2,1)}), bf16[4,64,1280]{2,1,0:T(8,128)(2,1)S(1)}, u32[]{:S(2)}, u32[]{:S(2)}) async-start(bf16[4,64,1280]{2,1,0:T(8,128)(2,1)} %bitcast.3), calls=%async_computation.2 | async-start | bytes 1310720 | tf_op jit(solution)/shard_map/all_to_all | solution.py:404
  78.0 1.4 %lay_first.1.buf_ref = bf16[2,64,5120]{2,1,0:T(8,128)(2,1)} custom-call(s32[1]{0:T(128)} %bitcast.place_ref, bf16[64,1280]{1,0:T(8,128)(2,1)S(1)} %get-tuple-element.37.refs_0_, bf16[64,1280]{1,0:T(8,128)(2,1)S(1)} %collective-permute-done.4.refs_1_, bf16[64,1280]{1,0:T(8,128)(2,1)S(1)} %collective-permute-done.5.refs_2_, ...), custom_call_target="tpu_custom_call" | custom-call | tf_op jit(solution)/shard_map/lay_first/pallas_call | solution.py:406
  79.5 8.9 %all-to-all-done.2.rows_ref = bf16[4,64,1280]{2,1,0:T(8,128)(2,1)S(1)} async-done(((bf16[4,64,1280]{2,1,0:T(8,128)(2,1)}), bf16[4,64,1280]{2,1,0:T(8,128)(2,1)S(1)}, u32[]{:S(2)}, u32[]{:S(2)}) %all-to-all-start.2) | async-done | bytes 655392 | tf_op jit(solution)/shard_map/all_to_all | solution.py:404
  88.4 1.4 %lay_second.1 = bf16[2,64,5120]{2,1,0:T(8,128)(2,1)} custom-call(bf16[2,64,5120]{2,1,0:T(8,128)(2,1)} %lay_first.1.buf_ref, bf16[4,64,1280]{2,1,0:T(8,128)(2,1)S(1)} %all-to-all-done.2.rows_ref), custom_call_target="tpu_custom_call", output_to_operand_aliasing={{}: (0, {})} | custom-call | tf_op jit(solution)/shard_map/lay_second/pallas_call | solution.py:418
Async XLA Ops:
  3.6 6.0 %collective-permute-start = (bf16[8,256,256]{2,1,0:T(8,128)(2,1)S(1)}, bf16[8,256,256]{2,1,0:T(8,128)(2,1)S(1)}, u32[]{:S(2)}, u32[]{:S(2)}) collective-permute-start(bf16[8,256,256]{2,1,0:T(8,128)(2,1)S(1)} %get-tuple-element.28), channel_id=1, source_target_pairs={{0,1},{1,0},{2,3},{3,2},{4,5},{5,4},{6,7},{7,6},{8,9},{9,8},{10,11... | collective-permute-start | bytes 3145736 | tf_op jit(solution)/shard_map/ppermute | solution.py:309
  10.8 19.4 %all-to-all-start = ((bf16[8,256,256]{2,1,0:T(8,128)(2,1)}), bf16[8,256,256]{2,1,0:T(8,128)(2,1)S(1)}, u32[]{:S(2)}, u32[]{:S(2)}) async-start(bf16[8,256,256]{2,1,0:T(8,128)(2,1)} %add_convert_fusion), calls=%async_computation | async-start | bytes 2097152 | tf_op jit(solution)/shard_map/all_to_all | solution.py:345
  19.5 17.5 %collective-permute-start.4 = (bf16[64,1280]{1,0:T(8,128)(2,1)S(1)}, bf16[64,1280]{1,0:T(8,128)(2,1)S(1)}, u32[]{:S(2)}, u32[]{:S(2)}) collective-permute-start(bf16[64,1280]{1,0:T(8,128)(2,1)S(1)} %get-tuple-element.30), channel_id=1, source_target_pairs={{0,64},{64,128},{128,192},{192,0},{1,65},{65,129},{129,193},{193,1... | collective-permute-start | bytes 491528 | tf_op jit(solution)/shard_map/ppermute | solution.py:339
  20.8 20.9 %collective-permute-start.5 = (bf16[64,1280]{1,0:T(8,128)(2,1)S(1)}, bf16[64,1280]{1,0:T(8,128)(2,1)S(1)}, u32[]{:S(2)}, u32[]{:S(2)}) collective-permute-start(bf16[64,1280]{1,0:T(8,128)(2,1)S(1)} %get-tuple-element.31), channel_id=1, source_target_pairs={{0,128},{64,192},{128,0},{192,64},{1,129},{65,193},{129,1},{193,65... | collective-permute-start | bytes 491528 | tf_op jit(solution)/shard_map/ppermute | solution.py:339
  23.2 18.5 %collective-permute-start.6 = (bf16[64,1280]{1,0:T(8,128)(2,1)S(1)}, bf16[64,1280]{1,0:T(8,128)(2,1)S(1)}, u32[]{:S(2)}, u32[]{:S(2)}) collective-permute-start(bf16[64,1280]{1,0:T(8,128)(2,1)S(1)} %get-tuple-element.32), channel_id=1, source_target_pairs={{0,192},{64,0},{128,64},{192,128},{1,193},{65,1},{129,65},{193,129... | collective-permute-start | bytes 491528 | tf_op jit(solution)/shard_map/ppermute | solution.py:339
  30.3 11.4 %collective-permute-start.1 = (bf16[256,256]{1,0:T(8,128)(2,1)S(1)}, bf16[256,256]{1,0:T(8,128)(2,1)S(1)}, u32[]{:S(2)}, u32[]{:S(2)}) collective-permute-start(bf16[256,256]{1,0:T(8,128)(2,1)S(1)} %reduce_sum.12.refs_0_), channel_id=1, source_target_pairs={{0,16},{16,40},{40,56},{56,0},{8,24},{24,32},{32,48},{48,8},{1,17}... | collective-permute-start | bytes 393224 | tf_op jit(solution)/shard_map/ppermute | solution.py:349
  33.4 13.3 %collective-permute-start.2 = (bf16[256,256]{1,0:T(8,128)(2,1)S(1)}, bf16[256,256]{1,0:T(8,128)(2,1)S(1)}, u32[]{:S(2)}, u32[]{:S(2)}) collective-permute-start(bf16[256,256]{1,0:T(8,128)(2,1)S(1)} %reduce_sum.12.refs_0_), channel_id=1, source_target_pairs={{0,40},{16,56},{40,0},{56,16},{8,32},{24,48},{32,8},{48,24},{1,41}... | collective-permute-start | bytes 393224 | tf_op jit(solution)/shard_map/ppermute | solution.py:349
  36.9 10.4 %collective-permute-start.3 = (bf16[256,256]{1,0:T(8,128)(2,1)S(1)}, bf16[256,256]{1,0:T(8,128)(2,1)S(1)}, u32[]{:S(2)}, u32[]{:S(2)}) collective-permute-start(bf16[256,256]{1,0:T(8,128)(2,1)S(1)} %reduce_sum.12.refs_0_), channel_id=1, source_target_pairs={{0,56},{16,0},{40,16},{56,40},{8,48},{24,8},{32,24},{48,32},{1,57}... | collective-permute-start | bytes 393224 | tf_op jit(solution)/shard_map/ppermute | solution.py:349
  67.6 4.8 %collective-permute-start.7 = (bf16[8,256,256]{2,1,0:T(8,128)(2,1)S(1)}, bf16[8,256,256]{2,1,0:T(8,128)(2,1)S(1)}, u32[]{:S(2)}, u32[]{:S(2)}) collective-permute-start(bf16[8,256,256]{2,1,0:T(8,128)(2,1)S(1)} %all_to_all.15.mine_ref), channel_id=1, source_target_pairs={{0,1},{1,0},{2,3},{3,2},{4,5},{5,4},{6,7},{7,6},{8,9},{9,8},{10,11... | collective-permute-start | bytes 3145736 | tf_op jit(solution)/shard_map/ppermute | solution.py:375
  74.0 14.3 %all-to-all-start.2 = ((bf16[4,64,1280]{2,1,0:T(8,128)(2,1)}), bf16[4,64,1280]{2,1,0:T(8,128)(2,1)S(1)}, u32[]{:S(2)}, u32[]{:S(2)}) async-start(bf16[4,64,1280]{2,1,0:T(8,128)(2,1)} %bitcast.3), calls=%async_computation.2 | async-start | bytes 1310720 | tf_op jit(solution)/shard_map/all_to_all | solution.py:404

commit v11 on v10

--- a/solution.py
+++ b/solution.py
@@ -252,8 +252,16 @@
             refs[-1][0] = ref[...]
 
 
-def lay_second_kernel(buf_ref, rows_ref, out_ref):
-    out_ref[...] = rows_ref[...]
+def lay_second_kernel(buf_ref, rows_ref, out_ref, sems):
+    count, _, width = rows_ref.shape
+    copies = [
+        pltpu.make_async_copy(rows_ref.at[i], out_ref.at[1, :, pl.ds(i * width, width)], sems.at[i])
+        for i in range(count)
+    ]
+    for copy in copies:
+        copy.start()
+    for copy in copies:
+        copy.wait()
 
 
 def local(queries, key_rows, value_rows, step_rates, gate_fast, up_fast, down_fast):
@@ -349,7 +357,7 @@
         lax.ppermute(
             partial, ("z_hi", "z_lo"), [(ring[i], ring[(i + hop) % N_FAR]) for ring in rings for i in range(N_FAR)]
         )
-        for hop in range(1, N_FAR)
+        for hop in (2, 1, 3)
     ]
     rows_full = pl.BlockSpec((rows, width), lambda *_: (0, 0))
     fast_spec = pl.BlockSpec((HEADS_HERE, HD, HD), lambda *_: (0, 0, 0))
@@ -417,14 +425,12 @@
     )(place, *firsts)
     return pl.pallas_call(
         lay_second_kernel,
-        grid=(n_head,),
-        in_specs=[
-            pl.BlockSpec(memory_space=pl.ANY),
-            pl.BlockSpec((1, part, width), lambda s: (s, 0, 0)),
-        ],
-        out_specs=pl.BlockSpec((1, part, width), lambda s: (1, 0, s)),
+        grid=(1,),
+        in_specs=[any_spec, pl.BlockSpec((n_head, part, width), lambda s: (0, 0, 0))],
+        out_specs=any_spec,
         out_shape=out_shape,
         input_output_aliases={0: 0},
+        scratch_shapes=[pltpu.SemaphoreType.DMA((n_head,))],
         compiler_params=params,
         name="lay_second",
     )(out, swapped)

time: 90.1 us -> 89.6 us (level)
  waiting for transfers between devices: 22.1 us -> 23.8 us
  starting transfers between devices: 27.6 us -> 26.1 us
    ppermute x3, waiting for transfers between devices: 5.66 us -> 7.37 us  [local(): lax.ppermute(partial, ('z_hi', 'z_lo'), [(ring[i], ring[(i + hop) % N_FAR...]
where the time goes in v11:
time: 89.6 us; the launch traced here: 89.3 us
  starting transfers between devices  26.1 us (29%)
  waiting for transfers between devices  23.8 us (27%)
  Pallas kernels  20.1 us (22%)
  blocking collectives  17.7 us (20%)
  other arithmetic  1.41 us (2%)
    all_to_all x1, blocking collectives, local(): lax.all_to_all(orth, slots, split_axis=0, concat_axis=0, tiled=True)  17.7 us
    all_to_all x1, waiting for transfers between devices, local(): lax.all_to_all(second.reshape(n_head, part, width), 'head', split_axis=0,...  8.9 us
    ppermute x3, starting transfers between devices, local(): lax.ppermute(partial, ('z_hi', 'z_lo'), [(ring[i], ring[(i + hop) % N_FAR...  8.12 us
    ppermute x3, waiting for transfers between devices, local(): lax.ppermute(partial, ('z_hi', 'z_lo'), [(ring[i], ring[(i + hop) % N_FAR...  7.37 us
    all_to_all x1, waiting for transfers between devices, local(): lax.all_to_all(chip_sum, slots, split_axis=0, concat_axis=0, tiled=True)  5.81 us
    ppermute x3, starting transfers between devices, local(): lax.ppermute(firsts[hop], 'head', [(i, (i + hop) % n_head) for i in range...  4.89 us
    pallas_call x1, Pallas kernels, local(): pl.pallas_call(first_kernel, grid_spec=pltpu.PrefetchScalarGridSpec(num_s...  4.84 us
    all_to_all x1, starting transfers between devices, local(): lax.all_to_all(second.reshape(n_head, part, width), 'head', split_axis=0,...  4.01 us
  transfers between devices with their start and end apart: 10, of which 5 were waited for; matrix products, arithmetic and copies ran while one was open for 0% of the time, Pallas kernels for 13%

profile of v11, /device:TPU:1, one launch (start us, length us, event | category | flops | bytes accessed | tf_op | source)
XLA Modules:
  0.0 89.3 jit_solution(5049928851731492442)
XLA Ops:
  0.0 3.6 %grads_sent.1 = (bf16[8,256,256]{2,1,0:T(8,128)(2,1)S(1)}, bf16[2,256,256]{2,1,0:T(8,128)(2,1)S(1)}) custom-call(s32[1]{0:T(128)} %bitcast.1.core_ref, s32[1]{0:T(128)} %bitcast.2.far_ref, bf16[256,1280]{1,0:T(8,128)(2,1)} %refs_0_.3, bf16[256,1280]{1,0:T(8,128)(2,1)} %refs_1_.3, f32[5,256]{1,0:T(8,128)} %refs_2_.3, f32[5,256,256]{2,1,0:T(8,128)} %g_ref.3, ...), custom_call_target="tpu_custom_call" | custom-call | tf_op jit(solution)/shard_map/grads_sent/pallas_call | solution.py:302
  3.6 3.4 %collective-permute-start = (bf16[8,256,256]{2,1,0:T(8,128)(2,1)S(1)}, bf16[8,256,256]{2,1,0:T(8,128)(2,1)S(1)}, u32[]{:S(2)}, u32[]{:S(2)}) collective-permute-start(bf16[8,256,256]{2,1,0:T(8,128)(2,1)S(1)} %get-tuple-element.28), channel_id=1, source_target_pairs={{0,1},{1,0},{2,3},{3,2},{4,5},{5,4},{6,7},{7,6},{8,9},{9,8},{10,11... | collective-permute-start | bytes 3145736 | tf_op jit(solution)/shard_map/ppermute | solution.py:317
  6.9 2.6 %grads_kept.1 = bf16[8,256,256]{2,1,0:T(8,128)(2,1)S(1)} custom-call(s32[1]{0:T(128)} %bitcast.1.core_ref, s32[1]{0:T(128)} %bitcast.2.far_ref, bf16[256,1280]{1,0:T(8,128)(2,1)} %refs_0_.3, bf16[256,1280]{1,0:T(8,128)(2,1)} %refs_1_.3, f32[5,256]{1,0:T(8,128)} %refs_2_.3, f32[5,256,256]{2,1,0:T(8,128)} %g_ref.3, f32[5,256,256]{2,1,0:T(8,128)} %u_ref.3, ...), custom_call_target="tpu_custom_call" | custom-call | tf_op jit(solution)/shard_map/grads_kept/pallas_call | solution.py:318
  9.5 0.0 collective-permute-done
  9.5 1.3 %add_convert_fusion = bf16[8,256,256]{2,1,0:T(8,128)(2,1)} fusion(bf16[8,256,256]{2,1,0:T(8,128)(2,1)S(1)} %collective-permute-done, bf16[8,256,256]{2,1,0:T(8,128)(2,1)S(1)} %grads_kept.1), kind=kLoop, calls=%fused_computation | loop fusion | flops 2097152 | bytes 3145728 | tf_op jit(solution)/shard_map/convert_element_type | solution.py:351
  10.8 3.8 %all-to-all-start = ((bf16[8,256,256]{2,1,0:T(8,128)(2,1)}), bf16[8,256,256]{2,1,0:T(8,128)(2,1)S(1)}, u32[]{:S(2)}, u32[]{:S(2)}) async-start(bf16[8,256,256]{2,1,0:T(8,128)(2,1)} %add_convert_fusion), calls=%async_computation | async-start | bytes 2097152 | tf_op jit(solution)/shard_map/all_to_all | solution.py:353
  14.6 4.8 %first.1 = (bf16[64,1280]{1,0:T(8,128)(2,1)S(1)}, bf16[64,1280]{1,0:T(8,128)(2,1)S(1)}, bf16[64,1280]{1,0:T(8,128)(2,1)S(1)}, bf16[64,1280]{1,0:T(8,128)(2,1)S(1)}) custom-call(s32[1]{0:T(128)} %bitcast.place_ref, bf16[2,256,1280]{2,1,0:T(8,128)(2,1)} %q_ref.3, f32[5,256,256]{2,1,0:T(8,128)} %g_ref.3, f32[5,256,256]{2,1,0:T(8,128)} %u_ref.3, ...), custom_call_target="tpu_custom_call" | custom-call | tf_op jit(solution)/shard_map/first/pallas_call | solution.py:333
  19.5 1.3 %collective-permute-start.4 = (bf16[64,1280]{1,0:T(8,128)(2,1)S(1)}, bf16[64,1280]{1,0:T(8,128)(2,1)S(1)}, u32[]{:S(2)}, u32[]{:S(2)}) collective-permute-start(bf16[64,1280]{1,0:T(8,128)(2,1)S(1)} %get-tuple-element.30), channel_id=1, source_target_pairs={{0,64},{64,128},{128,192},{192,0},{1,65},{65,129},{129,193},{193,1... | collective-permute-start | bytes 491528 | tf_op jit(solution)/shard_map/ppermute | solution.py:347
  20.8 2.4 %collective-permute-start.5 = (bf16[64,1280]{1,0:T(8,128)(2,1)S(1)}, bf16[64,1280]{1,0:T(8,128)(2,1)S(1)}, u32[]{:S(2)}, u32[]{:S(2)}) collective-permute-start(bf16[64,1280]{1,0:T(8,128)(2,1)S(1)} %get-tuple-element.31), channel_id=1, source_target_pairs={{0,128},{64,192},{128,0},{192,64},{1,129},{65,193},{129,1},{193,65... | collective-permute-start | bytes 491528 | tf_op jit(solution)/shard_map/ppermute | solution.py:347
  23.2 1.2 %collective-permute-start.6 = (bf16[64,1280]{1,0:T(8,128)(2,1)S(1)}, bf16[64,1280]{1,0:T(8,128)(2,1)S(1)}, u32[]{:S(2)}, u32[]{:S(2)}) collective-permute-start(bf16[64,1280]{1,0:T(8,128)(2,1)S(1)} %get-tuple-element.32), channel_id=1, source_target_pairs={{0,192},{64,0},{128,64},{192,128},{1,193},{65,1},{129,65},{193,129... | collective-permute-start | bytes 491528 | tf_op jit(solution)/shard_map/ppermute | solution.py:347
  24.4 5.8 %all-to-all-done = bf16[8,256,256]{2,1,0:T(8,128)(2,1)S(1)} async-done(((bf16[8,256,256]{2,1,0:T(8,128)(2,1)}), bf16[8,256,256]{2,1,0:T(8,128)(2,1)S(1)}, u32[]{:S(2)}, u32[]{:S(2)}) %all-to-all-start) | async-done | bytes 1048608 | tf_op jit(solution)/shard_map/all_to_all | solution.py:353
  30.2 0.1 reduce_sum.12.refs_0_
  30.3 5.4 %collective-permute-start.1 = (bf16[256,256]{1,0:T(8,128)(2,1)S(1)}, bf16[256,256]{1,0:T(8,128)(2,1)S(1)}, u32[]{:S(2)}, u32[]{:S(2)}) collective-permute-start(bf16[256,256]{1,0:T(8,128)(2,1)S(1)} %reduce_sum.12.refs_0_), channel_id=1, source_target_pairs={{0,40},{16,56},{40,0},{56,16},{8,32},{24,48},{32,8},{48,24},{1,41}... | collective-permute-start | bytes 393224 | tf_op jit(solution)/shard_map/ppermute | solution.py:357
  35.8 1.2 %collective-permute-start.2 = (bf16[256,256]{1,0:T(8,128)(2,1)S(1)}, bf16[256,256]{1,0:T(8,128)(2,1)S(1)}, u32[]{:S(2)}, u32[]{:S(2)}) collective-permute-start(bf16[256,256]{1,0:T(8,128)(2,1)S(1)} %reduce_sum.12.refs_0_), channel_id=1, source_target_pairs={{0,16},{16,40},{40,56},{56,0},{8,24},{24,32},{32,48},{48,8},{1,17}... | collective-permute-start | bytes 393224 | tf_op jit(solution)/shard_map/ppermute | solution.py:357
  36.9 0.0 collective-permute-done.4.refs_1_
  37.0 1.5 %collective-permute-start.3 = (bf16[256,256]{1,0:T(8,128)(2,1)S(1)}, bf16[256,256]{1,0:T(8,128)(2,1)S(1)}, u32[]{:S(2)}, u32[]{:S(2)}) collective-permute-start(bf16[256,256]{1,0:T(8,128)(2,1)S(1)} %reduce_sum.12.refs_0_), channel_id=1, source_target_pairs={{0,56},{16,0},{40,16},{56,40},{8,48},{24,8},{32,24},{48,32},{1,57}... | collective-permute-start | bytes 393224 | tf_op jit(solution)/shard_map/ppermute | solution.py:357
  38.4 2.3 %stage.1 = (bf16[256,1280]{1,0:T(8,128)(2,1)S(1)}, f32[5,256,256]{2,1,0:T(8,128)S(1)}, f32[5,256,256]{2,1,0:T(8,128)S(1)}, f32[5,256,256]{2,1,0:T(8,128)S(1)}) custom-call(bf16[2,256,1280]{2,1,0:T(8,128)(2,1)} %q_ref.3, f32[5,256,256]{2,1,0:T(8,128)} %g_ref.3, f32[5,256,256]{2,1,0:T(8,128)} %u_ref.3, f32[5,256,256]{2,1,0:T(8,128)} %d_ref.3), custom_call_target="tpu_custom_call" | custom-call | tf_op jit(solution)/shard_map/stage/pallas_call | solution.py:364
  40.8 0.0 collective-permute-done.5.refs_2_
  40.8 0.0 collective-permute-done.6.refs_3_
  40.8 0.0 collective-permute-done.1.refs_1_
  40.8 7.3 %collective-permute-done.2.refs_2_ = bf16[256,256]{1,0:T(8,128)(2,1)S(1)} collective-permute-done((bf16[256,256]{1,0:T(8,128)(2,1)S(1)}, bf16[256,256]{1,0:T(8,128)(2,1)S(1)}, u32[]{:S(2)}, u32[]{:S(2)}) %collective-permute-start.2) | collective-permute-done | bytes 131104 | tf_op jit(solution)/shard_map/ppermute | solution.py:357
  48.1 0.1 collective-permute-done.3.refs_3_
  48.2 2.2 %orthogonalize.1 = bf16[8,256,256]{2,1,0:T(8,128)(2,1)S(1)} custom-call(bf16[256,256]{1,0:T(8,128)(2,1)S(1)} %reduce_sum.12.refs_0_, bf16[256,256]{1,0:T(8,128)(2,1)S(1)} %collective-permute-done.1.refs_1_, bf16[256,256]{1,0:T(8,128)(2,1)S(1)} %collective-permute-done.2.refs_2_, bf16[256,256]{1,0:T(8,128)(2,1)S(1)} %collective-permute-done.3.refs_3_), custom_call_target="tpu_custom_call" | custom-call | tf_op jit(solution)/shard_map/orthogonalize/pallas_call | solution.py:376
  50.4 17.7 %all_to_all.15.mine_ref = bf16[8,256,256]{2,1,0:T(8,128)(2,1)S(1)} all-to-all(bf16[8,256,256]{2,1,0:T(8,128)(2,1)S(1)} %orthogonalize.1), channel_id=1, replica_groups=mesh['head'=4,'z_hi'=4,'z_lo'=2,'y'=4,'core'=2] {'y','z_lo'}, dimensions={0} | all-to-all | bytes 2097152 | tf_op jit(solution)/shard_map/all_to_all | solution.py:382
  68.1 1.9 %collective-permute-start.7 = (bf16[8,256,256]{2,1,0:T(8,128)(2,1)S(1)}, bf16[8,256,256]{2,1,0:T(8,128)(2,1)S(1)}, u32[]{:S(2)}, u32[]{:S(2)}) collective-permute-start(bf16[8,256,256]{2,1,0:T(8,128)(2,1)S(1)} %all_to_all.15.mine_ref), channel_id=1, source_target_pairs={{0,1},{1,0},{2,3},{3,2},{4,5},{5,4},{6,7},{7,6},{8,9},{9,8},{10,11... | collective-permute-start | bytes 3145736 | tf_op jit(solution)/shard_map/ppermute | solution.py:383
  70.0 0.6 second_own.1.own_ref
  70.6 1.7 %collective-permute-done.7.other_ref = bf16[8,256,256]{2,1,0:T(8,128)(2,1)S(1)} collective-permute-done((bf16[8,256,256]{2,1,0:T(8,128)(2,1)S(1)}, bf16[8,256,256]{2,1,0:T(8,128)(2,1)S(1)}, u32[]{:S(2)}, u32[]{:S(2)}) %collective-permute-start.7) | collective-permute-done | bytes 1048608 | tf_op jit(solution)/shard_map/ppermute | solution.py:383
  72.3 1.7 %second_rest.1 = bf16[256,1280]{1,0:T(8,128)(2,1)} custom-call(s32[1]{0:T(128)} %bitcast.1.core_ref, s32[1]{0:T(128)} %bitcast.2.far_ref, bf16[256,1280]{1,0:T(8,128)(2,1)S(1)} %get-tuple-element.41.q_ref, f32[5,256,256]{2,1,0:T(8,128)S(1)} %get-tuple-element.42.g_ref, f32[5,256,256]{2,1,0:T(8,128)S(1)} %get-tuple-element.43.u_ref, ...), custom_call_target="tpu_custom_call" | custom-call | tf_op jit(solution)/shard_map/second_rest/pallas_call | solution.py:399
  73.9 4.0 %all-to-all-start.2 = ((bf16[4,64,1280]{2,1,0:T(8,128)(2,1)}), bf16[4,64,1280]{2,1,0:T(8,128)(2,1)S(1)}, u32[]{:S(2)}, u32[]{:S(2)}) async-start(bf16[4,64,1280]{2,1,0:T(8,128)(2,1)} %bitcast.3), calls=%async_computation.2 | async-start | bytes 1310720 | tf_op jit(solution)/shard_map/all_to_all | solution.py:412
  77.9 1.4 %lay_first.1.buf_ref = bf16[2,64,5120]{2,1,0:T(8,128)(2,1)} custom-call(s32[1]{0:T(128)} %bitcast.place_ref, bf16[64,1280]{1,0:T(8,128)(2,1)S(1)} %get-tuple-element.37.refs_0_, bf16[64,1280]{1,0:T(8,128)(2,1)S(1)} %collective-permute-done.4.refs_1_, bf16[64,1280]{1,0:T(8,128)(2,1)S(1)} %collective-permute-done.5.refs_2_, ...), custom_call_target="tpu_custom_call" | custom-call | tf_op jit(solution)/shard_map/lay_first/pallas_call | solution.py:414
  79.4 8.9 %all-to-all-done.2.rows_ref = bf16[4,64,1280]{2,1,0:T(8,128)(2,1)S(1)} async-done(((bf16[4,64,1280]{2,1,0:T(8,128)(2,1)}), bf16[4,64,1280]{2,1,0:T(8,128)(2,1)S(1)}, u32[]{:S(2)}, u32[]{:S(2)}) %all-to-all-start.2) | async-done | bytes 655392 | tf_op jit(solution)/shard_map/all_to_all | solution.py:412
  88.3 0.9 lay_second.1
Async XLA Ops:
  3.6 6.0 %collective-permute-start = (bf16[8,256,256]{2,1,0:T(8,128)(2,1)S(1)}, bf16[8,256,256]{2,1,0:T(8,128)(2,1)S(1)}, u32[]{:S(2)}, u32[]{:S(2)}) collective-permute-start(bf16[8,256,256]{2,1,0:T(8,128)(2,1)S(1)} %get-tuple-element.28), channel_id=1, source_target_pairs={{0,1},{1,0},{2,3},{3,2},{4,5},{5,4},{6,7},{7,6},{8,9},{9,8},{10,11... | collective-permute-start | bytes 3145736 | tf_op jit(solution)/shard_map/ppermute | solution.py:317
  10.8 19.4 %all-to-all-start = ((bf16[8,256,256]{2,1,0:T(8,128)(2,1)}), bf16[8,256,256]{2,1,0:T(8,128)(2,1)S(1)}, u32[]{:S(2)}, u32[]{:S(2)}) async-start(bf16[8,256,256]{2,1,0:T(8,128)(2,1)} %add_convert_fusion), calls=%async_computation | async-start | bytes 2097152 | tf_op jit(solution)/shard_map/all_to_all | solution.py:353
  19.5 17.5 %collective-permute-start.4 = (bf16[64,1280]{1,0:T(8,128)(2,1)S(1)}, bf16[64,1280]{1,0:T(8,128)(2,1)S(1)}, u32[]{:S(2)}, u32[]{:S(2)}) collective-permute-start(bf16[64,1280]{1,0:T(8,128)(2,1)S(1)} %get-tuple-element.30), channel_id=1, source_target_pairs={{0,64},{64,128},{128,192},{192,0},{1,65},{65,129},{129,193},{193,1... | collective-permute-start | bytes 491528 | tf_op jit(solution)/shard_map/ppermute | solution.py:347
  20.8 20.0 %collective-permute-start.5 = (bf16[64,1280]{1,0:T(8,128)(2,1)S(1)}, bf16[64,1280]{1,0:T(8,128)(2,1)S(1)}, u32[]{:S(2)}, u32[]{:S(2)}) collective-permute-start(bf16[64,1280]{1,0:T(8,128)(2,1)S(1)} %get-tuple-element.31), channel_id=1, source_target_pairs={{0,128},{64,192},{128,0},{192,64},{1,129},{65,193},{129,1},{193,65... | collective-permute-start | bytes 491528 | tf_op jit(solution)/shard_map/ppermute | solution.py:347
  23.2 17.6 %collective-permute-start.6 = (bf16[64,1280]{1,0:T(8,128)(2,1)S(1)}, bf16[64,1280]{1,0:T(8,128)(2,1)S(1)}, u32[]{:S(2)}, u32[]{:S(2)}) collective-permute-start(bf16[64,1280]{1,0:T(8,128)(2,1)S(1)} %get-tuple-element.32), channel_id=1, source_target_pairs={{0,192},{64,0},{128,64},{192,128},{1,193},{65,1},{129,65},{193,129... | collective-permute-start | bytes 491528 | tf_op jit(solution)/shard_map/ppermute | solution.py:347
  30.3 10.5 %collective-permute-start.1 = (bf16[256,256]{1,0:T(8,128)(2,1)S(1)}, bf16[256,256]{1,0:T(8,128)(2,1)S(1)}, u32[]{:S(2)}, u32[]{:S(2)}) collective-permute-start(bf16[256,256]{1,0:T(8,128)(2,1)S(1)} %reduce_sum.12.refs_0_), channel_id=1, source_target_pairs={{0,40},{16,56},{40,0},{56,16},{8,32},{24,48},{32,8},{48,24},{1,41}... | collective-permute-start | bytes 393224 | tf_op jit(solution)/shard_map/ppermute | solution.py:357
  35.8 12.4 %collective-permute-start.2 = (bf16[256,256]{1,0:T(8,128)(2,1)S(1)}, bf16[256,256]{1,0:T(8,128)(2,1)S(1)}, u32[]{:S(2)}, u32[]{:S(2)}) collective-permute-start(bf16[256,256]{1,0:T(8,128)(2,1)S(1)} %reduce_sum.12.refs_0_), channel_id=1, source_target_pairs={{0,16},{16,40},{40,56},{56,0},{8,24},{24,32},{32,48},{48,8},{1,17}... | collective-permute-start | bytes 393224 | tf_op jit(solution)/shard_map/ppermute | solution.py:357
  37.0 11.2 %collective-permute-start.3 = (bf16[256,256]{1,0:T(8,128)(2,1)S(1)}, bf16[256,256]{1,0:T(8,128)(2,1)S(1)}, u32[]{:S(2)}, u32[]{:S(2)}) collective-permute-start(bf16[256,256]{1,0:T(8,128)(2,1)S(1)} %reduce_sum.12.refs_0_), channel_id=1, source_target_pairs={{0,56},{16,0},{40,16},{56,40},{8,48},{24,8},{32,24},{48,32},{1,57}... | collective-permute-start | bytes 393224 | tf_op jit(solution)/shard_map/ppermute | solution.py:357
  68.1 4.2 %collective-permute-start.7 = (bf16[8,256,256]{2,1,0:T(8,128)(2,1)S(1)}, bf16[8,256,256]{2,1,0:T(8,128)(2,1)S(1)}, u32[]{:S(2)}, u32[]{:S(2)}) collective-permute-start(bf16[8,256,256]{2,1,0:T(8,128)(2,1)S(1)} %all_to_all.15.mine_ref), channel_id=1, source_target_pairs={{0,1},{1,0},{2,3},{3,2},{4,5},{5,4},{6,7},{7,6},{8,9},{9,8},{10,11... | collective-permute-start | bytes 3145736 | tf_op jit(solution)/shard_map/ppermute | solution.py:383
  73.9 14.3 %all-to-all-start.2 = ((bf16[4,64,1280]{2,1,0:T(8,128)(2,1)}), bf16[4,64,1280]{2,1,0:T(8,128)(2,1)S(1)}, u32[]{:S(2)}, u32[]{:S(2)}) async-start(bf16[4,64,1280]{2,1,0:T(8,128)(2,1)} %bitcast.3), calls=%async_computation.2 | async-start | bytes 1310720 | tf_op jit(solution)/shard_map/all_to_all | solution.py:412

commit v12 on v11

--- a/solution.py
+++ b/solution.py
@@ -63,28 +63,33 @@
     rates, keys, values, gates, ups, downs, rate_sem, sems = scratch
     rate_copy = pltpu.make_async_copy(rate_ref, rates, rate_sem)
     rate_copy.start()
+    cols = pl.ds(heads[0] * HD, len(heads) * HD)
+    wide = [
+        pltpu.make_async_copy(k_ref.at[:, cols], keys, sems.at[0, 3]),
+        pltpu.make_async_copy(v_ref.at[:, cols], values, sems.at[0, 4]),
+    ]
+    for copy in wide:
+        copy.start()
     copies = []
     for at, head in enumerate(heads):
-        cols = pl.ds(head * HD, HD)
-        pairs = (
-            (k_ref.at[:, cols], keys),
-            (v_ref.at[:, cols], values),
-            (g_ref.at[head], gates),
-            (u_ref.at[head], ups),
-            (d_ref.at[head], downs),
+        pairs = ((g_ref, gates), (u_ref, ups), (d_ref, downs))
+        copies.append(
+            [pltpu.make_async_copy(src.at[head], dst.at[at], sems.at[at, i]) for i, (src, dst) in enumerate(pairs)]
         )
-        copies.append([pltpu.make_async_copy(src, dst.at[at], sems.at[at, i]) for i, (src, dst) in enumerate(pairs)])
         for copy in copies[-1]:
             copy.start()
     rate_copy.wait()
+    for copy in wide:
+        copy.wait()
     for at, head in enumerate(heads):
         for copy in copies[at]:
             copy.wait()
+        mine = slice(at * HD, (at + 1) * HD)
         yield (
             head,
             head_grads(
-                keys[at],
-                values[at],
+                keys[:, mine],
+                values[:, mine],
                 rates[head : head + 1, :],
                 gates[at].astype(BF16),
                 ups[at].astype(BF16),
@@ -289,8 +294,8 @@
     def copy_scratch(heads):
         return [
             pltpu.VMEM((HEADS_HERE, rows), F32),
-            pltpu.VMEM((heads, rows, HD), BF16),
-            pltpu.VMEM((heads, rows, HD), BF16),
+            pltpu.VMEM((rows, heads * HD), BF16),
+            pltpu.VMEM((rows, heads * HD), BF16),
             pltpu.VMEM((heads, HD, HD), F32),
             pltpu.VMEM((heads, HD, HD), F32),
             pltpu.VMEM((heads, HD, HD), F32),

time: 89.6 us -> 89.6 us (level)
  no operation moved by 1% of the time
where the time goes in v12:
time: 89.6 us; the launch traced here: 89.3 us
  starting transfers between devices  26.1 us (29%)
  waiting for transfers between devices  23.8 us (27%)
  Pallas kernels  20 us (22%)
  blocking collectives  17.7 us (20%)
  other arithmetic  1.41 us (2%)
    all_to_all x1, blocking collectives, local(): lax.all_to_all(orth, slots, split_axis=0, concat_axis=0, tiled=True)  17.7 us
    all_to_all x1, waiting for transfers between devices, local(): lax.all_to_all(second.reshape(n_head, part, width), 'head', split_axis=0,...  8.9 us
    ppermute x3, starting transfers between devices, local(): lax.ppermute(partial, ('z_hi', 'z_lo'), [(ring[i], ring[(i + hop) % N_FAR...  8.13 us
    ppermute x3, waiting for transfers between devices, local(): lax.ppermute(partial, ('z_hi', 'z_lo'), [(ring[i], ring[(i + hop) % N_FAR...  7.39 us
    all_to_all x1, waiting for transfers between devices, local(): lax.all_to_all(chip_sum, slots, split_axis=0, concat_axis=0, tiled=True)  5.81 us
    ppermute x3, starting transfers between devices, local(): lax.ppermute(firsts[hop], 'head', [(i, (i + hop) % n_head) for i in range...  4.89 us
    pallas_call x1, Pallas kernels, local(): pl.pallas_call(first_kernel, grid_spec=pltpu.PrefetchScalarGridSpec(num_s...  4.84 us
    all_to_all x1, starting transfers between devices, local(): lax.all_to_all(second.reshape(n_head, part, width), 'head', split_axis=0,...  4.02 us
  transfers between devices with their start and end apart: 10, of which 5 were waited for; matrix products, arithmetic and copies ran while one was open for 0% of the time, Pallas kernels for 13%

profile of v12, /device:TPU:1, one launch (start us, length us, event | category | flops | bytes accessed | tf_op | source)
XLA Modules:
  0.0 89.3 jit_solution(1651928802079500734)
XLA Ops:
  0.0 3.5 %grads_sent.1 = (bf16[8,256,256]{2,1,0:T(8,128)(2,1)S(1)}, bf16[2,256,256]{2,1,0:T(8,128)(2,1)S(1)}) custom-call(s32[1]{0:T(128)} %bitcast.1.core_ref, s32[1]{0:T(128)} %bitcast.2.far_ref, bf16[256,1280]{1,0:T(8,128)(2,1)} %refs_0_.3, bf16[256,1280]{1,0:T(8,128)(2,1)} %refs_1_.3, f32[5,256]{1,0:T(8,128)} %refs_2_.3, f32[5,256,256]{2,1,0:T(8,128)} %g_ref.3, ...), custom_call_target="tpu_custom_call" | custom-call | tf_op jit(solution)/shard_map/grads_sent/pallas_call | solution.py:307
  3.5 3.4 %collective-permute-start = (bf16[8,256,256]{2,1,0:T(8,128)(2,1)S(1)}, bf16[8,256,256]{2,1,0:T(8,128)(2,1)S(1)}, u32[]{:S(2)}, u32[]{:S(2)}) collective-permute-start(bf16[8,256,256]{2,1,0:T(8,128)(2,1)S(1)} %get-tuple-element.28), channel_id=1, source_target_pairs={{0,1},{1,0},{2,3},{3,2},{4,5},{5,4},{6,7},{7,6},{8,9},{9,8},{10,11... | collective-permute-start | bytes 3145736 | tf_op jit(solution)/shard_map/ppermute | solution.py:322
  6.9 2.6 %grads_kept.1 = bf16[8,256,256]{2,1,0:T(8,128)(2,1)S(1)} custom-call(s32[1]{0:T(128)} %bitcast.1.core_ref, s32[1]{0:T(128)} %bitcast.2.far_ref, bf16[256,1280]{1,0:T(8,128)(2,1)} %refs_0_.3, bf16[256,1280]{1,0:T(8,128)(2,1)} %refs_1_.3, f32[5,256]{1,0:T(8,128)} %refs_2_.3, f32[5,256,256]{2,1,0:T(8,128)} %g_ref.3, f32[5,256,256]{2,1,0:T(8,128)} %u_ref.3, ...), custom_call_target="tpu_custom_call" | custom-call | tf_op jit(solution)/shard_map/grads_kept/pallas_call | solution.py:323
  9.5 0.0 collective-permute-done
  9.5 1.3 %add_convert_fusion = bf16[8,256,256]{2,1,0:T(8,128)(2,1)} fusion(bf16[8,256,256]{2,1,0:T(8,128)(2,1)S(1)} %collective-permute-done, bf16[8,256,256]{2,1,0:T(8,128)(2,1)S(1)} %grads_kept.1), kind=kLoop, calls=%fused_computation | loop fusion | flops 2097152 | bytes 3145728 | tf_op jit(solution)/shard_map/convert_element_type | solution.py:356
  10.8 3.8 %all-to-all-start = ((bf16[8,256,256]{2,1,0:T(8,128)(2,1)}), bf16[8,256,256]{2,1,0:T(8,128)(2,1)S(1)}, u32[]{:S(2)}, u32[]{:S(2)}) async-start(bf16[8,256,256]{2,1,0:T(8,128)(2,1)} %add_convert_fusion), calls=%async_computation | async-start | bytes 2097152 | tf_op jit(solution)/shard_map/all_to_all | solution.py:358
  14.6 4.8 %first.1 = (bf16[64,1280]{1,0:T(8,128)(2,1)S(1)}, bf16[64,1280]{1,0:T(8,128)(2,1)S(1)}, bf16[64,1280]{1,0:T(8,128)(2,1)S(1)}, bf16[64,1280]{1,0:T(8,128)(2,1)S(1)}) custom-call(s32[1]{0:T(128)} %bitcast.place_ref, bf16[2,256,1280]{2,1,0:T(8,128)(2,1)} %q_ref.3, f32[5,256,256]{2,1,0:T(8,128)} %g_ref.3, f32[5,256,256]{2,1,0:T(8,128)} %u_ref.3, ...), custom_call_target="tpu_custom_call" | custom-call | tf_op jit(solution)/shard_map/first/pallas_call | solution.py:338
  19.5 1.3 %collective-permute-start.4 = (bf16[64,1280]{1,0:T(8,128)(2,1)S(1)}, bf16[64,1280]{1,0:T(8,128)(2,1)S(1)}, u32[]{:S(2)}, u32[]{:S(2)}) collective-permute-start(bf16[64,1280]{1,0:T(8,128)(2,1)S(1)} %get-tuple-element.30), channel_id=1, source_target_pairs={{0,64},{64,128},{128,192},{192,0},{1,65},{65,129},{129,193},{193,1... | collective-permute-start | bytes 491528 | tf_op jit(solution)/shard_map/ppermute | solution.py:352
  20.7 2.4 %collective-permute-start.5 = (bf16[64,1280]{1,0:T(8,128)(2,1)S(1)}, bf16[64,1280]{1,0:T(8,128)(2,1)S(1)}, u32[]{:S(2)}, u32[]{:S(2)}) collective-permute-start(bf16[64,1280]{1,0:T(8,128)(2,1)S(1)} %get-tuple-element.31), channel_id=1, source_target_pairs={{0,128},{64,192},{128,0},{192,64},{1,129},{65,193},{129,1},{193,65... | collective-permute-start | bytes 491528 | tf_op jit(solution)/shard_map/ppermute | solution.py:352
  23.2 1.2 %collective-permute-start.6 = (bf16[64,1280]{1,0:T(8,128)(2,1)S(1)}, bf16[64,1280]{1,0:T(8,128)(2,1)S(1)}, u32[]{:S(2)}, u32[]{:S(2)}) collective-permute-start(bf16[64,1280]{1,0:T(8,128)(2,1)S(1)} %get-tuple-element.32), channel_id=1, source_target_pairs={{0,192},{64,0},{128,64},{192,128},{1,193},{65,1},{129,65},{193,129... | collective-permute-start | bytes 491528 | tf_op jit(solution)/shard_map/ppermute | solution.py:352
  24.3 5.8 %all-to-all-done = bf16[8,256,256]{2,1,0:T(8,128)(2,1)S(1)} async-done(((bf16[8,256,256]{2,1,0:T(8,128)(2,1)}), bf16[8,256,256]{2,1,0:T(8,128)(2,1)S(1)}, u32[]{:S(2)}, u32[]{:S(2)}) %all-to-all-start) | async-done | bytes 1048608 | tf_op jit(solution)/shard_map/all_to_all | solution.py:358
  30.2 0.1 reduce_sum.12.refs_0_
  30.3 5.5 %collective-permute-start.1 = (bf16[256,256]{1,0:T(8,128)(2,1)S(1)}, bf16[256,256]{1,0:T(8,128)(2,1)S(1)}, u32[]{:S(2)}, u32[]{:S(2)}) collective-permute-start(bf16[256,256]{1,0:T(8,128)(2,1)S(1)} %reduce_sum.12.refs_0_), channel_id=1, source_target_pairs={{0,40},{16,56},{40,0},{56,16},{8,32},{24,48},{32,8},{48,24},{1,41}... | collective-permute-start | bytes 393224 | tf_op jit(solution)/shard_map/ppermute | solution.py:362
  35.8 1.2 %collective-permute-start.2 = (bf16[256,256]{1,0:T(8,128)(2,1)S(1)}, bf16[256,256]{1,0:T(8,128)(2,1)S(1)}, u32[]{:S(2)}, u32[]{:S(2)}) collective-permute-start(bf16[256,256]{1,0:T(8,128)(2,1)S(1)} %reduce_sum.12.refs_0_), channel_id=1, source_target_pairs={{0,16},{16,40},{40,56},{56,0},{8,24},{24,32},{32,48},{48,8},{1,17}... | collective-permute-start | bytes 393224 | tf_op jit(solution)/shard_map/ppermute | solution.py:362
  36.9 0.0 collective-permute-done.4.refs_1_
  36.9 1.5 %collective-permute-start.3 = (bf16[256,256]{1,0:T(8,128)(2,1)S(1)}, bf16[256,256]{1,0:T(8,128)(2,1)S(1)}, u32[]{:S(2)}, u32[]{:S(2)}) collective-permute-start(bf16[256,256]{1,0:T(8,128)(2,1)S(1)} %reduce_sum.12.refs_0_), channel_id=1, source_target_pairs={{0,56},{16,0},{40,16},{56,40},{8,48},{24,8},{32,24},{48,32},{1,57}... | collective-permute-start | bytes 393224 | tf_op jit(solution)/shard_map/ppermute | solution.py:362
  38.4 2.3 %stage.1 = (bf16[256,1280]{1,0:T(8,128)(2,1)S(1)}, f32[5,256,256]{2,1,0:T(8,128)S(1)}, f32[5,256,256]{2,1,0:T(8,128)S(1)}, f32[5,256,256]{2,1,0:T(8,128)S(1)}) custom-call(bf16[2,256,1280]{2,1,0:T(8,128)(2,1)} %q_ref.3, f32[5,256,256]{2,1,0:T(8,128)} %g_ref.3, f32[5,256,256]{2,1,0:T(8,128)} %u_ref.3, f32[5,256,256]{2,1,0:T(8,128)} %d_ref.3), custom_call_target="tpu_custom_call" | custom-call | tf_op jit(solution)/shard_map/stage/pallas_call | solution.py:369
  40.8 0.0 collective-permute-done.5.refs_2_
  40.8 0.0 collective-permute-done.6.refs_3_
  40.8 0.0 collective-permute-done.1.refs_1_
  40.8 7.3 %collective-permute-done.2.refs_2_ = bf16[256,256]{1,0:T(8,128)(2,1)S(1)} collective-permute-done((bf16[256,256]{1,0:T(8,128)(2,1)S(1)}, bf16[256,256]{1,0:T(8,128)(2,1)S(1)}, u32[]{:S(2)}, u32[]{:S(2)}) %collective-permute-start.2) | collective-permute-done | bytes 131104 | tf_op jit(solution)/shard_map/ppermute | solution.py:362
  48.1 0.1 collective-permute-done.3.refs_3_
  48.2 2.2 %orthogonalize.1 = bf16[8,256,256]{2,1,0:T(8,128)(2,1)S(1)} custom-call(bf16[256,256]{1,0:T(8,128)(2,1)S(1)} %reduce_sum.12.refs_0_, bf16[256,256]{1,0:T(8,128)(2,1)S(1)} %collective-permute-done.1.refs_1_, bf16[256,256]{1,0:T(8,128)(2,1)S(1)} %collective-permute-done.2.refs_2_, bf16[256,256]{1,0:T(8,128)(2,1)S(1)} %collective-permute-done.3.refs_3_), custom_call_target="tpu_custom_call" | custom-call | tf_op jit(solution)/shard_map/orthogonalize/pallas_call | solution.py:381
  50.4 17.7 %all_to_all.15.mine_ref = bf16[8,256,256]{2,1,0:T(8,128)(2,1)S(1)} all-to-all(bf16[8,256,256]{2,1,0:T(8,128)(2,1)S(1)} %orthogonalize.1), channel_id=1, replica_groups=mesh['head'=4,'z_hi'=4,'z_lo'=2,'y'=4,'core'=2] {'y','z_lo'}, dimensions={0} | all-to-all | bytes 2097152 | tf_op jit(solution)/shard_map/all_to_all | solution.py:387
  68.1 1.9 %collective-permute-start.7 = (bf16[8,256,256]{2,1,0:T(8,128)(2,1)S(1)}, bf16[8,256,256]{2,1,0:T(8,128)(2,1)S(1)}, u32[]{:S(2)}, u32[]{:S(2)}) collective-permute-start(bf16[8,256,256]{2,1,0:T(8,128)(2,1)S(1)} %all_to_all.15.mine_ref), channel_id=1, source_target_pairs={{0,1},{1,0},{2,3},{3,2},{4,5},{5,4},{6,7},{7,6},{8,9},{9,8},{10,11... | collective-permute-start | bytes 3145736 | tf_op jit(solution)/shard_map/ppermute | solution.py:388
  70.0 0.6 second_own.1.own_ref
  70.5 1.7 %collective-permute-done.7.other_ref = bf16[8,256,256]{2,1,0:T(8,128)(2,1)S(1)} collective-permute-done((bf16[8,256,256]{2,1,0:T(8,128)(2,1)S(1)}, bf16[8,256,256]{2,1,0:T(8,128)(2,1)S(1)}, u32[]{:S(2)}, u32[]{:S(2)}) %collective-permute-start.7) | collective-permute-done | bytes 1048608 | tf_op jit(solution)/shard_map/ppermute | solution.py:388
  72.2 1.7 %second_rest.1 = bf16[256,1280]{1,0:T(8,128)(2,1)} custom-call(s32[1]{0:T(128)} %bitcast.1.core_ref, s32[1]{0:T(128)} %bitcast.2.far_ref, bf16[256,1280]{1,0:T(8,128)(2,1)S(1)} %get-tuple-element.41.q_ref, f32[5,256,256]{2,1,0:T(8,128)S(1)} %get-tuple-element.42.g_ref, f32[5,256,256]{2,1,0:T(8,128)S(1)} %get-tuple-element.43.u_ref, ...), custom_call_target="tpu_custom_call" | custom-call | tf_op jit(solution)/shard_map/second_rest/pallas_call | solution.py:404
  73.9 4.0 %all-to-all-start.2 = ((bf16[4,64,1280]{2,1,0:T(8,128)(2,1)}), bf16[4,64,1280]{2,1,0:T(8,128)(2,1)S(1)}, u32[]{:S(2)}, u32[]{:S(2)}) async-start(bf16[4,64,1280]{2,1,0:T(8,128)(2,1)} %bitcast.3), calls=%async_computation.2 | async-start | bytes 1310720 | tf_op jit(solution)/shard_map/all_to_all | solution.py:417
  77.9 1.4 %lay_first.1.buf_ref = bf16[2,64,5120]{2,1,0:T(8,128)(2,1)} custom-call(s32[1]{0:T(128)} %bitcast.place_ref, bf16[64,1280]{1,0:T(8,128)(2,1)S(1)} %get-tuple-element.37.refs_0_, bf16[64,1280]{1,0:T(8,128)(2,1)S(1)} %collective-permute-done.4.refs_1_, bf16[64,1280]{1,0:T(8,128)(2,1)S(1)} %collective-permute-done.5.refs_2_, ...), custom_call_target="tpu_custom_call" | custom-call | tf_op jit(solution)/shard_map/lay_first/pallas_call | solution.py:419
  79.4 8.9 %all-to-all-done.2.rows_ref = bf16[4,64,1280]{2,1,0:T(8,128)(2,1)S(1)} async-done(((bf16[4,64,1280]{2,1,0:T(8,128)(2,1)}), bf16[4,64,1280]{2,1,0:T(8,128)(2,1)S(1)}, u32[]{:S(2)}, u32[]{:S(2)}) %all-to-all-start.2) | async-done | bytes 655392 | tf_op jit(solution)/shard_map/all_to_all | solution.py:417
  88.3 0.9 lay_second.1
Async XLA Ops:
  3.5 6.0 %collective-permute-start = (bf16[8,256,256]{2,1,0:T(8,128)(2,1)S(1)}, bf16[8,256,256]{2,1,0:T(8,128)(2,1)S(1)}, u32[]{:S(2)}, u32[]{:S(2)}) collective-permute-start(bf16[8,256,256]{2,1,0:T(8,128)(2,1)S(1)} %get-tuple-element.28), channel_id=1, source_target_pairs={{0,1},{1,0},{2,3},{3,2},{4,5},{5,4},{6,7},{7,6},{8,9},{9,8},{10,11... | collective-permute-start | bytes 3145736 | tf_op jit(solution)/shard_map/ppermute | solution.py:322
  10.8 19.4 %all-to-all-start = ((bf16[8,256,256]{2,1,0:T(8,128)(2,1)}), bf16[8,256,256]{2,1,0:T(8,128)(2,1)S(1)}, u32[]{:S(2)}, u32[]{:S(2)}) async-start(bf16[8,256,256]{2,1,0:T(8,128)(2,1)} %add_convert_fusion), calls=%async_computation | async-start | bytes 2097152 | tf_op jit(solution)/shard_map/all_to_all | solution.py:358
  19.5 17.5 %collective-permute-start.4 = (bf16[64,1280]{1,0:T(8,128)(2,1)S(1)}, bf16[64,1280]{1,0:T(8,128)(2,1)S(1)}, u32[]{:S(2)}, u32[]{:S(2)}) collective-permute-start(bf16[64,1280]{1,0:T(8,128)(2,1)S(1)} %get-tuple-element.30), channel_id=1, source_target_pairs={{0,64},{64,128},{128,192},{192,0},{1,65},{65,129},{129,193},{193,1... | collective-permute-start | bytes 491528 | tf_op jit(solution)/shard_map/ppermute | solution.py:352
  20.7 20.1 %collective-permute-start.5 = (bf16[64,1280]{1,0:T(8,128)(2,1)S(1)}, bf16[64,1280]{1,0:T(8,128)(2,1)S(1)}, u32[]{:S(2)}, u32[]{:S(2)}) collective-permute-start(bf16[64,1280]{1,0:T(8,128)(2,1)S(1)} %get-tuple-element.31), channel_id=1, source_target_pairs={{0,128},{64,192},{128,0},{192,64},{1,129},{65,193},{129,1},{193,65... | collective-permute-start | bytes 491528 | tf_op jit(solution)/shard_map/ppermute | solution.py:352
  23.2 17.6 %collective-permute-start.6 = (bf16[64,1280]{1,0:T(8,128)(2,1)S(1)}, bf16[64,1280]{1,0:T(8,128)(2,1)S(1)}, u32[]{:S(2)}, u32[]{:S(2)}) collective-permute-start(bf16[64,1280]{1,0:T(8,128)(2,1)S(1)} %get-tuple-element.32), channel_id=1, source_target_pairs={{0,192},{64,0},{128,64},{192,128},{1,193},{65,1},{129,65},{193,129... | collective-permute-start | bytes 491528 | tf_op jit(solution)/shard_map/ppermute | solution.py:352
  30.3 10.5 %collective-permute-start.1 = (bf16[256,256]{1,0:T(8,128)(2,1)S(1)}, bf16[256,256]{1,0:T(8,128)(2,1)S(1)}, u32[]{:S(2)}, u32[]{:S(2)}) collective-permute-start(bf16[256,256]{1,0:T(8,128)(2,1)S(1)} %reduce_sum.12.refs_0_), channel_id=1, source_target_pairs={{0,40},{16,56},{40,0},{56,16},{8,32},{24,48},{32,8},{48,24},{1,41}... | collective-permute-start | bytes 393224 | tf_op jit(solution)/shard_map/ppermute | solution.py:362
  35.8 12.4 %collective-permute-start.2 = (bf16[256,256]{1,0:T(8,128)(2,1)S(1)}, bf16[256,256]{1,0:T(8,128)(2,1)S(1)}, u32[]{:S(2)}, u32[]{:S(2)}) collective-permute-start(bf16[256,256]{1,0:T(8,128)(2,1)S(1)} %reduce_sum.12.refs_0_), channel_id=1, source_target_pairs={{0,16},{16,40},{40,56},{56,0},{8,24},{24,32},{32,48},{48,8},{1,17}... | collective-permute-start | bytes 393224 | tf_op jit(solution)/shard_map/ppermute | solution.py:362
  36.9 11.3 %collective-permute-start.3 = (bf16[256,256]{1,0:T(8,128)(2,1)S(1)}, bf16[256,256]{1,0:T(8,128)(2,1)S(1)}, u32[]{:S(2)}, u32[]{:S(2)}) collective-permute-start(bf16[256,256]{1,0:T(8,128)(2,1)S(1)} %reduce_sum.12.refs_0_), channel_id=1, source_target_pairs={{0,56},{16,0},{40,16},{56,40},{8,48},{24,8},{32,24},{48,32},{1,57}... | collective-permute-start | bytes 393224 | tf_op jit(solution)/shard_map/ppermute | solution.py:362
  68.1 4.2 %collective-permute-start.7 = (bf16[8,256,256]{2,1,0:T(8,128)(2,1)S(1)}, bf16[8,256,256]{2,1,0:T(8,128)(2,1)S(1)}, u32[]{:S(2)}, u32[]{:S(2)}) collective-permute-start(bf16[8,256,256]{2,1,0:T(8,128)(2,1)S(1)} %all_to_all.15.mine_ref), channel_id=1, source_target_pairs={{0,1},{1,0},{2,3},{3,2},{4,5},{5,4},{6,7},{7,6},{8,9},{9,8},{10,11... | collective-permute-start | bytes 3145736 | tf_op jit(solution)/shard_map/ppermute | solution.py:388
  73.9 14.4 %all-to-all-start.2 = ((bf16[4,64,1280]{2,1,0:T(8,128)(2,1)}), bf16[4,64,1280]{2,1,0:T(8,128)(2,1)S(1)}, u32[]{:S(2)}, u32[]{:S(2)}) async-start(bf16[4,64,1280]{2,1,0:T(8,128)(2,1)} %bitcast.3), calls=%async_computation.2 | async-start | bytes 1310720 | tf_op jit(solution)/shard_map/all_to_all | solution.py:417
